TPU v7x, 128 devices: a whole 4x4x4 slice. The times are simulated.
128 devices in a mesh: row: 16 (over x, y_hi, core), col: 8 (over z, y_lo).
Axes of the slice: x: 4, y: 4 (y_hi: 2, y_lo: 2; y = y_hi * 2 + y_lo), z: 4, core: 2. Of those that a mesh axis runs over, the one named last changes fastest.
Arguments:
- a_vals: bfloat16 [512, 8, 64, 1024], P('row', 'col'), may hold values from -0.0625 to 0.0625
- a_cols: int32 [512, 8, 16], P('row', 'col'), may hold values from 0 to 63, all different within a row
- p_vals: bfloat16 [512, 64, 256], P(('row', 'col')), may hold values from -1.5 to 1.5
- p_cols: int32 [512, 4], P(('row', 'col')), may hold values from 0 to 15, all different within a row
Outputs:
- coarse_op: float32 [1024, 1024], P('row', 'col')
Inputs may be any that keep to these rules, and one draw needn't show every extreme that they name: `a_cols`: within one fine block row and column range the 16 entries are distinct. `p_cols`: within one fine block row the 4 entries are distinct.
All inputs are finite; a program needn't handle non-finite values.
Results may differ from a plain program's by a relative error of at most 0.0003.
Values may be sent and summed in bfloat16 or wider, within the bound.
No kernel may reach another device: no remote copies, remote signals or barrier semaphores. Data moves between devices by JAX's collectives and lax.ppermute only.
A program may use at most 128 MiB of HBM per device.

v0:
```python
import math

import jax
import jax.numpy as jnp
from jax import lax
from jax.sharding import PartitionSpec as P


def from_root(value, axis, source):
    kept = jnp.where(lax.axis_index(axis) == source, value, 0).astype(value.dtype)
    return lax.psum(kept, axis)


def contract_rows(p_slabs, p_kinds, wide, coarse):
    fine_rows = p_slabs.shape[0]
    block = p_slabs.shape[1]
    touched = p_kinds.shape[1]
    width = wide.shape[1]
    group = math.gcd(fine_rows, 4)
    slabs_g = p_slabs.reshape(fine_rows // group, group, block, touched * block)
    kinds_g = p_kinds.reshape(fine_rows // group, group, touched)
    wide_g = wide.reshape(fine_rows // group, group, block, width)

    def step(total, pieces):
        slab_part, kind_part, wide_part = pieces
        folded = jnp.einsum(
            "ire,irq->ieq",
            slab_part.astype(jnp.float32),
            wide_part,
            precision=lax.Precision.HIGHEST,
        )
        onehot = (kind_part[:, :, None] == lax.iota(jnp.int32, coarse)[None, None, :]).astype(
            jnp.float32
        )
        placed = jnp.einsum(
            "imn,imeq->neq",
            onehot,
            folded.reshape(group, touched, block, width),
            precision=lax.Precision.HIGHEST,
        )
        return (total + placed.reshape(coarse * block, width), None)

    start_total = jnp.zeros((coarse * block, width), jnp.float32)
    total, unused = lax.scan(step, start_total, (slabs_g, kinds_g, wide_g))
    return total


def shards(a_vals, a_cols, p_vals, p_cols):
    n_row = lax.axis_size("row")
    n_col = lax.axis_size("col")
    ratio = n_row // n_col
    block = a_vals.shape[2]
    per_row = a_cols.shape[2]
    touched = p_cols.shape[1]
    fine_rows = a_vals.shape[0]
    col_index = lax.axis_index("col")
    vals_r, ids_r = (
        lax.all_gather(p_vals, "col", axis=0, tiled=True),
        lax.all_gather(p_cols, "col", axis=0, tiled=True),
    )
    got_vals = []
    got_ids = []
    for offset in range(ratio):
        one_vals, one_ids = (
            from_root(vals_r, "row", ratio * col_index + offset),
            from_root(ids_r, "row", ratio * col_index + offset),
        )
        got_vals.append(one_vals)
        got_ids.append(one_ids)
    vals_c = jnp.concatenate(got_vals, axis=0)
    ids_c = jnp.concatenate(got_ids, axis=0)
    group = math.gcd(fine_rows, 4)
    tiles_a = a_vals[:, 0].reshape(fine_rows // group, group, block, per_row, block)
    where_a = a_cols[:, 0].reshape(fine_rows // group, group, per_row)

    def one_group(pair):
        tiles_part, where = pair
        flat_where = where.reshape(-1)
        picked = vals_c[flat_where].reshape(group, per_row, block, touched * block)
        kinds = ids_c[flat_where].reshape(group, per_row * touched)
        product = jnp.einsum(
            "irkf,ikfe->irke", tiles_part, picked, preferred_element_type=jnp.float32
        )
        product = product.reshape(group, block, per_row * touched, block)
        onehot = (kinds[:, :, None] == lax.iota(jnp.int32, n_row)[None, None, :]).astype(
            jnp.float32
        )
        placed = jnp.einsum("irsd,isn->irnd", product, onehot, precision=lax.Precision.HIGHEST)
        return placed.reshape(group * block, n_row * block)

    partial_w = lax.map(one_group, (tiles_a, where_a)).reshape(fine_rows * block, n_row * block)
    rows_out = n_row * block // n_row
    cols_out = n_row * block // n_col
    total = contract_rows(vals_r, ids_r, partial_w, n_row)
    total = total.reshape(n_row, rows_out, n_col, cols_out)
    total = jnp.transpose(total, (0, 2, 1, 3)).reshape(n_row * n_col * rows_out, cols_out)
    return lax.psum_scatter(total, ("row", "col"), scatter_dimension=0, tiled=True)


def solution(mesh):
    in_specs = (
        P("row", "col", None, None),
        P("row", "col", None),
        P(("row", "col"), None, None),
        P(("row", "col"), None),
    )
    out_specs = P("row", "col")
    return jax.shard_map(shards, mesh=mesh, in_specs=in_specs, out_specs=out_specs, check_vma=False)
```

profile of v0, /device:TPU:0, one launch (start us, length us, event | category | flops | bytes accessed | tf_op | source)
XLA Modules:
  0.0 1218.0 jit_solution(4784218886099866676)
XLA Ops:
  7.3 45.0 %all-gather.3.cloned.1.call-done = bf16[32,64,256]{2,1,0:T(8,128)(2,1)} async-done(((bf16[4,64,256]{2,1,0:T(8,128)(2,1)}), bf16[32,64,256]{2,1,0:T(8,128)(2,1)}) %all-gather.3.cloned.1.call-update) | async-done | bytes 1048592 | tf_op jit(solution)/shard_map/all_gather | solution.py:58
  55.1 24.8 %all-gather = s32[8,4,4]{2,1,0:T(4,128)S(1)} all-gather(s32[1,4,4]{2,1,0:T(4,128)S(1)} %bitcast.92), channel_id=1, replica_groups=mesh['row'=16,'col'=8] {'col'}, dimensions={0}, use_global_device_ids=true | all-gather | bytes 576 | tf_op jit(solution)/shard_map/all_gather | solution.py:59
  80.0 13.7 %all-reduce = (s32[32,4]{0,1:T(4,128)S(1)}, s32[32,4]{0,1:T(4,128)S(1)}) all-reduce(s32[32,4]{0,1:T(4,128)S(1)} %copy.32, s32[32,4]{0,1:T(4,128)S(1)} %copy.31), channel_id=1, replica_groups=mesh['row'=16,'col'=8] {'row'}, use_global_device_ids=true, to_apply=%region_3.4 | all-reduce | flops 256 | bytes 2048 | tf_op jit(solution)/shard_map/psum | solution.py:11
  93.9 11.6 reshape_squeeze.7
  105.6 94.5 %all-reduce.4.cloned.1.call-done = (bf16[32,64,256]{2,1,0:T(8,128)(2,1)}, bf16[32,64,256]{2,1,0:T(8,128)(2,1)}) async-done(((bf16[32,64,256]{2,1,0:T(8,128)(2,1)}, bf16[32,64,256]{2,1,0:T(8,128)(2,1)}), (bf16[32,64,256]{2,1,0:T(8,128)(2,1)}, bf16[32,64,256]{2,1,0:T(8,128)(2,1)})) %all-reduce.4.cloned.1.call-update) | async-done | bytes 2097168 | tf_op jit(solution)/shard_map/psum | solution.py:11
  203.2 186.4 %while.21 = (s32[]{:T(128)}, f32[8,256,1024]{2,1,0:T(8,128)}, s32[8,4,16]{2,1,0:T(4,128)S(1)}, s32[64,4]{1,0:T(8,128)S(1)}, bf16[64,64,256]{2,1,0:T(8,128)(2,1)}, /*index=5*/bf16[8,4,64,16,64]{4,3,2,1,0:T(8,128)(2,1)}, s32[]{:T(128)}) while((s32[]{:T(128)}, f32[8,256,1024]{2,1,0:T(8,128)}, s32[8,4,16]{2,1,0:T(4,128)S(1)}, ...), condition=%wide.region_5.6_spmd, body=%wide.region_4.5_spmd.sunk | while | flops 335549632 | bytes 38285140 | solution.py:91
  207.7 4.3 copy.46
  212.0 7.0 reshape.107
  219.7 5.2 convolution_bitcast_fusion.5
  231.0 4.3 copy.46
  235.4 7.0 reshape.107
  243.0 5.1 convolution_bitcast_fusion.5
  254.3 4.3 copy.46
  258.6 7.0 reshape.107
  266.3 5.2 convolution_bitcast_fusion.5
  277.6 4.3 copy.46
  281.9 7.0 reshape.107
  289.6 5.1 convolution_bitcast_fusion.5
  300.9 4.3 copy.46
  305.2 7.0 reshape.107
  312.9 5.2 convolution_bitcast_fusion.5
  324.2 4.3 copy.46
  328.6 7.0 reshape.107
  336.2 5.2 convolution_bitcast_fusion.5
  347.5 4.3 copy.46
  351.8 7.0 reshape.107
  359.5 5.1 convolution_bitcast_fusion.5
  370.8 4.3 copy.46
  375.1 7.0 reshape.107
  382.8 5.1 convolution_bitcast_fusion.5
  389.6 165.1 %while.22 = (s32[]{:T(128)}, f32[1024,1024]{1,0:T(8,128)}, s32[8,4,4]{2,1,0:T(4,128)S(1)}, bf16[8,4,64,256]{3,2,1,0:T(8,128)(2,1)}, f32[8,4,64,1024]{3,2,1,0:T(8,128)}, /*index=5*/s32[]{:T(128)}, s32[]{:T(128)}) while((s32[]{:T(128)}, f32[1024,1024]{1,0:T(8,128)}, s32[8,4,4]{2,1,0:T(4,128)S(1)}, bf16[8,4,64,256]{3,2,1,0:T(8,128)(2,1)}, ...), condition=%wide.region_7.8_spmd.clone, body=%wide.region_6.7_spmd.clone.sunk | while | flops 1008730368 | bytes 34735384 | solution.py:44
  392.7 6.4 fusion.39
  399.1 4.4 copy.48
  403.5 5.6 bitcast_add_fusion.2
  409.1 3.2 fusion.38
  412.3 6.4 fusion.39
  418.6 4.4 copy.48
  423.0 6.9 bitcast_add_fusion.2
  429.9 3.2 fusion.38
  433.1 6.4 fusion.39
  439.4 4.4 copy.48
  443.8 6.9 bitcast_add_fusion.2
  450.7 3.2 fusion.38
  453.9 6.4 fusion.39
  460.2 4.4 copy.48
  464.6 6.9 bitcast_add_fusion.2
  471.5 3.2 fusion.38
  474.7 6.4 fusion.39
  481.0 4.4 copy.48
  485.4 6.9 bitcast_add_fusion.2
  492.3 3.2 fusion.38
  495.5 6.4 fusion.39
  501.8 4.4 copy.48
  506.2 6.9 bitcast_add_fusion.2
  513.1 3.2 fusion.38
  516.3 6.4 fusion.39
  522.6 4.4 copy.48
  527.0 6.9 bitcast_add_fusion.2
  533.9 3.2 fusion.38
  537.1 6.4 fusion.39
  543.4 4.4 copy.48
  547.8 6.9 bitcast_add_fusion.2
  554.7 3.2 copy.34
  560.6 650.9 %reduce-scatter.2.cloned.1.call-done = f32[64,128]{1,0:T(8,128)} async-done(((f32[8192,128]{1,0:T(8,128)}), f32[64,128]{1,0:T(8,128)}) %reduce-scatter.2.cloned.1.call-update) | async-done | bytes 32784 | tf_op jit(solution)/shard_map/reduce_scatter | solution.py:97
  (118 shorter events, 67.3 us)
Async XLA Ops:
  6.5 48.5 %copy-start.1 = (s32[4,4]{1,0:T(4,128)S(1)}, s32[4,4]{1,0:T(4,128)}, u32[]{:S(2)}) copy-start(s32[4,4]{1,0:T(4,128)} %param.11) | copy-start | bytes 196
  6.5 45.8 %all-gather.3.cloned.1.call-start = ((), (), s32[]{:S(2)}) async-start(), calls=%async_computation.1 | async-start | bytes 1179648 | tf_op jit(solution)/shard_map/all_gather | solution.py:58
  7.3 192.9 %all-reduce.4.cloned.1.call-start = ((), (), s32[]{:S(2)}) async-start(), calls=%async_computation.3 | async-start | bytes 4194304 | tf_op jit(solution)/shard_map/psum | solution.py:11
  55.0 1156.4 %reduce-scatter.2.cloned.1.call-start = ((), (), s32[]{:S(2)}) async-start(), calls=%async_computation.2 | async-start | bytes 4227072 | tf_op jit(solution)/shard_map/reduce_scatter | solution.py:97
  93.9 11.6 copy-start
Sparse Core Ops, SparseCore 0:
  9.0 43.3 all-gather.2
  55.1 144.9 all-reduce.3
  560.7 650.7 reduce-scatter.1
where the time goes:
time: 1220 us
  waiting for transfers between devices  791 us (65%)
  local copies, waits for them, and re-layouts  192 us (16%)
  matrix products  123 us (10%)
  other arithmetic  59.6 us (5%)
  blocking collectives  38.5 us (3%)
  between operations  13.2 us (1%)
    reduce_scatter x1, waiting for transfers between devices, shards(): lax.psum_scatter(total, ('row', 'col'), scatter_dimension=0, tiled=True)  651 us
    psum x1, waiting for transfers between devices, from_root(): return lax.psum(kept, axis)  94.5 us
    reshape x8, local copies, waits for them, and re-layouts, one_group(): product = product.reshape(group, block, per_row * touched, block)  55.7 us
    add x8, other arithmetic, step(): return (total + placed.reshape(coarse * block, width), None)  53.6 us
    dot_general x8, matrix products, step(): jnp.einsum('imn,imeq->neq', onehot, folded.reshape(group, touched, block,...  50.8 us
    all_gather x1, waiting for transfers between devices, shards(): lax.all_gather(p_vals, 'col', axis=0, tiled=True)  45 us
    dot_general x8, matrix products, one_group(): jnp.einsum('irsd,isn->irnd', product, onehot, precision=lax.Precision.HIG...  41.2 us
    dot_general x8, local copies, waits for them, and re-layouts, step(): jnp.einsum('imn,imeq->neq', onehot, folded.reshape(group, touched, block,...  35 us
  transfers between devices with their start and end apart: 3, of which 3 were waited for; matrix products, arithmetic and copies ran while one was open for 1% of the time, Pallas kernels for 0%

commit v1 on v0

v1 whole, which is shorter than its diff:
```python
import functools

import jax
import jax.numpy as jnp
from jax import lax
from jax.experimental import pallas as pl
from jax.experimental.pallas import tpu as pltpu
from jax.sharding import Mesh
from jax.sharding import PartitionSpec as P

AXES = ("x", "yh", "core", "z", "yl")
SIZES = (4, 2, 2, 4, 2)
BF16 = jnp.bfloat16
F32 = jnp.float32
BS = 64
PAD = 16


def linear(place):
    index = 0
    for at, size in zip(place, SIZES):
        index = index * size + at
    return index


def route(target):
    pairs = []
    for x in range(4):
        for yh in range(2):
            for core in range(2):
                for z in range(4):
                    for yl in range(2):
                        to_x, to_y, to_core, to_z = target(x, 2 * yh + yl, core, z)
                        to_x, to_y, to_z = to_x % 4, to_y % 4, to_z % 4
                        to = linear((to_x, to_y // 2, to_core, to_z, to_y % 2))
                        pairs.append((linear((x, yh, core, z, yl)), to))
    return pairs


def swap_y(y):
    return (y % 2) * 2 + y // 2


MIRROR = route(lambda x, y, c, z: (z, swap_y(y), c, x))
MIRROR_FAR = route(lambda x, y, c, z: (z, swap_y(y) + 2, c, x))
OTHER_CORE = route(lambda x, y, c, z: (x, y, 1 - c, z))
NEXT_X = route(lambda x, y, c, z: (x + 1, y, c, z))
LAST_X = route(lambda x, y, c, z: (x - 1, y, c, z))
NEXT_Z = route(lambda x, y, c, z: (x, y, c, z + 1))
LAST_Z = route(lambda x, y, c, z: (x, y, c, z - 1))
BESIDE = route(lambda x, y, c, z: (x, y ^ 1, c, z))


def send(value, pairs):
    return lax.ppermute(value, AXES, pairs)


def ring_of_four(own, forward, backward):
    half = own.shape[0] // 2
    behind = send(own, forward)
    ahead = send(own, backward)
    far_a = send(behind[:half], forward)
    far_b = send(ahead[half:], backward)
    return own, behind, ahead, far_a, far_b


def spread(tile, ids, coarse_pairs, store):
    lane = lax.broadcasted_iota(jnp.int32, (1, 128), 1)
    low = lane < BS
    parts = []
    for pair in range(2):
        v = tile[:, 128 * pair : 128 * (pair + 1)]
        r = jnp.concatenate([v[:, BS:], v[:, :BS]], axis=1)
        d = ids[:, 128 * pair : 128 * (pair + 1)]
        e = jnp.concatenate([d[:, BS:], d[:, :BS]], axis=1)
        parts.append((jnp.where(low, v, r), jnp.where(low, d, e)))
        parts.append((jnp.where(low, r, v), jnp.where(low, e, d)))
    for g in range(coarse_pairs):
        here = jnp.where(low, 2.0 * g, 2.0 * g + 1.0)
        out = jnp.zeros((BS, 128), tile.dtype)
        for v, d in parts:
            out = jnp.where(jnp.broadcast_to(d == here, (BS, 128)), v, out)
        store(g, out)


def galerkin(cols_ref, core_ref, a_ref, pc_ref, pr_ref, own_ref, other_ref, dense, turned, hi, lo):
    core = core_ref[0]
    pieces = pc_ref.shape[0]
    fine_rows = a_ref.shape[0]

    @pl.loop(0, pieces)
    def _(piece):
        for b in range(4):
            tile = pc_ref[piece, pl.ds(BS * b, BS), :].astype(F32)
            ids = pc_ref[piece, pl.ds(4 * BS, PAD), :].astype(F32)[b : b + 1]

            def store(g, out):
                dense[4 * piece + b, :, 128 * g : 128 * (g + 1)] = out.astype(BF16)

            spread(tile, ids, 8, store)

    @pl.loop(0, pr_ref.shape[0])
    def _(piece):
        ids4 = pr_ref[piece, pl.ds(4 * BS, PAD), :].astype(F32)
        lane = lax.broadcasted_iota(jnp.int32, (1, 128), 1)
        low = lane < BS
        for pair in range(2):
            tile = pr_ref[piece, pl.ds(128 * pair, 128), :].astype(F32)
            flipped = tile.T
            ida = ids4[2 * pair : 2 * pair + 1]
            idb = ids4[2 * pair + 1 : 2 * pair + 2]
            where = []
            for m in range(4):
                a = ida[:, BS * m : BS * (m + 1)]
                b = idb[:, BS * m : BS * (m + 1)]
                where.append(jnp.concatenate([a, b], axis=1))
            for n in range(16):
                out = jnp.zeros((BS, 128), F32)
                for m in range(4):
                    hit = jnp.broadcast_to(where[m] == float(n), (BS, 128))
                    out = jnp.where(hit, flipped[BS * m : BS * (m + 1)], out)
                slot = core if n % 2 == 0 else 1 - core
                at = pl.multiple_of(256 * piece + 128 * pair, 128)
                turned[slot, pl.ds(BS * (n // 2), BS), pl.ds(at, 128)] = out.astype(BF16)

    @pl.loop(0, fine_rows)
    def _(i):
        for n in range(4):
            total = None
            for k in range(4):
                tiles = [
                    dense[cols_ref[i, 4 * k + j], :, 256 * n : 256 * (n + 1)] for j in range(4)
                ]
                weights = jnp.concatenate(tiles, axis=0)
                left = a_ref[i, :, 256 * k : 256 * (k + 1)]
                part = jnp.dot(left, weights, preferred_element_type=F32)
                total = part if total is None else total + part
            top = total.astype(BF16)
            rows = pl.ds(pl.multiple_of(i * BS, BS), BS)
            hi[rows, 256 * n : 256 * (n + 1)] = top
            lo[rows, 256 * n : 256 * (n + 1)] = (total - top.astype(F32)).astype(BF16)

    for slot, out_ref in ((1, other_ref), (0, own_ref)):

        @pl.loop(0, 4)
        def _(n):
            at = pl.ds(pl.multiple_of(256 * n, 256), 256)
            left = turned[slot]
            c = jnp.dot(left, hi[:, at], preferred_element_type=F32)
            c = c + jnp.dot(left, lo[:, at], preferred_element_type=F32)
            for q in range(8):
                for j in range(2):
                    out_ref[8 * q + 2 * n + j] = c[
                        BS * q : BS * (q + 1), 128 * j : 128 * (j + 1)
                    ]


def compute(cols, core, a, pc, pr):
    half = jax.ShapeDtypeStruct((64, BS, 128), F32)
    vmem = pl.BlockSpec(memory_space=pltpu.VMEM)
    smem = pl.BlockSpec(memory_space=pltpu.SMEM)
    rows = a.shape[0] * BS
    return pl.pallas_call(
        galerkin,
        out_shape=(half, half),
        in_specs=[smem, smem, vmem, vmem, vmem],
        out_specs=(vmem, vmem),
        scratch_shapes=[
            pltpu.VMEM((64, BS, 1024), BF16),
            pltpu.VMEM((2, 512, rows), BF16),
            pltpu.VMEM((rows, 1024), BF16),
            pltpu.VMEM((rows, 1024), BF16),
        ],
        compiler_params=pltpu.CompilerParams(vmem_limit_bytes=48 << 20),
        name="galerkin",
    )(cols, core, a, pc, pr)


def gather_pieces(piece):
    near = send(piece, MIRROR)
    far = send(piece, MIRROR_FAR)
    yh = lax.axis_index("yh")
    x = lax.axis_index("x")
    z = lax.axis_index("z")
    yl = lax.axis_index("yl")
    rows = piece.shape[0]
    pair = jnp.stack([jnp.where(yh == 0, near, far), jnp.where(yh == 0, far, near)])
    own, behind, ahead, far_a, far_b = ring_of_four(pair, NEXT_X, LAST_X)
    opposite = jnp.concatenate([far_a, far_b])
    ring = jnp.stack([own, ahead, opposite, behind])
    ring = jnp.roll(ring, x, axis=0)
    half = ring.reshape(8, rows, piece.shape[1])
    other = send(half, OTHER_CORE)
    core = lax.axis_index("core")
    pc = jnp.concatenate([jnp.where(core == 0, half, other), jnp.where(core == 0, other, half)])

    beside = send(piece, BESIDE)
    pair = jnp.stack([jnp.where(yl == 0, piece, beside), jnp.where(yl == 0, beside, piece)])
    own, behind, ahead, far_a, far_b = ring_of_four(pair, NEXT_Z, LAST_Z)
    opposite = jnp.concatenate([far_a, far_b])
    ring = jnp.stack([own, ahead, opposite, behind])
    ring = jnp.roll(ring, z, axis=0)
    pr = ring.reshape(8, rows, piece.shape[1])
    return pc, pr


def shards(a_vals, a_cols, p_vals, p_cols):
    ids = jnp.repeat(p_cols.astype(BF16), BS, axis=1)
    piece = jnp.concatenate([p_vals.reshape(4 * BS, 4 * BS), ids, jnp.zeros((PAD - 4, 4 * BS), BF16)])
    pc, pr = gather_pieces(piece)
    core = lax.axis_index("core").astype(jnp.int32).reshape(1)
    own, other = compute(a_cols[:, 0], core, a_vals[:, 0], pc, pr)
    total = own + send(other, OTHER_CORE)
    mixed = lax.all_to_all(total, ("x", "yh", "z", "yl"), 0, 0, tiled=True)
    return jnp.sum(mixed, axis=0)


def solution(mesh):
    fine = Mesh(mesh.devices.reshape(SIZES), AXES)
    row, col = ("x", "yh", "core"), ("z", "yl")
    in_specs = (
        P(row, col, None, None),
        P(row, col, None),
        P(row + col, None, None),
        P(row + col, None),
    )
    return jax.shard_map(
        shards, mesh=fine, in_specs=in_specs, out_specs=P(row, col), check_vma=False
    )
```

time: 1220 us -> 156 us (0.13)
  waiting for transfers between devices: 791 us -> 34.5 us
  local copies, waits for them, and re-layouts: 192 us -> 1.04 us
  matrix products: 123 us -> 0 us
  other arithmetic: 59.6 us -> 7.58 us
  Pallas kernels: 0 us -> 39.3 us
  starting transfers between devices: 0.08 us -> 33 us
  between operations: 13.2 us -> 0.16 us
    reduce_scatter x1 -> x0, waiting for transfers between devices: 651 us -> none  [shards(): lax.psum_scatter(total, ('row', 'col'), scatter_dimension=0, tiled=True)]
    dot_general x32 -> x0, matrix products: 123 us -> none  [the longest x8 50.8 us: step(): jnp.einsum('imn,imeq->neq', onehot, folded.reshape(group, touched, block,...]
    psum x1 -> x0, waiting for transfers between devices: 94.5 us -> none  [from_root(): return lax.psum(kept, axis)]
    reshape x17 -> x1, local copies, waits for them, and re-layouts: 59.1 us -> 0.09 us  [shards(): ids = jnp.repeat(p_cols.astype(BF16), BS, axis=1)]
    add x8 -> x1, other arithmetic: 53.6 us -> 0.39 us  [shards(): total = own + send(other, OTHER_CORE)]
    all_gather x1 -> x0, waiting for transfers between devices: 45 us -> none  [shards(): lax.all_gather(p_vals, 'col', axis=0, tiled=True)]
    all_to_all x0 -> x1, blocking collectives: none -> 40.1 us  [shards(): mixed = lax.all_to_all(total, ('x', 'yh', 'z', 'yl'), 0, 0, tiled=True)]
    pallas_call x0 -> x1, Pallas kernels: none -> 39.3 us  [compute(): pl.pallas_call(galerkin, out_shape=(half, half), in_specs=[smem, smem, vm...]
  transfers between devices with their start and end apart: 3 -> 13, of which waited for: 3 -> 8; matrix products, arithmetic and copies ran while one was open for 1% -> 2% of each run, Pallas kernels for 0% -> 0%
where the time goes in v1:
time: 156 us
  blocking collectives  40.1 us (26%)
  Pallas kernels  39.3 us (25%)
  waiting for transfers between devices  34.5 us (22%)
  starting transfers between devices  33 us (21%)
  other arithmetic  7.58 us (5%)
    all_to_all x1, blocking collectives, shards(): mixed = lax.all_to_all(total, ('x', 'yh', 'z', 'yl'), 0, 0, tiled=True)  40.1 us
    pallas_call x1, Pallas kernels, compute(): pl.pallas_call(galerkin, out_shape=(half, half), in_specs=[smem, smem, vm...  39.3 us
    ppermute x13, waiting for transfers between devices, send(): return lax.ppermute(value, AXES, pairs)  34.5 us
    ppermute x13, starting transfers between devices, send(): return lax.ppermute(value, AXES, pairs)  33 us
  transfers between devices with their start and end apart: 13, of which 8 were waited for; matrix products, arithmetic and copies ran while one was open for 2% of the time, Pallas kernels for 0%

profile of v1, /device:TPU:0, one launch (start us, length us, event | category | flops | bytes accessed | tf_op | source)
XLA Modules:
  0.0 155.7 jit_solution(2518823976140712122)
XLA Ops:
  0.0 0.7 convert_element_type.3
  0.7 0.1 broadcast_in_dim.6
  0.8 0.1 reshape.17
  0.9 0.1 pad.28.clone
  0.9 1.0 maximum_maximum_fusion
  1.9 3.4 %collective-permute-start.1 = (bf16[272,256]{1,0:T(8,128)(2,1)S(1)}, bf16[272,256]{1,0:T(8,128)(2,1)S(1)}, u32[]{:S(2)}, u32[]{:S(2)}) collective-permute-start(bf16[272,256]{1,0:T(8,128)(2,1)S(1)} %maximum_maximum_fusion), channel_id=1, source_target_pairs={{0,16},{1,0},{2,48},{3,32},{4,80},{5,64},{6,112},{7,96},{8,24},{9,... | collective-permute-start | bytes 417800 | tf_op jit(solution)/shard_map/ppermute | solution.py:55
  5.3 0.7 collective-permute-start
  6.0 12.3 %collective-permute-done.1 = bf16[272,256]{1,0:T(8,128)(2,1)S(1)} collective-permute-done((bf16[272,256]{1,0:T(8,128)(2,1)S(1)}, bf16[272,256]{1,0:T(8,128)(2,1)S(1)}, u32[]{:S(2)}, u32[]{:S(2)}) %collective-permute-start.1) | collective-permute-done | bytes 139296 | tf_op jit(solution)/shard_map/ppermute | solution.py:55
  18.3 0.0 collective-permute-done
  18.4 9.0 %collective-permute-start.2 = (bf16[2,272,256]{2,1,0:T(8,128)(2,1)S(1)}, bf16[2,272,256]{2,1,0:T(8,128)(2,1)S(1)}, u32[]{:S(2)}, u32[]{:S(2)}) collective-permute-start(bf16[2,272,256]{2,1,0:T(8,128)(2,1)S(1)} %get-tuple-element.14), channel_id=1, source_target_pairs={{0,96},{1,97},{2,98},{3,99},{4,100},{5,101},{6,102},{7,103},{8,104... | collective-permute-start | bytes 835592 | tf_op jit(solution)/shard_map/ppermute | solution.py:55
  27.4 0.0 collective-permute-start.3
  27.4 5.1 %collective-permute-done.2 = bf16[2,272,256]{2,1,0:T(8,128)(2,1)S(1)} collective-permute-done((bf16[2,272,256]{2,1,0:T(8,128)(2,1)S(1)}, bf16[2,272,256]{2,1,0:T(8,128)(2,1)S(1)}, u32[]{:S(2)}, u32[]{:S(2)}) %collective-permute-start.2) | collective-permute-done | bytes 278560 | tf_op jit(solution)/shard_map/ppermute | solution.py:55
  32.5 3.8 %collective-permute-start.5 = (bf16[1,272,256]{2,1,0:T(8,128)(2,1)S(1)}, bf16[1,272,256]{2,1,0:T(8,128)(2,1)S(1)}, u32[]{:S(2)}, u32[]{:S(2)}) collective-permute-start(bf16[1,272,256]{2,1,0:T(8,128)(2,1)S(1)} %slice.17), channel_id=1, source_target_pairs={{0,96},{1,97},{2,98},{3,99},{4,100},{5,101},{6,102},{7,103},{8,104... | collective-permute-start | bytes 417800 | tf_op jit(solution)/shard_map/ppermute | solution.py:55
  36.3 0.0 collective-permute-done.3
  36.3 0.1 collective-permute-start.4
  36.4 6.1 %collective-permute-start.7 = (bf16[272,256]{1,0:T(8,128)(2,1)S(1)}, bf16[272,256]{1,0:T(8,128)(2,1)S(1)}, u32[]{:S(2)}, u32[]{:S(2)}) collective-permute-start(bf16[272,256]{1,0:T(8,128)(2,1)S(1)} %maximum_maximum_fusion), channel_id=1, source_target_pairs={{0,1},{1,0},{2,3},{3,2},{4,5},{5,4},{6,7},{7,6},{8,9},{9,8},{10,11... | collective-permute-start | bytes 417800 | tf_op jit(solution)/shard_map/ppermute | solution.py:55
  42.4 0.0 collective-permute-done.5
  42.4 0.2 collective-permute-done.4
  42.6 0.0 copy-start
  42.7 1.3 fusion.10
  44.0 0.0 copy-start.1
  44.0 0.1 collective-permute-start.6
  44.1 1.4 collective-permute-done.7
  45.5 0.0 copy-done
  45.5 0.1 select_bitcast_fusion.1
  45.7 6.1 %collective-permute-start.8 = (bf16[2,272,256]{2,1,0:T(8,128)(2,1)S(1)}, bf16[2,272,256]{2,1,0:T(8,128)(2,1)S(1)}, u32[]{:S(2)}, u32[]{:S(2)}) collective-permute-start(bf16[2,272,256]{2,1,0:T(8,128)(2,1)S(1)} %get-tuple-element.12), channel_id=1, source_target_pairs={{0,6},{1,7},{2,0},{3,1},{4,2},{5,3},{6,4},{7,5},{8,14},{9,15},{10,... | collective-permute-start | bytes 835592 | tf_op jit(solution)/shard_map/ppermute | solution.py:55
  51.8 0.0 collective-permute-start.9
  51.8 5.0 %collective-permute-done.8 = bf16[2,272,256]{2,1,0:T(8,128)(2,1)S(1)} collective-permute-done((bf16[2,272,256]{2,1,0:T(8,128)(2,1)S(1)}, bf16[2,272,256]{2,1,0:T(8,128)(2,1)S(1)}, u32[]{:S(2)}, u32[]{:S(2)}) %collective-permute-start.8) | collective-permute-done | bytes 278560 | tf_op jit(solution)/shard_map/ppermute | solution.py:55
  56.9 3.8 %collective-permute-start.11 = (bf16[1,272,256]{2,1,0:T(8,128)(2,1)S(1)}, bf16[1,272,256]{2,1,0:T(8,128)(2,1)S(1)}, u32[]{:S(2)}, u32[]{:S(2)}) collective-permute-start(bf16[1,272,256]{2,1,0:T(8,128)(2,1)S(1)} %slice.19), channel_id=1, source_target_pairs={{0,6},{1,7},{2,0},{3,1},{4,2},{5,3},{6,4},{7,5},{8,14},{9,15},{10,... | collective-permute-start | bytes 417800 | tf_op jit(solution)/shard_map/ppermute | solution.py:55
  60.6 0.0 collective-permute-done.9
  60.6 0.7 slice.18
  61.3 0.0 collective-permute-start.10
  61.3 0.0 copy-done.1
  61.3 0.1 copy.5
  61.4 1.8 %collective-permute-done.11 = bf16[1,272,256]{2,1,0:T(8,128)(2,1)S(1)} collective-permute-done((bf16[1,272,256]{2,1,0:T(8,128)(2,1)S(1)}, bf16[1,272,256]{2,1,0:T(8,128)(2,1)S(1)}, u32[]{:S(2)}, u32[]{:S(2)}) %collective-permute-start.11) | collective-permute-done | bytes 139296 | tf_op jit(solution)/shard_map/ppermute | solution.py:55
  63.2 4.6 %collective-permute-done.10 = bf16[1,272,256]{2,1,0:T(8,128)(2,1)S(1)} collective-permute-done((bf16[1,272,256]{2,1,0:T(8,128)(2,1)}, bf16[1,272,256]{2,1,0:T(8,128)(2,1)S(1)}, u32[]{:S(2)}, u32[]{:S(2)}) %collective-permute-start.10) | collective-permute-done | bytes 139296 | tf_op jit(solution)/shard_map/ppermute | solution.py:55
  67.8 1.3 fusion.3
  69.1 0.0 collective-permute-done.6
  69.2 0.2 broadcast_select_fusion.1
  69.4 1.6 %pad_maximum_fusion.pc_ref = bf16[16,272,256]{2,1,0:T(8,128)(2,1)} fusion(bf16[8,272,256]{2,1,0:T(8,128)(2,1)S(1)} %get-tuple-element.11, bf16[8,272,256]{2,1,0:T(8,128)(2,1)S(1)} %get-tuple-element.10), kind=kLoop, calls=%fused_computation.8 | loop fusion | flops 1114112 | bytes 4456448 | tf_op jit(solution)/shard_map/concatenate | solution.py:195
  70.9 39.3 %galerkin.1 = (f32[64,64,128]{2,1,0:T(8,128)S(1)}, f32[64,64,128]{2,1,0:T(8,128)S(1)}) custom-call(s32[32,16]{1,0:T(8,128)S(1)} %bitcast.29, s32[1]{0:T(128)} %bitcast.1.core_ref, bf16[32,64,1024]{2,1,0:T(8,128)(2,1)} %bitcast.31, bf16[16,272,256]{2,1,0:T(8,128)(2,1)} %pad_maximum_fusion.pc_ref, bf16[8,272,256]{2,1,0:T(8,128)(2,1)S(1)} %bitcast.28), custom_call_target="tpu_custom_call" | custom-call | tf_op jit(solution)/shard_map/galerkin/pallas_call | solution.py:163
  110.2 0.1 collective-permute-start.12
  110.3 4.1 %collective-permute-done.12 = f32[64,64,128]{2,1,0:T(8,128)S(1)} collective-permute-done((f32[64,64,128]{2,1,0:T(8,128)S(1)}, f32[64,64,128]{2,1,0:T(8,128)S(1)}, u32[]{:S(2)}, u32[]{:S(2)}) %collective-permute-start.12) | collective-permute-done | bytes 2097184 | tf_op jit(solution)/shard_map/ppermute | solution.py:55
  114.5 0.4 add.11
  114.9 40.1 %all_to_all.5 = f32[64,64,128]{2,1,0:T(8,128)S(1)} all-to-all(f32[64,64,128]{2,1,0:T(8,128)S(1)} %add.11), channel_id=1, replica_groups=mesh['x'=4,'yh'=2,'core'=2,'z'=4,'yl'=2] {'x','yh','z','yl'}, dimensions={0} | all-to-all | bytes 4194304 | tf_op jit(solution)/shard_map/all_to_all | solution.py:214
  154.9 0.8 reduce_sum.9
  (9 shorter events, 0.2 us)
Async XLA Ops:
  1.9 16.4 %collective-permute-start.1 = (bf16[272,256]{1,0:T(8,128)(2,1)S(1)}, bf16[272,256]{1,0:T(8,128)(2,1)S(1)}, u32[]{:S(2)}, u32[]{:S(2)}) collective-permute-start(bf16[272,256]{1,0:T(8,128)(2,1)S(1)} %maximum_maximum_fusion), channel_id=1, source_target_pairs={{0,16},{1,0},{2,48},{3,32},{4,80},{5,64},{6,112},{7,96},{8,24},{9,... | collective-permute-start | bytes 417800 | tf_op jit(solution)/shard_map/ppermute | solution.py:55
  5.3 13.0 %collective-permute-start = (bf16[272,256]{1,0:T(8,128)(2,1)S(1)}, bf16[272,256]{1,0:T(8,128)(2,1)S(1)}, u32[]{:S(2)}, u32[]{:S(2)}) collective-permute-start(bf16[272,256]{1,0:T(8,128)(2,1)S(1)} %maximum_maximum_fusion), channel_id=1, source_target_pairs={{0,0},{1,16},{2,32},{3,48},{4,64},{5,80},{6,96},{7,112},{8,8},{9,2... | collective-permute-start | bytes 417800 | tf_op jit(solution)/shard_map/ppermute | solution.py:55
  18.4 14.1 %collective-permute-start.2 = (bf16[2,272,256]{2,1,0:T(8,128)(2,1)S(1)}, bf16[2,272,256]{2,1,0:T(8,128)(2,1)S(1)}, u32[]{:S(2)}, u32[]{:S(2)}) collective-permute-start(bf16[2,272,256]{2,1,0:T(8,128)(2,1)S(1)} %get-tuple-element.14), channel_id=1, source_target_pairs={{0,96},{1,97},{2,98},{3,99},{4,100},{5,101},{6,102},{7,103},{8,104... | collective-permute-start | bytes 835592 | tf_op jit(solution)/shard_map/ppermute | solution.py:55
  27.4 8.8 %collective-permute-start.3 = (bf16[2,272,256]{2,1,0:T(8,128)(2,1)S(1)}, bf16[2,272,256]{2,1,0:T(8,128)(2,1)S(1)}, u32[]{:S(2)}, u32[]{:S(2)}) collective-permute-start(bf16[2,272,256]{2,1,0:T(8,128)(2,1)S(1)} %get-tuple-element.14), channel_id=1, source_target_pairs={{0,32},{1,33},{2,34},{3,35},{4,36},{5,37},{6,38},{7,39},{8,40},{9,... | collective-permute-start | bytes 835592 | tf_op jit(solution)/shard_map/ppermute | solution.py:55
  32.5 9.9 %collective-permute-start.5 = (bf16[1,272,256]{2,1,0:T(8,128)(2,1)S(1)}, bf16[1,272,256]{2,1,0:T(8,128)(2,1)S(1)}, u32[]{:S(2)}, u32[]{:S(2)}) collective-permute-start(bf16[1,272,256]{2,1,0:T(8,128)(2,1)S(1)} %slice.17), channel_id=1, source_target_pairs={{0,96},{1,97},{2,98},{3,99},{4,100},{5,101},{6,102},{7,103},{8,104... | collective-permute-start | bytes 417800 | tf_op jit(solution)/shard_map/ppermute | solution.py:55
  36.3 6.3 %collective-permute-start.4 = (bf16[1,272,256]{2,1,0:T(8,128)(2,1)S(1)}, bf16[1,272,256]{2,1,0:T(8,128)(2,1)S(1)}, u32[]{:S(2)}, u32[]{:S(2)}) collective-permute-start(bf16[1,272,256]{2,1,0:T(8,128)(2,1)S(1)} %slice.16), channel_id=1, source_target_pairs={{0,32},{1,33},{2,34},{3,35},{4,36},{5,37},{6,38},{7,39},{8,40},{9,... | collective-permute-start | bytes 417800 | tf_op jit(solution)/shard_map/ppermute | solution.py:55
  36.4 9.1 %collective-permute-start.7 = (bf16[272,256]{1,0:T(8,128)(2,1)S(1)}, bf16[272,256]{1,0:T(8,128)(2,1)S(1)}, u32[]{:S(2)}, u32[]{:S(2)}) collective-permute-start(bf16[272,256]{1,0:T(8,128)(2,1)S(1)} %maximum_maximum_fusion), channel_id=1, source_target_pairs={{0,1},{1,0},{2,3},{3,2},{4,5},{5,4},{6,7},{7,6},{8,9},{9,8},{10,11... | collective-permute-start | bytes 417800 | tf_op jit(solution)/shard_map/ppermute | solution.py:55
  42.6 2.8 %copy-start = (bf16[4,64,256]{2,1,0:T(8,128)(2,1)S(1)}, bf16[4,64,256]{2,1,0:T(8,128)(2,1)}, u32[]{:S(2)}) copy-start(bf16[4,64,256]{2,1,0:T(8,128)(2,1)} %param.8) | copy-start | bytes 393220
  44.0 17.3 %copy-start.1 = (s32[32,1,16]{0,2,1:T(8,128)S(1)}, s32[32,1,16]{0,2,1:T(8,128)}, u32[]{:S(2)}) copy-start(s32[32,1,16]{0,2,1:T(8,128)} %param.7) | copy-start | bytes 6148
  44.0 25.1 %collective-permute-start.6 = (bf16[8,272,256]{2,1,0:T(8,128)(2,1)S(1)}, bf16[8,272,256]{2,1,0:T(8,128)(2,1)S(1)}, u32[]{:S(2)}, u32[]{:S(2)}) collective-permute-start(bf16[8,272,256]{2,1,0:T(8,128)(2,1)S(1)} %bitcast.30), channel_id=1, source_target_pairs={{0,8},{1,9},{2,10},{3,11},{4,12},{5,13},{6,14},{7,15},{8,0},{9,1},... | collective-permute-start | bytes 3342344 | tf_op jit(solution)/shard_map/ppermute | solution.py:55
  45.7 11.2 %collective-permute-start.8 = (bf16[2,272,256]{2,1,0:T(8,128)(2,1)S(1)}, bf16[2,272,256]{2,1,0:T(8,128)(2,1)S(1)}, u32[]{:S(2)}, u32[]{:S(2)}) collective-permute-start(bf16[2,272,256]{2,1,0:T(8,128)(2,1)S(1)} %get-tuple-element.12), channel_id=1, source_target_pairs={{0,6},{1,7},{2,0},{3,1},{4,2},{5,3},{6,4},{7,5},{8,14},{9,15},{10,... | collective-permute-start | bytes 835592 | tf_op jit(solution)/shard_map/ppermute | solution.py:55
  51.8 8.8 %collective-permute-start.9 = (bf16[2,272,256]{2,1,0:T(8,128)(2,1)S(1)}, bf16[2,272,256]{2,1,0:T(8,128)(2,1)S(1)}, u32[]{:S(2)}, u32[]{:S(2)}) collective-permute-start(bf16[2,272,256]{2,1,0:T(8,128)(2,1)S(1)} %get-tuple-element.12), channel_id=1, source_target_pairs={{0,2},{1,3},{2,4},{3,5},{4,6},{5,7},{6,0},{7,1},{8,10},{9,11},{10,... | collective-permute-start | bytes 835592 | tf_op jit(solution)/shard_map/ppermute | solution.py:55
  56.9 6.4 %collective-permute-start.11 = (bf16[1,272,256]{2,1,0:T(8,128)(2,1)S(1)}, bf16[1,272,256]{2,1,0:T(8,128)(2,1)S(1)}, u32[]{:S(2)}, u32[]{:S(2)}) collective-permute-start(bf16[1,272,256]{2,1,0:T(8,128)(2,1)S(1)} %slice.19), channel_id=1, source_target_pairs={{0,6},{1,7},{2,0},{3,1},{4,2},{5,3},{6,4},{7,5},{8,14},{9,15},{10,... | collective-permute-start | bytes 417800 | tf_op jit(solution)/shard_map/ppermute | solution.py:55
  61.3 6.5 %collective-permute-start.10 = (bf16[1,272,256]{2,1,0:T(8,128)(2,1)}, bf16[1,272,256]{2,1,0:T(8,128)(2,1)S(1)}, u32[]{:S(2)}, u32[]{:S(2)}) collective-permute-start(bf16[1,272,256]{2,1,0:T(8,128)(2,1)} %slice.18), channel_id=1, source_target_pairs={{0,2},{1,3},{2,4},{3,5},{4,6},{5,7},{6,0},{7,1},{8,10},{9,11},{10,... | collective-permute-start | bytes 417800 | tf_op jit(solution)/shard_map/ppermute | solution.py:55
  110.2 4.2 %collective-permute-start.12 = (f32[64,64,128]{2,1,0:T(8,128)S(1)}, f32[64,64,128]{2,1,0:T(8,128)S(1)}, u32[]{:S(2)}, u32[]{:S(2)}) collective-permute-start(f32[64,64,128]{2,1,0:T(8,128)S(1)} %get-tuple-element.9), channel_id=1, source_target_pairs={{0,8},{1,9},{2,10},{3,11},{4,12},{5,13},{6,14},{7,15},{8,0},{9,1},... | collective-permute-start | bytes 6291464 | tf_op jit(solution)/shard_map/ppermute | solution.py:55

commit v2 on v1

--- a/solution.py
+++ b/solution.py
@@ -1,5 +1,3 @@
-import functools
-
 import jax
 import jax.numpy as jnp
 from jax import lax
@@ -13,6 +11,7 @@
 BF16 = jnp.bfloat16
 F32 = jnp.float32
 BS = 64
+ROWS = 72
 PAD = 16
 
 
@@ -41,8 +40,8 @@
     return (y % 2) * 2 + y // 2
 
 
-MIRROR = route(lambda x, y, c, z: (z, swap_y(y), c, x))
-MIRROR_FAR = route(lambda x, y, c, z: (z, swap_y(y) + 2, c, x))
+REFLECT = route(lambda x, y, c, z: (2 * x - z, swap_y(y), c, x))
+REFLECT_FAR = route(lambda x, y, c, z: (2 * x - z, swap_y(y) + 2, c, x))
 OTHER_CORE = route(lambda x, y, c, z: (x, y, 1 - c, z))
 NEXT_X = route(lambda x, y, c, z: (x + 1, y, c, z))
 LAST_X = route(lambda x, y, c, z: (x - 1, y, c, z))
@@ -55,13 +54,8 @@
     return lax.ppermute(value, AXES, pairs)
 
 
-def ring_of_four(own, forward, backward):
-    half = own.shape[0] // 2
-    behind = send(own, forward)
-    ahead = send(own, backward)
-    far_a = send(behind[:half], forward)
-    far_b = send(ahead[half:], backward)
-    return own, behind, ahead, far_a, far_b
+def together(*values):
+    return lax.optimization_barrier(values)
 
 
 def spread(tile, ids, coarse_pairs, store):
@@ -83,10 +77,24 @@
         store(g, out)
 
 
-def galerkin(cols_ref, core_ref, a_ref, pc_ref, pr_ref, own_ref, other_ref, dense, turned, hi, lo):
+def galerkin(cols_ref, core_ref, slot_c, slot_r, a_hbm, *refs):
+    pc_in, pr_in, refs = refs[:10], refs[10:15], refs[15:]
+    own_ref, other_ref, a_ref, pc_ref, pr_ref, dense, turned, hi, lo, sems = refs
     core = core_ref[0]
     pieces = pc_ref.shape[0]
     fine_rows = a_ref.shape[0]
+    copies = []
+    for group, held in ((pc_in, pc_ref), (pr_in, pr_ref)):
+        at = 0
+        for ref in group:
+            here = held.at[pl.ds(at, ref.shape[0])]
+            copies.append(pltpu.make_async_copy(ref, here, sems.at[len(copies)]))
+            at += ref.shape[0]
+    copies.append(pltpu.make_async_copy(a_hbm, a_ref, sems.at[len(copies)]))
+    for copy in copies:
+        copy.start()
+    for copy in copies[:10]:
+        copy.wait()
 
     @pl.loop(0, pieces)
     def _(piece):
@@ -95,9 +103,12 @@
             ids = pc_ref[piece, pl.ds(4 * BS, PAD), :].astype(F32)[b : b + 1]
 
             def store(g, out):
-                dense[4 * piece + b, :, 128 * g : 128 * (g + 1)] = out.astype(BF16)
+                dense[4 * slot_c[piece] + b, :, 128 * g : 128 * (g + 1)] = out.astype(BF16)
 
             spread(tile, ids, 8, store)
+
+    for copy in copies[10:15]:
+        copy.wait()
 
     @pl.loop(0, pr_ref.shape[0])
     def _(piece):
@@ -120,8 +131,10 @@
                     hit = jnp.broadcast_to(where[m] == float(n), (BS, 128))
                     out = jnp.where(hit, flipped[BS * m : BS * (m + 1)], out)
                 slot = core if n % 2 == 0 else 1 - core
-                at = pl.multiple_of(256 * piece + 128 * pair, 128)
+                at = pl.multiple_of(256 * slot_r[piece] + 128 * pair, 128)
                 turned[slot, pl.ds(BS * (n // 2), BS), pl.ds(at, 128)] = out.astype(BF16)
+
+    copies[15].wait()
 
     @pl.loop(0, fine_rows)
     def _(i):
@@ -155,64 +168,111 @@
                     ]
 
 
-def compute(cols, core, a, pc, pr):
+def compute(cols, core, slot_c, slot_r, a, pc, pr):
     half = jax.ShapeDtypeStruct((64, BS, 128), F32)
     vmem = pl.BlockSpec(memory_space=pltpu.VMEM)
     smem = pl.BlockSpec(memory_space=pltpu.SMEM)
+    hbm = pl.BlockSpec(memory_space=pl.ANY)
     rows = a.shape[0] * BS
+    piece = pc[0].shape[1:]
     return pl.pallas_call(
         galerkin,
         out_shape=(half, half),
-        in_specs=[smem, smem, vmem, vmem, vmem],
+        in_specs=[smem] * 4 + [hbm] * 16,
         out_specs=(vmem, vmem),
         scratch_shapes=[
+            pltpu.VMEM(a.shape, BF16),
+            pltpu.VMEM((16,) + piece, BF16),
+            pltpu.VMEM((8,) + piece, BF16),
             pltpu.VMEM((64, BS, 1024), BF16),
             pltpu.VMEM((2, 512, rows), BF16),
             pltpu.VMEM((rows, 1024), BF16),
             pltpu.VMEM((rows, 1024), BF16),
+            pltpu.SemaphoreType.DMA((16,)),
         ],
         compiler_params=pltpu.CompilerParams(vmem_limit_bytes=48 << 20),
         name="galerkin",
-    )(cols, core, a, pc, pr)
+    )(cols, core, slot_c, slot_r, a, *pc, *pr)
 
 
 def gather_pieces(piece):
-    near = send(piece, MIRROR)
-    far = send(piece, MIRROR_FAR)
-    yh = lax.axis_index("yh")
-    x = lax.axis_index("x")
-    z = lax.axis_index("z")
-    yl = lax.axis_index("yl")
-    rows = piece.shape[0]
-    pair = jnp.stack([jnp.where(yh == 0, near, far), jnp.where(yh == 0, far, near)])
-    own, behind, ahead, far_a, far_b = ring_of_four(pair, NEXT_X, LAST_X)
-    opposite = jnp.concatenate([far_a, far_b])
-    ring = jnp.stack([own, ahead, opposite, behind])
-    ring = jnp.roll(ring, x, axis=0)
-    half = ring.reshape(8, rows, piece.shape[1])
-    other = send(half, OTHER_CORE)
-    core = lax.axis_index("core")
-    pc = jnp.concatenate([jnp.where(core == 0, half, other), jnp.where(core == 0, other, half)])
-
-    beside = send(piece, BESIDE)
-    pair = jnp.stack([jnp.where(yl == 0, piece, beside), jnp.where(yl == 0, beside, piece)])
-    own, behind, ahead, far_a, far_b = ring_of_four(pair, NEXT_Z, LAST_Z)
-    opposite = jnp.concatenate([far_a, far_b])
-    ring = jnp.stack([own, ahead, opposite, behind])
-    ring = jnp.roll(ring, z, axis=0)
-    pr = ring.reshape(8, rows, piece.shape[1])
-    return pc, pr
+    near, far, beside = together(
+        send(piece, REFLECT), send(piece, REFLECT_FAR), send(piece, BESIDE)
+    )
+    c0 = jnp.concatenate([near, far])
+    r0 = jnp.concatenate([piece, beside])
+    c1, c2, r1, r2, d0 = together(
+        send(c0, NEXT_X), send(c0, LAST_X), send(r0, NEXT_Z), send(r0, LAST_Z), send(c0, OTHER_CORE)
+    )
+    c3, c4, r3, r4, d1, d2 = together(
+        send(c1[:1], NEXT_X),
+        send(c2[1:], LAST_X),
+        send(r1[:1], NEXT_Z),
+        send(r2[1:], LAST_Z),
+        send(c1, OTHER_CORE),
+        send(c2, OTHER_CORE),
+    )
+    d3, d4 = send(c3, OTHER_CORE), send(c4, OTHER_CORE)
+    return (c0, c1, c2, c3, c4, d0, d1, d2, d3, d4), (r0, r1, r2, r3, r4)
+
+
+def slots():
+    x, yh, core, z, yl = (lax.axis_index(name).astype(jnp.int32) for name in AXES)
+    step = jnp.array([0, 0, -1, -1, 1, 1, 2, 2], jnp.int32)
+    side = jnp.array([0, 1, 0, 1, 0, 1, 0, 1], jnp.int32)
+    mine = 2 * ((2 * z - x - step) % 4) + (yh ^ side)
+    slot_c = jnp.concatenate([mine + 8 * core, mine + 8 * (1 - core)])
+    slot_r = 2 * ((z + step) % 4) + (yl ^ side)
+    return core.reshape(1), slot_c, slot_r
+
+
+def pack(a_ref, b_ref, out_ref):
+    total = a_ref[...] + b_ref[...]
+    largest = jnp.max(jnp.abs(total), axis=1, keepdims=True)
+    power = jnp.clip(jnp.ceil(jnp.log2(jnp.maximum(largest, 1e-36))), -110.0, 60.0)
+    scaled = total * jnp.exp2(15.0 - power)
+    scaled = jnp.clip(jnp.floor(scaled + 0.5), -32767.0, 32767.0)
+    out_ref[:, :BS, :] = scaled.astype(jnp.int32).astype(jnp.int16)
+    power = jnp.broadcast_to(power, (power.shape[0], ROWS - BS, 128))
+    out_ref[:, BS:, :] = power.astype(jnp.int32).astype(jnp.int16)
+
+
+def unpack(in_ref, out_ref):
+    def step(j, total):
+        value = in_ref[j].astype(jnp.int32).astype(F32)
+        return total + value[:BS] * jnp.exp2(value[BS : BS + 1] - 15.0)
+
+    out_ref[...] = lax.fori_loop(0, in_ref.shape[0], step, jnp.zeros((BS, 128), F32), unroll=4)
+
+
+def packed_sum(a, b):
+    block = pl.BlockSpec((8, BS, 128), lambda i: (i, 0, 0))
+    return pl.pallas_call(
+        pack,
+        grid=(8,),
+        out_shape=jax.ShapeDtypeStruct((64, ROWS, 128), jnp.int16),
+        in_specs=[block, block],
+        out_specs=pl.BlockSpec((8, ROWS, 128), lambda i: (i, 0, 0)),
+        name="pack",
+    )(a, b)
+
+
+def unpacked_sum(mixed):
+    return pl.pallas_call(
+        unpack, out_shape=jax.ShapeDtypeStruct((BS, 128), F32), name="unpack"
+    )(mixed)
 
 
 def shards(a_vals, a_cols, p_vals, p_cols):
     ids = jnp.repeat(p_cols.astype(BF16), BS, axis=1)
-    piece = jnp.concatenate([p_vals.reshape(4 * BS, 4 * BS), ids, jnp.zeros((PAD - 4, 4 * BS), BF16)])
-    pc, pr = gather_pieces(piece)
-    core = lax.axis_index("core").astype(jnp.int32).reshape(1)
-    own, other = compute(a_cols[:, 0], core, a_vals[:, 0], pc, pr)
-    total = own + send(other, OTHER_CORE)
-    mixed = lax.all_to_all(total, ("x", "yh", "z", "yl"), 0, 0, tiled=True)
-    return jnp.sum(mixed, axis=0)
+    blank = jnp.zeros((PAD - 4, 4 * BS), BF16)
+    piece = jnp.concatenate([p_vals.reshape(4 * BS, 4 * BS), ids, blank])
+    pc, pr = gather_pieces(piece[None])
+    core, slot_c, slot_r = slots()
+    own, other = compute(a_cols[:, 0], core, slot_c, slot_r, a_vals[:, 0], pc, pr)
+    packed = packed_sum(own, send(other, OTHER_CORE))
+    mixed = lax.all_to_all(packed, ("x", "yh", "z", "yl"), 0, 0, tiled=True)
+    return unpacked_sum(mixed)
 
 
 def solution(mesh):

time: 156 us -> 133 us (0.85)
  waiting for transfers between devices: 34.5 us -> 22.9 us
  blocking collectives: 40.1 us -> 31.5 us
  Pallas kernels: 39.3 us -> 47.5 us
  starting transfers between devices: 33 us -> 26.7 us
  other arithmetic: 7.58 us -> 1.86 us
    ppermute x13 -> x17, waiting for transfers between devices: 34.5 us -> 22.9 us  [send(): return lax.ppermute(value, AXES, pairs)]
    all_to_all x1, blocking collectives: 40.1 us -> 31.5 us  [shards(): mixed = lax.all_to_all(packed, ('x', 'yh', 'z', 'yl'), 0, 0, tiled=True)]
    pallas_call x1 -> x3, Pallas kernels: 39.3 us -> 47.5 us  [the longest x1 39 us: compute(): pl.pallas_call(galerkin, out_shape=(half, half), in_specs=[smem] * 4 + [h...]
    ppermute x13 -> x17, starting transfers between devices: 33 us -> 26.7 us  [send(): return lax.ppermute(value, AXES, pairs)]
    concatenate x4 -> x2, other arithmetic: 5.24 us -> 0.1 us  [the longest x1 0.07 us: slots(): slot_c = jnp.concatenate([mine + 8 * core, mine + 8 * (1 - core)])]
  transfers between devices with their start and end apart: 13 -> 17, of which waited for: 8 -> 12; matrix products, arithmetic and copies ran while one was open for 2% -> 0% of each run, Pallas kernels for 0% -> 0%
where the time goes in v2:
time: 133 us; the launch traced here: 132 us
  Pallas kernels  47.5 us (36%)
  blocking collectives  31.5 us (24%)
  starting transfers between devices  26.7 us (20%)
  waiting for transfers between devices  22.9 us (17%)
  other arithmetic  1.86 us (1%)
  local copies, waits for them, and re-layouts  1.71 us (1%)
    pallas_call x1, Pallas kernels, compute(): pl.pallas_call(galerkin, out_shape=(half, half), in_specs=[smem] * 4 + [h...  39 us
    all_to_all x1, blocking collectives, shards(): mixed = lax.all_to_all(packed, ('x', 'yh', 'z', 'yl'), 0, 0, tiled=True)  31.5 us
    ppermute x17, starting transfers between devices, send(): return lax.ppermute(value, AXES, pairs)  26.7 us
    ppermute x17, waiting for transfers between devices, send(): return lax.ppermute(value, AXES, pairs)  22.9 us
    pallas_call x1, Pallas kernels, packed_sum(): pl.pallas_call(pack, grid=(8,), out_shape=jax.ShapeDtypeStruct((64, ROWS,...  6.2 us
  transfers between devices with their start and end apart: 17, of which 12 were waited for; matrix products, arithmetic and copies ran while one was open for 0% of the time, Pallas kernels for 0%

profile of v2, /device:TPU:0, one launch (start us, length us, event | category | flops | bytes accessed | tf_op | source)
XLA Modules:
  0.0 132.3 jit_solution(2698774608169600740)
XLA Ops:
  0.0 0.0 copy-start.2
  0.0 0.0 copy-start.3
  0.0 0.0 copy-start.4
  0.0 0.0 copy-start.1
  0.0 0.7 convert_element_type.3
  0.7 0.1 broadcast_in_dim.9
  0.8 0.1 reshape.11
  0.9 0.1 pad.4.clone
  1.0 1.0 maximum_bitcast_fusion
  2.0 1.8 %collective-permute-start.2 = (bf16[1,272,256]{2,1,0:T(8,128)(2,1)S(1)}, bf16[1,272,256]{2,1,0:T(8,128)(2,1)S(1)}, u32[]{:S(2)}, u32[]{:S(2)}) collective-permute-start(bf16[1,272,256]{2,1,0:T(8,128)(2,1)S(1)} %maximum_bitcast_fusion), channel_id=1, source_target_pairs={{0,1},{1,0},{2,3},{3,2},{4,5},{5,4},{6,7},{7,6},{8,9},{9,8},{10,11... | collective-permute-start | bytes 417800 | tf_op jit(solution)/shard_map/ppermute | solution.py:54
  3.8 2.9 %collective-permute-start.1 = (bf16[1,272,256]{2,1,0:T(8,128)(2,1)S(1)}, bf16[1,272,256]{2,1,0:T(8,128)(2,1)S(1)}, u32[]{:S(2)}, u32[]{:S(2)}) collective-permute-start(bf16[1,272,256]{2,1,0:T(8,128)(2,1)S(1)} %maximum_bitcast_fusion), channel_id=1, source_target_pairs={{0,16},{1,0},{2,112},{3,96},{4,80},{5,64},{6,48},{7,32},{8,24},{9,... | collective-permute-start | bytes 417800 | tf_op jit(solution)/shard_map/ppermute | solution.py:54
  6.7 0.7 collective-permute-start
  7.3 1.3 collective-permute-done.2
  8.6 1.8 %collective-permute-done.1 = bf16[1,272,256]{2,1,0:T(8,128)(2,1)S(1)} collective-permute-done((bf16[1,272,256]{2,1,0:T(8,128)(2,1)S(1)}, bf16[1,272,256]{2,1,0:T(8,128)(2,1)S(1)}, u32[]{:S(2)}, u32[]{:S(2)}) %collective-permute-start.1) | collective-permute-done | bytes 139296 | tf_op jit(solution)/shard_map/ppermute | solution.py:54
  10.4 0.0 collective-permute-done
  10.5 0.1 collective-permute-start.7
  10.6 11.9 %collective-permute-start.4 = (bf16[2,272,256]{2,1,0:T(8,128)(2,1)S(1)}, bf16[2,272,256]{2,1,0:T(8,128)(2,1)S(1)}, u32[]{:S(2)}, u32[]{:S(2)}) collective-permute-start(bf16[2,272,256]{2,1,0:T(8,128)(2,1)S(1)} %constant_dynamic-update-slice_fusion.refs_0_), channel_id=1, source_target_pairs={{0,96},{1,97},{2,98},{3,99},{4,100},{5,101},{6,102},{7,103},{8,104... | collective-permute-start | bytes 835592 | tf_op jit(solution)/shard_map/ppermute | solution.py:54
  22.4 0.0 collective-permute-start.3
  22.4 2.5 %collective-permute-start.6 = (bf16[2,272,256]{2,1,0:T(8,128)(2,1)S(1)}, bf16[2,272,256]{2,1,0:T(8,128)(2,1)S(1)}, u32[]{:S(2)}, u32[]{:S(2)}) collective-permute-start(bf16[2,272,256]{2,1,0:T(8,128)(2,1)S(1)} %pad_maximum_fusion.refs_10_), channel_id=1, source_target_pairs={{0,6},{1,7},{2,0},{3,1},{4,2},{5,3},{6,4},{7,5},{8,14},{9,15},{10,... | collective-permute-start | bytes 835592 | tf_op jit(solution)/shard_map/ppermute | solution.py:54
  25.0 0.9 collective-permute-start.5
  25.8 0.0 collective-permute-done.7.refs_5_
  25.8 3.1 %collective-permute-done.4.refs_2_ = bf16[2,272,256]{2,1,0:T(8,128)(2,1)S(1)} collective-permute-done((bf16[2,272,256]{2,1,0:T(8,128)(2,1)S(1)}, bf16[2,272,256]{2,1,0:T(8,128)(2,1)S(1)}, u32[]{:S(2)}, u32[]{:S(2)}) %collective-permute-start.4) | collective-permute-done | bytes 278560 | tf_op jit(solution)/shard_map/ppermute | solution.py:54
  28.9 3.4 %collective-permute-done.3.refs_1_ = bf16[2,272,256]{2,1,0:T(8,128)(2,1)S(1)} collective-permute-done((bf16[2,272,256]{2,1,0:T(8,128)(2,1)S(1)}, bf16[2,272,256]{2,1,0:T(8,128)(2,1)S(1)}, u32[]{:S(2)}, u32[]{:S(2)}) %collective-permute-start.3) | collective-permute-done | bytes 278560 | tf_op jit(solution)/shard_map/ppermute | solution.py:54
  32.3 0.4 collective-permute-done.6.refs_12_
  32.7 1.8 %collective-permute-done.5.refs_11_ = bf16[2,272,256]{2,1,0:T(8,128)(2,1)S(1)} collective-permute-done((bf16[2,272,256]{2,1,0:T(8,128)(2,1)S(1)}, bf16[2,272,256]{2,1,0:T(8,128)(2,1)S(1)}, u32[]{:S(2)}, u32[]{:S(2)}) %collective-permute-start.5) | collective-permute-done | bytes 278560 | tf_op jit(solution)/shard_map/ppermute | solution.py:54
  34.6 1.2 collective-permute-start.9
  35.8 0.0 collective-permute-start.12
  35.8 0.5 collective-permute-start.13
  36.3 0.9 collective-permute-start.8
  37.3 1.5 %collective-permute-start.11 = (bf16[1,272,256]{2,1,0:T(8,128)(2,1)S(1)}, bf16[1,272,256]{2,1,0:T(8,128)(2,1)S(1)}, u32[]{:S(2)}, u32[]{:S(2)}) collective-permute-start(bf16[1,272,256]{2,1,0:T(8,128)(2,1)S(1)} %slice.15), channel_id=1, source_target_pairs={{0,6},{1,7},{2,0},{3,1},{4,2},{5,3},{6,4},{7,5},{8,14},{9,15},{10,... | collective-permute-start | bytes 417800 | tf_op jit(solution)/shard_map/ppermute | solution.py:54
  38.8 0.9 collective-permute-done.9.refs_4_
  39.7 1.0 collective-permute-start.10
  40.7 0.0 copy-done.2
  40.7 0.0 copy-done.3
  40.7 0.0 copy-done.4
  40.7 2.4 %collective-permute-done.8.refs_3_ = bf16[1,272,256]{2,1,0:T(8,128)(2,1)S(1)} collective-permute-done((bf16[1,272,256]{2,1,0:T(8,128)(2,1)S(1)}, bf16[1,272,256]{2,1,0:T(8,128)(2,1)S(1)}, u32[]{:S(2)}, u32[]{:S(2)}) %collective-permute-start.8) | collective-permute-done | bytes 139296 | tf_op jit(solution)/shard_map/ppermute | solution.py:54
  43.2 0.0 collective-permute-done.11.refs_14_
  43.2 2.8 %collective-permute-done.10.refs_13_ = bf16[1,272,256]{2,1,0:T(8,128)(2,1)S(1)} collective-permute-done((bf16[1,272,256]{2,1,0:T(8,128)(2,1)S(1)}, bf16[1,272,256]{2,1,0:T(8,128)(2,1)S(1)}, u32[]{:S(2)}, u32[]{:S(2)}) %collective-permute-start.10) | collective-permute-done | bytes 139296 | tf_op jit(solution)/shard_map/ppermute | solution.py:54
  45.9 0.0 collective-permute-done.12.refs_6_
  45.9 0.0 collective-permute-done.13.refs_7_
  46.0 0.0 collective-permute-start.14
  46.0 0.5 collective-permute-start.15
  46.5 0.0 copy-done.1
  46.5 0.1 copy.7
  46.5 0.1 pad_add_fusion.slot_c
  46.6 0.7 collective-permute-done.14.refs_8_
  47.3 0.2 collective-permute-done.15.refs_9_
  47.5 39.0 %galerkin.1 = (f32[64,64,128]{2,1,0:T(8,128)S(1)}, f32[64,64,128]{2,1,0:T(8,128)}) custom-call(s32[32,16]{1,0:T(8,128)S(1)} %bitcast.6, s32[1]{0:T(128)} %bitcast.1.core_ref, s32[16]{0:T(128)S(1)} %pad_add_fusion.slot_c, s32[8]{0:T(128)S(1)} %get-tuple-element.39.slot_r, bf16[32,64,1024]{2,1,0:T(8,128)(2,1)} %bitcast.7, ...), custom_call_target="tpu_custom_call" | custom-call | tf_op jit(solution)/shard_map/galerkin/pallas_call | solution.py:178
  86.6 0.0 copy-start
  86.6 1.3 copy-done
  87.9 0.3 collective-permute-start.16
  88.2 4.2 %collective-permute-done.16.b_ref = f32[64,64,128]{2,1,0:T(8,128)} collective-permute-done((f32[64,64,128]{2,1,0:T(8,128)}, f32[64,64,128]{2,1,0:T(8,128)}, u32[]{:S(2)}, u32[]{:S(2)}) %collective-permute-start.16) | collective-permute-done | bytes 2097184 | tf_op jit(solution)/shard_map/ppermute | solution.py:54
  92.4 6.2 %pack.1 = s16[64,72,128]{2,1,0:T(8,128)(2,1)} custom-call(f32[64,64,128]{2,1,0:T(8,128)} %copy-done, f32[64,64,128]{2,1,0:T(8,128)} %collective-permute-done.16.b_ref), custom_call_target="tpu_custom_call" | custom-call | tf_op jit(solution)/shard_map/pack/pallas_call | solution.py:250
  98.6 31.5 %all_to_all.5.in_ref = s16[64,72,128]{2,1,0:T(8,128)(2,1)} all-to-all(s16[64,72,128]{2,1,0:T(8,128)(2,1)} %pack.1), channel_id=1, replica_groups=mesh['x'=4,'yh'=2,'core'=2,'z'=4,'yl'=2] {'x','yh','z','yl'}, dimensions={0} | all-to-all | bytes 2359296 | tf_op jit(solution)/shard_map/all_to_all | solution.py:274
  130.1 2.3 %unpack.1 = f32[64,128]{1,0:T(8,128)} custom-call(s16[64,72,128]{2,1,0:T(8,128)(2,1)} %all_to_all.5.in_ref), custom_call_target="tpu_custom_call" | custom-call | tf_op jit(solution)/shard_map/unpack/pallas_call | solution.py:261
  (10 shorter events, 0.1 us)
Async XLA Ops:
  0.0 40.7 %copy-start.2 = (s32[8]{0:T(128)S(1)}, s32[8]{0:T(128)}, u32[]{:S(2)}) copy-start(s32[8]{0:T(128)} %constant.58) | copy-start | bytes 100
  0.0 40.7 %copy-start.3 = (s32[8]{0:T(128)S(1)}, s32[8]{0:T(128)}, u32[]{:S(2)}) copy-start(s32[8]{0:T(128)} %constant.53.clone) | copy-start | bytes 100
  0.0 40.7 %copy-start.4 = (s32[8]{0:T(128)S(1)}, s32[8]{0:T(128)}, u32[]{:S(2)}) copy-start(s32[8]{0:T(128)} %constant.52.clone) | copy-start | bytes 100
  0.0 46.5 %copy-start.1 = (s32[32,1,16]{0,2,1:T(8,128)S(1)}, s32[32,1,16]{0,2,1:T(8,128)}, u32[]{:S(2)}) copy-start(s32[32,1,16]{0,2,1:T(8,128)} %param.7) | copy-start | bytes 6148
  2.0 6.6 %collective-permute-start.2 = (bf16[1,272,256]{2,1,0:T(8,128)(2,1)S(1)}, bf16[1,272,256]{2,1,0:T(8,128)(2,1)S(1)}, u32[]{:S(2)}, u32[]{:S(2)}) collective-permute-start(bf16[1,272,256]{2,1,0:T(8,128)(2,1)S(1)} %maximum_bitcast_fusion), channel_id=1, source_target_pairs={{0,1},{1,0},{2,3},{3,2},{4,5},{5,4},{6,7},{7,6},{8,9},{9,8},{10,11... | collective-permute-start | bytes 417800 | tf_op jit(solution)/shard_map/ppermute | solution.py:54
  3.8 6.7 %collective-permute-start.1 = (bf16[1,272,256]{2,1,0:T(8,128)(2,1)S(1)}, bf16[1,272,256]{2,1,0:T(8,128)(2,1)S(1)}, u32[]{:S(2)}, u32[]{:S(2)}) collective-permute-start(bf16[1,272,256]{2,1,0:T(8,128)(2,1)S(1)} %maximum_bitcast_fusion), channel_id=1, source_target_pairs={{0,16},{1,0},{2,112},{3,96},{4,80},{5,64},{6,48},{7,32},{8,24},{9,... | collective-permute-start | bytes 417800 | tf_op jit(solution)/shard_map/ppermute | solution.py:54
  6.7 3.8 %collective-permute-start = (bf16[1,272,256]{2,1,0:T(8,128)(2,1)S(1)}, bf16[1,272,256]{2,1,0:T(8,128)(2,1)S(1)}, u32[]{:S(2)}, u32[]{:S(2)}) collective-permute-start(bf16[1,272,256]{2,1,0:T(8,128)(2,1)S(1)} %maximum_bitcast_fusion), channel_id=1, source_target_pairs={{0,0},{1,16},{2,96},{3,112},{4,64},{5,80},{6,32},{7,48},{8,8},{9,2... | collective-permute-start | bytes 417800 | tf_op jit(solution)/shard_map/ppermute | solution.py:54
  10.5 15.4 %collective-permute-start.7 = (bf16[2,272,256]{2,1,0:T(8,128)(2,1)S(1)}, bf16[2,272,256]{2,1,0:T(8,128)(2,1)S(1)}, u32[]{:S(2)}, u32[]{:S(2)}) collective-permute-start(bf16[2,272,256]{2,1,0:T(8,128)(2,1)S(1)} %constant_dynamic-update-slice_fusion.refs_0_), channel_id=1, source_target_pairs={{0,8},{1,9},{2,10},{3,11},{4,12},{5,13},{6,14},{7,15},{8,0},{9,1},... | collective-permute-start | bytes 835592 | tf_op jit(solution)/shard_map/ppermute | solution.py:54
  10.6 18.4 %collective-permute-start.4 = (bf16[2,272,256]{2,1,0:T(8,128)(2,1)S(1)}, bf16[2,272,256]{2,1,0:T(8,128)(2,1)S(1)}, u32[]{:S(2)}, u32[]{:S(2)}) collective-permute-start(bf16[2,272,256]{2,1,0:T(8,128)(2,1)S(1)} %constant_dynamic-update-slice_fusion.refs_0_), channel_id=1, source_target_pairs={{0,96},{1,97},{2,98},{3,99},{4,100},{5,101},{6,102},{7,103},{8,104... | collective-permute-start | bytes 835592 | tf_op jit(solution)/shard_map/ppermute | solution.py:54
  22.4 9.9 %collective-permute-start.3 = (bf16[2,272,256]{2,1,0:T(8,128)(2,1)S(1)}, bf16[2,272,256]{2,1,0:T(8,128)(2,1)S(1)}, u32[]{:S(2)}, u32[]{:S(2)}) collective-permute-start(bf16[2,272,256]{2,1,0:T(8,128)(2,1)S(1)} %constant_dynamic-update-slice_fusion.refs_0_), channel_id=1, source_target_pairs={{0,32},{1,33},{2,34},{3,35},{4,36},{5,37},{6,38},{7,39},{8,40},{9,... | collective-permute-start | bytes 835592 | tf_op jit(solution)/shard_map/ppermute | solution.py:54
  22.4 10.3 %collective-permute-start.6 = (bf16[2,272,256]{2,1,0:T(8,128)(2,1)S(1)}, bf16[2,272,256]{2,1,0:T(8,128)(2,1)S(1)}, u32[]{:S(2)}, u32[]{:S(2)}) collective-permute-start(bf16[2,272,256]{2,1,0:T(8,128)(2,1)S(1)} %pad_maximum_fusion.refs_10_), channel_id=1, source_target_pairs={{0,6},{1,7},{2,0},{3,1},{4,2},{5,3},{6,4},{7,5},{8,14},{9,15},{10,... | collective-permute-start | bytes 835592 | tf_op jit(solution)/shard_map/ppermute | solution.py:54
  25.0 9.6 %collective-permute-start.5 = (bf16[2,272,256]{2,1,0:T(8,128)(2,1)S(1)}, bf16[2,272,256]{2,1,0:T(8,128)(2,1)S(1)}, u32[]{:S(2)}, u32[]{:S(2)}) collective-permute-start(bf16[2,272,256]{2,1,0:T(8,128)(2,1)S(1)} %pad_maximum_fusion.refs_10_), channel_id=1, source_target_pairs={{0,2},{1,3},{2,4},{3,5},{4,6},{5,7},{6,0},{7,1},{8,10},{9,11},{10,... | collective-permute-start | bytes 835592 | tf_op jit(solution)/shard_map/ppermute | solution.py:54
  34.6 5.1 %collective-permute-start.9 = (bf16[1,272,256]{2,1,0:T(8,128)(2,1)S(1)}, bf16[1,272,256]{2,1,0:T(8,128)(2,1)S(1)}, u32[]{:S(2)}, u32[]{:S(2)}) collective-permute-start(bf16[1,272,256]{2,1,0:T(8,128)(2,1)S(1)} %slice.13), channel_id=1, source_target_pairs={{0,96},{1,97},{2,98},{3,99},{4,100},{5,101},{6,102},{7,103},{8,104... | collective-permute-start | bytes 417800 | tf_op jit(solution)/shard_map/ppermute | solution.py:54
  35.8 10.2 %collective-permute-start.12 = (bf16[2,272,256]{2,1,0:T(8,128)(2,1)S(1)}, bf16[2,272,256]{2,1,0:T(8,128)(2,1)S(1)}, u32[]{:S(2)}, u32[]{:S(2)}) collective-permute-start(bf16[2,272,256]{2,1,0:T(8,128)(2,1)S(1)} %collective-permute-done.3.refs_1_), channel_id=1, source_target_pairs={{0,8},{1,9},{2,10},{3,11},{4,12},{5,13},{6,14},{7,15},{8,0},{9,1},... | collective-permute-start | bytes 835592 | tf_op jit(solution)/shard_map/ppermute | solution.py:54
  35.8 10.2 %collective-permute-start.13 = (bf16[2,272,256]{2,1,0:T(8,128)(2,1)S(1)}, bf16[2,272,256]{2,1,0:T(8,128)(2,1)S(1)}, u32[]{:S(2)}, u32[]{:S(2)}) collective-permute-start(bf16[2,272,256]{2,1,0:T(8,128)(2,1)S(1)} %collective-permute-done.4.refs_2_), channel_id=1, source_target_pairs={{0,8},{1,9},{2,10},{3,11},{4,12},{5,13},{6,14},{7,15},{8,0},{9,1},... | collective-permute-start | bytes 835592 | tf_op jit(solution)/shard_map/ppermute | solution.py:54
  36.3 6.9 %collective-permute-start.8 = (bf16[1,272,256]{2,1,0:T(8,128)(2,1)S(1)}, bf16[1,272,256]{2,1,0:T(8,128)(2,1)S(1)}, u32[]{:S(2)}, u32[]{:S(2)}) collective-permute-start(bf16[1,272,256]{2,1,0:T(8,128)(2,1)S(1)} %slice.12), channel_id=1, source_target_pairs={{0,32},{1,33},{2,34},{3,35},{4,36},{5,37},{6,38},{7,39},{8,40},{9,... | collective-permute-start | bytes 417800 | tf_op jit(solution)/shard_map/ppermute | solution.py:54
  37.3 5.9 %collective-permute-start.11 = (bf16[1,272,256]{2,1,0:T(8,128)(2,1)S(1)}, bf16[1,272,256]{2,1,0:T(8,128)(2,1)S(1)}, u32[]{:S(2)}, u32[]{:S(2)}) collective-permute-start(bf16[1,272,256]{2,1,0:T(8,128)(2,1)S(1)} %slice.15), channel_id=1, source_target_pairs={{0,6},{1,7},{2,0},{3,1},{4,2},{5,3},{6,4},{7,5},{8,14},{9,15},{10,... | collective-permute-start | bytes 417800 | tf_op jit(solution)/shard_map/ppermute | solution.py:54
  39.7 6.3 %collective-permute-start.10 = (bf16[1,272,256]{2,1,0:T(8,128)(2,1)S(1)}, bf16[1,272,256]{2,1,0:T(8,128)(2,1)S(1)}, u32[]{:S(2)}, u32[]{:S(2)}) collective-permute-start(bf16[1,272,256]{2,1,0:T(8,128)(2,1)S(1)} %slice.14), channel_id=1, source_target_pairs={{0,2},{1,3},{2,4},{3,5},{4,6},{5,7},{6,0},{7,1},{8,10},{9,11},{10,... | collective-permute-start | bytes 417800 | tf_op jit(solution)/shard_map/ppermute | solution.py:54
  46.0 1.4 %collective-permute-start.14 = (bf16[1,272,256]{2,1,0:T(8,128)(2,1)S(1)}, bf16[1,272,256]{2,1,0:T(8,128)(2,1)S(1)}, u32[]{:S(2)}, u32[]{:S(2)}) collective-permute-start(bf16[1,272,256]{2,1,0:T(8,128)(2,1)S(1)} %collective-permute-done.8.refs_3_), channel_id=1, source_target_pairs={{0,8},{1,9},{2,10},{3,11},{4,12},{5,13},{6,14},{7,15},{8,0},{9,1},... | collective-permute-start | bytes 417800 | tf_op jit(solution)/shard_map/ppermute | solution.py:54
  46.0 1.6 %collective-permute-start.15 = (bf16[1,272,256]{2,1,0:T(8,128)(2,1)S(1)}, bf16[1,272,256]{2,1,0:T(8,128)(2,1)S(1)}, u32[]{:S(2)}, u32[]{:S(2)}) collective-permute-start(bf16[1,272,256]{2,1,0:T(8,128)(2,1)S(1)} %collective-permute-done.9.refs_4_), channel_id=1, source_target_pairs={{0,8},{1,9},{2,10},{3,11},{4,12},{5,13},{6,14},{7,15},{8,0},{9,1},... | collective-permute-start | bytes 417800 | tf_op jit(solution)/shard_map/ppermute | solution.py:54
  86.6 1.3 %copy-start = (f32[64,64,128]{2,1,0:T(8,128)}, f32[64,64,128]{2,1,0:T(8,128)S(1)}, u32[]{:S(2)}) copy-start(f32[64,64,128]{2,1,0:T(8,128)S(1)} %get-tuple-element.35.a_ref) | copy-start | bytes 6291460
  87.9 4.5 %collective-permute-start.16 = (f32[64,64,128]{2,1,0:T(8,128)}, f32[64,64,128]{2,1,0:T(8,128)}, u32[]{:S(2)}, u32[]{:S(2)}) collective-permute-start(f32[64,64,128]{2,1,0:T(8,128)} %get-tuple-element.36), channel_id=1, source_target_pairs={{0,8},{1,9},{2,10},{3,11},{4,12},{5,13},{6,14},{7,15},{8,0},{9,1},... | collective-permute-start | bytes 6291464 | tf_op jit(solution)/shard_map/ppermute | solution.py:54

commit v3 on v2

v3 whole, which is shorter than its diff:
```python
import jax
import jax.numpy as jnp
from jax import lax
from jax.experimental import pallas as pl
from jax.experimental.pallas import tpu as pltpu
from jax.sharding import Mesh
from jax.sharding import PartitionSpec as P

AXES = ("x", "yh", "core", "z", "yl")
SIZES = (4, 2, 2, 4, 2)
BF16 = jnp.bfloat16
F32 = jnp.float32
BS = 64
ROWS = 72
PAD = 16


def linear(place):
    index = 0
    for at, size in zip(place, SIZES):
        index = index * size + at
    return index


def route(target):
    pairs = []
    for x in range(4):
        for yh in range(2):
            for core in range(2):
                for z in range(4):
                    for yl in range(2):
                        to_x, to_y, to_core, to_z = target(x, 2 * yh + yl, core, z)
                        to_x, to_y, to_z = to_x % 4, to_y % 4, to_z % 4
                        to = linear((to_x, to_y // 2, to_core, to_z, to_y % 2))
                        pairs.append((linear((x, yh, core, z, yl)), to))
    return pairs


def swap_y(y):
    return (y % 2) * 2 + y // 2


REFLECT = route(lambda x, y, c, z: (2 * x - z, swap_y(y), c, x))
REFLECT_FAR = route(lambda x, y, c, z: (2 * x - z, swap_y(y) + 2, c, x))
OTHER_CORE = route(lambda x, y, c, z: (x, y, 1 - c, z))
NEXT_X = route(lambda x, y, c, z: (x + 1, y, c, z))
LAST_X = route(lambda x, y, c, z: (x - 1, y, c, z))
NEXT_Z = route(lambda x, y, c, z: (x, y, c, z + 1))
LAST_Z = route(lambda x, y, c, z: (x, y, c, z - 1))
ACROSS_Z = route(lambda x, y, c, z: (x, y, c, z + 2))
BESIDE = route(lambda x, y, c, z: (x, y ^ 1, c, z))


def send(value, pairs):
    return lax.ppermute(value, AXES, pairs)


def together(*values):
    return lax.optimization_barrier(values)


def rows16(row):
    return jnp.broadcast_to(row.astype(F32), (16, 128)).astype(BF16)


def choose(ids, number, values):
    out = [jnp.zeros((16, 128), BF16)] * 4
    for value, at in zip(values, ids):
        hit = at == number
        out = [jnp.where(hit, value[16 * t : 16 * (t + 1)], out[t]) for t in range(4)]
    return jnp.concatenate(out, axis=0)


def swap_halves(v):
    return jnp.concatenate([v[:, BS:], v[:, :BS]], axis=1)


def spread(tile, ids, store):
    low = lax.broadcasted_iota(jnp.int32, (BS, 128), 1) < BS
    low1 = lax.broadcasted_iota(jnp.int32, (1, 128), 1) < BS
    values, where = [], []
    for pair in range(2):
        v = tile[:, 128 * pair : 128 * (pair + 1)].astype(F32)
        r = swap_halves(v)
        d = ids[:, 128 * pair : 128 * (pair + 1)]
        e = swap_halves(d)
        values += [jnp.where(low, v, r).astype(BF16), jnp.where(low, r, v).astype(BF16)]
        for full in (jnp.where(low1, d, e), jnp.where(low1, e, d)):
            where.append(rows16(full - jnp.where(low1, 0.0, 1.0)))
    for g in range(8):
        store(g, choose(where, jnp.asarray(2.0 * g, BF16), values))


def fine_product(cols_ref, slot_c, a_hbm, *refs):
    pc_in, (hi, lo, a_ref, pc_ref, dense, sems) = refs[:10], refs[10:]
    copies, at = [], 0
    for ref in pc_in:
        here = pc_ref.at[pl.ds(at, ref.shape[0])]
        copies.append(pltpu.make_async_copy(ref, here, sems.at[len(copies)]))
        at += ref.shape[0]
    fetch = pltpu.make_async_copy(a_hbm, a_ref, sems.at[10])
    fetch.start()
    for copy in copies:
        copy.start()
    for copy in copies:
        copy.wait()

    @pl.loop(0, pc_ref.shape[0])
    def _(piece):
        ids = pc_ref[piece, pl.ds(4 * BS, PAD), :].astype(F32)
        for b in range(4):

            def store(g, out):
                dense[4 * slot_c[piece] + b, :, 128 * g : 128 * (g + 1)] = out

            spread(pc_ref[piece, pl.ds(BS * b, BS), :], ids[b : b + 1], store)

    fetch.wait()

    @pl.loop(0, a_ref.shape[0])
    def _(i):
        for n in range(4):
            total = None
            for k in range(4):
                tiles = [
                    dense[cols_ref[i, 4 * k + j], :, 256 * n : 256 * (n + 1)] for j in range(4)
                ]
                weights = jnp.concatenate(tiles, axis=0)
                left = a_ref[i, :, 256 * k : 256 * (k + 1)]
                part = jnp.dot(left, weights, preferred_element_type=F32)
                total = part if total is None else total + part
            top = total.astype(BF16)
            rows = pl.ds(pl.multiple_of(i * BS, BS), BS)
            hi[rows, 256 * n : 256 * (n + 1)] = top
            lo[rows, 256 * n : 256 * (n + 1)] = (total - top.astype(F32)).astype(BF16)


def turn(pr_ref, piece, turned, core, at):
    ids4 = pr_ref[piece, pl.ds(4 * BS, PAD), :].astype(F32)
    for pair in range(2):
        flipped = pr_ref[piece, pl.ds(128 * pair, 128), :].astype(F32).T.astype(BF16)
        where, values = [], []
        for m in range(4):
            a = ids4[2 * pair : 2 * pair + 1, BS * m : BS * (m + 1)]
            b = ids4[2 * pair + 1 : 2 * pair + 2, BS * m : BS * (m + 1)]
            where.append(rows16(jnp.concatenate([a, b], axis=1)))
            values.append(flipped[BS * m : BS * (m + 1)])
        for n in range(16):
            out = choose(where, jnp.asarray(float(n), BF16), values)
            slot = core if n % 2 == 0 else 1 - core
            to = pl.ds(pl.multiple_of(at + 128 * pair, 128), 128)
            turned[slot, pl.ds(BS * (n // 2), BS), to] = out


def half_product(turned, slot, hi, lo, out_ref):
    @pl.loop(0, 4)
    def _(n):
        at = pl.ds(pl.multiple_of(256 * n, 256), 256)
        left = turned[slot]
        c = jnp.dot(left, hi[:, at], preferred_element_type=F32)
        c = c + jnp.dot(left, lo[:, at], preferred_element_type=F32)
        for q in range(8):
            for j in range(2):
                out_ref[8 * q + 2 * n + j] = c[BS * q : BS * (q + 1), 128 * j : 128 * (j + 1)]


def other_half(core_ref, slot_r, hi, lo, r0, r1, r2, r3, turned, out_ref):
    at = 0
    for ref in (r0, r1, r2, r3):

        @pl.loop(0, 2)
        def _(side):
            turn(ref, side, turned, core_ref[0], 256 * slot_r[at + side])

        at += 2
    half_product(turned, 1, hi, lo, out_ref)


def own_half(hi, lo, turned, out_ref):
    half_product(turned, 0, hi, lo, out_ref)


VMEM = pl.BlockSpec(memory_space=pltpu.VMEM)
SMEM = pl.BlockSpec(memory_space=pltpu.SMEM)
ANY = pl.BlockSpec(memory_space=pl.ANY)
HALF = jax.ShapeDtypeStruct((64, BS, 128), F32)


def cost(flops):
    return pl.CostEstimate(flops=flops, bytes_accessed=1 << 23, transcendentals=0)


def run_fine_product(cols, slot_c, a, pc):
    rows = a.shape[0] * BS
    return pl.pallas_call(
        fine_product,
        out_shape=(pltpu.VMEM((rows, 1024), BF16),) * 2,
        in_specs=[SMEM] * 2 + [ANY] * 11,
        out_specs=(VMEM, VMEM),
        scratch_shapes=[
            pltpu.VMEM(a.shape, BF16),
            pltpu.VMEM((16,) + pc[0].shape[1:], BF16),
            pltpu.VMEM((64, BS, 1024), BF16),
            pltpu.SemaphoreType.DMA((11,)),
        ],
        compiler_params=pltpu.CompilerParams(vmem_limit_bytes=28 << 20),
        cost_estimate=cost(2 << 33),
        name="fine_product",
    )(cols, slot_c, a, *pc)


def run_other_half(core, slot_r, hi, lo, pr):
    return pl.pallas_call(
        other_half,
        out_shape=(pltpu.VMEM((2, 512, hi.shape[0]), BF16), HALF),
        in_specs=[SMEM] * 2 + [VMEM] * 6,
        out_specs=(VMEM, VMEM),
        compiler_params=pltpu.CompilerParams(vmem_limit_bytes=28 << 20),
        cost_estimate=cost(1 << 33),
        name="other_half",
    )(core, slot_r, hi, lo, *pr)


def run_own_half(hi, lo, turned):
    return pl.pallas_call(
        own_half,
        out_shape=HALF,
        in_specs=[VMEM] * 3,
        out_specs=VMEM,
        compiler_params=pltpu.CompilerParams(vmem_limit_bytes=28 << 20),
        cost_estimate=cost(1 << 33),
        name="own_half",
    )(hi, lo, turned)


def gather_pieces(piece):
    near, far, beside = together(
        send(piece, REFLECT), send(piece, REFLECT_FAR), send(piece, BESIDE)
    )
    c0 = jnp.concatenate([near, far])
    r0 = jnp.concatenate([piece, beside])
    c1, c2, d0 = together(send(c0, NEXT_X), send(c0, LAST_X), send(c0, OTHER_CORE))
    c3, c4, d1, d2, r0 = together(
        send(c1[:1], NEXT_X), send(c2[1:], LAST_X), send(c1, OTHER_CORE), send(c2, OTHER_CORE), r0
    )
    d3, d4 = send(c3, OTHER_CORE), send(c4, OTHER_CORE)
    r1, r2, r3 = send(r0, NEXT_Z), send(r0, LAST_Z), send(r0, ACROSS_Z)
    return (c0, c1, c2, c3, c4, d0, d1, d2, d3, d4), (r0, r1, r2, r3)


def slots():
    x, yh, core, z, yl = (lax.axis_index(name).astype(jnp.int32) for name in AXES)
    step = jnp.array([0, 0, -1, -1, 1, 1, 2, 2], jnp.int32)
    side = jnp.array([0, 1, 0, 1, 0, 1, 0, 1], jnp.int32)
    mine = 2 * ((2 * z - x - step) % 4) + (yh ^ side)
    slot_c = jnp.concatenate([mine + 8 * core, mine + 8 * (1 - core)])
    slot_r = 2 * ((z + step) % 4) + (yl ^ side)
    return core.reshape(1), slot_c, slot_r


def pack(a_ref, b_ref, out_ref):
    @pl.loop(0, a_ref.shape[0])
    def _(i):
        total = a_ref[i] + b_ref[i]
        largest = jnp.max(jnp.abs(total), axis=0, keepdims=True)
        power = jnp.clip(jnp.ceil(jnp.log2(jnp.maximum(largest, 1e-36))), -110.0, 60.0)
        scaled = jnp.floor(total * jnp.exp2(15.0 - power) + 0.5)
        scaled = jnp.minimum(scaled, 32767.0)
        out_ref[i, :BS, :] = scaled.astype(jnp.int32).astype(jnp.int16)
        power = jnp.broadcast_to(power, (ROWS - BS, 128))
        out_ref[i, BS:, :] = power.astype(jnp.int32).astype(jnp.int16)


def unpack(in_ref, out_ref):
    def step(j, total):
        value = in_ref[j].astype(jnp.int32).astype(F32)
        return total + value[:BS] * jnp.exp2(value[BS : BS + 1] - 15.0)

    out_ref[...] = lax.fori_loop(0, in_ref.shape[0], step, jnp.zeros((BS, 128), F32), unroll=4)


def packed_sum(a, b):
    return pl.pallas_call(
        pack,
        out_shape=jax.ShapeDtypeStruct((64, ROWS, 128), jnp.int16),
        in_specs=[VMEM, VMEM],
        out_specs=VMEM,
        name="pack",
    )(a, b)


def unpacked_sum(mixed):
    return pl.pallas_call(
        unpack, out_shape=jax.ShapeDtypeStruct((BS, 128), F32), name="unpack"
    )(mixed)


def shards(a_vals, a_cols, p_vals, p_cols):
    ids = jnp.repeat(p_cols.astype(BF16), BS, axis=1)
    blank = jnp.zeros((PAD - 4, 4 * BS), BF16)
    piece = jnp.concatenate([p_vals.reshape(4 * BS, 4 * BS), ids, blank])
    pc, pr = gather_pieces(piece[None])
    core, slot_c, slot_r = slots()
    hi, lo = run_fine_product(a_cols[:, 0], slot_c, a_vals[:, 0], pc)
    turned, other = run_other_half(core, slot_r, hi, lo, pr)
    met = send(other, OTHER_CORE)
    own = run_own_half(hi, lo, turned)
    packed = packed_sum(own, met)
    mixed = lax.all_to_all(packed, ("x", "yh", "z", "yl"), 0, 0, tiled=True)
    return unpacked_sum(mixed)


def solution(mesh):
    fine = Mesh(mesh.devices.reshape(SIZES), AXES)
    row, col = ("x", "yh", "core"), ("z", "yl")
    in_specs = (
        P(row, col, None, None),
        P(row, col, None),
        P(row + col, None, None),
        P(row + col, None),
    )
    return jax.shard_map(
        shards, mesh=fine, in_specs=in_specs, out_specs=P(row, col), check_vma=False
    )
```

time: 133 us -> 124 us (0.932)
  waiting for transfers between devices: 22.9 us -> 17.8 us
  local copies, waits for them, and re-layouts: 1.71 us -> 5.87 us
  Pallas kernels: 47.5 us -> 43.6 us
  blocking collectives: 31.5 us -> 28.2 us
    ppermute x17 -> x16, waiting for transfers between devices: 22.9 us -> 17.8 us  [send(): return lax.ppermute(value, AXES, pairs)]
    unnamed x12 -> x8, local copies, waits for them, and re-layouts: 1.42 us -> 5.59 us
    pallas_call x2 -> x4, Pallas kernels: 45.2 us -> 41.3 us  [the longest x1 22.3 us: run_fine_product(): pl.pallas_call(fine_product, out_shape=(pltpu.VMEM((rows, 1024), BF16),)...]
    all_to_all x1, blocking collectives: 31.5 us -> 28.2 us  [shards(): mixed = lax.all_to_all(packed, ('x', 'yh', 'z', 'yl'), 0, 0, tiled=True)]
    ppermute x17 -> x16, starting transfers between devices: 26.7 us -> 25.9 us  [send(): return lax.ppermute(value, AXES, pairs)]
  transfers between devices with their start and end apart: 17 -> 16, of which waited for: 12 -> 6; matrix products, arithmetic and copies ran while one was open for 0% -> 1% of each run, Pallas kernels for 0% -> 22%
where the time goes in v3:
time: 124 us
  Pallas kernels  43.6 us (35%)
  blocking collectives  28.2 us (23%)
  starting transfers between devices  25.9 us (21%)
  waiting for transfers between devices  17.8 us (14%)
  local copies, waits for them, and re-layouts  5.87 us (5%)
  other arithmetic  2.5 us (2%)
    all_to_all x1, blocking collectives, shards(): mixed = lax.all_to_all(packed, ('x', 'yh', 'z', 'yl'), 0, 0, tiled=True)  28.2 us
    ppermute x16, starting transfers between devices, send(): return lax.ppermute(value, AXES, pairs)  25.9 us
    pallas_call x1, Pallas kernels, run_fine_product(): pl.pallas_call(fine_product, out_shape=(pltpu.VMEM((rows, 1024), BF16),)...  22.3 us
    ppermute x16, waiting for transfers between devices, send(): return lax.ppermute(value, AXES, pairs)  17.8 us
    pallas_call x1, Pallas kernels, run_other_half(): pl.pallas_call(other_half, out_shape=(pltpu.VMEM((2, 512, hi.shape[0]), B...  8.22 us
    pallas_call x1, Pallas kernels, packed_sum(): pl.pallas_call(pack, out_shape=jax.ShapeDtypeStruct((64, ROWS, 128), jnp....  5.73 us
    unnamed x8, local copies, waits for them, and re-layouts  5.59 us
    pallas_call x1, Pallas kernels, run_own_half(): pl.pallas_call(own_half, out_shape=HALF, in_specs=[VMEM] * 3, out_specs=V...  5.1 us
  transfers between devices with their start and end apart: 16, of which 6 were waited for; matrix products, arithmetic and copies ran while one was open for 1% of the time, Pallas kernels for 22%

profile of v3, /device:TPU:0, one launch (start us, length us, event | category | flops | bytes accessed | tf_op | source)
XLA Modules:
  0.0 124.0 jit_solution(12248555406545971793)
XLA Ops:
  0.0 0.7 convert_element_type.3
  0.7 0.1 broadcast_in_dim.9
  0.8 0.1 reshape.10
  0.9 0.1 pad.4.clone
  0.9 1.0 maximum_bitcast_fusion
  1.9 1.8 %collective-permute-start.2 = (bf16[1,272,256]{2,1,0:T(8,128)(2,1)S(1)}, bf16[1,272,256]{2,1,0:T(8,128)(2,1)S(1)}, u32[]{:S(2)}, u32[]{:S(2)}) collective-permute-start(bf16[1,272,256]{2,1,0:T(8,128)(2,1)S(1)} %maximum_bitcast_fusion), channel_id=1, source_target_pairs={{0,1},{1,0},{2,3},{3,2},{4,5},{5,4},{6,7},{7,6},{8,9},{9,8},{10,11... | collective-permute-start | bytes 417800 | tf_op jit(solution)/shard_map/ppermute | solution.py:55
  3.7 2.9 %collective-permute-start.1 = (bf16[1,272,256]{2,1,0:T(8,128)(2,1)S(1)}, bf16[1,272,256]{2,1,0:T(8,128)(2,1)S(1)}, u32[]{:S(2)}, u32[]{:S(2)}) collective-permute-start(bf16[1,272,256]{2,1,0:T(8,128)(2,1)S(1)} %maximum_bitcast_fusion), channel_id=1, source_target_pairs={{0,16},{1,0},{2,112},{3,96},{4,80},{5,64},{6,48},{7,32},{8,24},{9,... | collective-permute-start | bytes 417800 | tf_op jit(solution)/shard_map/ppermute | solution.py:55
  6.6 0.7 collective-permute-start
  7.3 1.3 %collective-permute-done.2 = bf16[1,272,256]{2,1,0:T(8,128)(2,1)S(1)} collective-permute-done((bf16[1,272,256]{2,1,0:T(8,128)(2,1)S(1)}, bf16[1,272,256]{2,1,0:T(8,128)(2,1)S(1)}, u32[]{:S(2)}, u32[]{:S(2)}) %collective-permute-start.2) | collective-permute-done | bytes 139296 | tf_op jit(solution)/shard_map/ppermute | solution.py:55
  8.6 1.8 %collective-permute-done.1 = bf16[1,272,256]{2,1,0:T(8,128)(2,1)S(1)} collective-permute-done((bf16[1,272,256]{2,1,0:T(8,128)(2,1)S(1)}, bf16[1,272,256]{2,1,0:T(8,128)(2,1)S(1)}, u32[]{:S(2)}, u32[]{:S(2)}) %collective-permute-start.1) | collective-permute-done | bytes 139296 | tf_op jit(solution)/shard_map/ppermute | solution.py:55
  10.4 0.0 collective-permute-done
  10.4 0.1 collective-permute-start.5
  10.5 11.9 %collective-permute-start.4 = (bf16[2,272,256]{2,1,0:T(8,128)(2,1)S(1)}, bf16[2,272,256]{2,1,0:T(8,128)(2,1)S(1)}, u32[]{:S(2)}, u32[]{:S(2)}) collective-permute-start(bf16[2,272,256]{2,1,0:T(8,128)(2,1)S(1)} %constant_dynamic-update-slice_fusion.refs_0_), channel_id=1, source_target_pairs={{0,96},{1,97},{2,98},{3,99},{4,100},{5,101},{6,102},{7,103},{8,104... | collective-permute-start | bytes 835592 | tf_op jit(solution)/shard_map/ppermute | solution.py:55
  22.4 0.0 collective-permute-start.3
  22.4 0.0 collective-permute-done.5.refs_5_
  22.4 6.5 %collective-permute-done.4.refs_2_ = bf16[2,272,256]{2,1,0:T(8,128)(2,1)S(1)} collective-permute-done((bf16[2,272,256]{2,1,0:T(8,128)(2,1)S(1)}, bf16[2,272,256]{2,1,0:T(8,128)(2,1)S(1)}, u32[]{:S(2)}, u32[]{:S(2)}) %collective-permute-start.4) | collective-permute-done | bytes 278560 | tf_op jit(solution)/shard_map/ppermute | solution.py:55
  28.9 3.4 %collective-permute-done.3.refs_1_ = bf16[2,272,256]{2,1,0:T(8,128)(2,1)S(1)} collective-permute-done((bf16[2,272,256]{2,1,0:T(8,128)(2,1)S(1)}, bf16[2,272,256]{2,1,0:T(8,128)(2,1)S(1)}, u32[]{:S(2)}, u32[]{:S(2)}) %collective-permute-start.3) | collective-permute-done | bytes 278560 | tf_op jit(solution)/shard_map/ppermute | solution.py:55
  32.3 0.1 collective-permute-start.8
  32.4 0.6 collective-permute-start.9
  33.0 0.9 collective-permute-start.7
  33.9 1.1 collective-permute-start.6
  35.0 0.7 broadcast_add_fusion.1
  35.7 2.9 %collective-permute-done.7.refs_4_ = bf16[1,272,256]{2,1,0:T(8,128)(2,1)S(1)} collective-permute-done((bf16[1,272,256]{2,1,0:T(8,128)(2,1)S(1)}, bf16[1,272,256]{2,1,0:T(8,128)(2,1)S(1)}, u32[]{:S(2)}, u32[]{:S(2)}) %collective-permute-start.7) | collective-permute-done | bytes 139296 | tf_op jit(solution)/shard_map/ppermute | solution.py:55
  38.6 1.9 %collective-permute-done.6.refs_3_ = bf16[1,272,256]{2,1,0:T(8,128)(2,1)S(1)} collective-permute-done((bf16[1,272,256]{2,1,0:T(8,128)(2,1)S(1)}, bf16[1,272,256]{2,1,0:T(8,128)(2,1)S(1)}, u32[]{:S(2)}, u32[]{:S(2)}) %collective-permute-start.6) | collective-permute-done | bytes 139296 | tf_op jit(solution)/shard_map/ppermute | solution.py:55
  40.5 0.0 collective-permute-done.8.refs_6_
  40.5 0.0 collective-permute-done.9.refs_7_
  40.5 0.0 collective-permute-start.10
  40.5 0.5 collective-permute-start.11
  41.0 0.8 copy.7
  41.8 0.1 pad_add_fusion.slot_c
  41.9 0.8 collective-permute-start.14
  42.7 4.5 %collective-permute-start.13 = (bf16[2,272,256]{2,1,0:T(8,128)(2,1)S(1)}, bf16[2,272,256]{2,1,0:T(8,128)(2,1)S(1)}, u32[]{:S(2)}, u32[]{:S(2)}) collective-permute-start(bf16[2,272,256]{2,1,0:T(8,128)(2,1)S(1)} %pad_maximum_fusion.r0), channel_id=1, source_target_pairs={{0,6},{1,7},{2,0},{3,1},{4,2},{5,3},{6,4},{7,5},{8,14},{9,15},{10,... | collective-permute-start | bytes 835592 | tf_op jit(solution)/shard_map/ppermute | solution.py:55
  47.2 0.0 collective-permute-start.12
  47.2 0.0 collective-permute-done.10.refs_8_
  47.2 0.0 collective-permute-done.11.refs_9_
  47.2 0.0 copy-start.1
  47.2 2.2 %copy-done.1 = bf16[32,1,64,1024]{3,2,1,0:T(8,128)(2,1)S(1)} copy-done((bf16[32,1,64,1024]{3,2,1,0:T(8,128)(2,1)S(1)}, bf16[32,1,64,1024]{3,2,1,0:T(8,128)(2,1)}, u32[]{:S(2)}) %copy-start.1) | copy-done | bytes 4194328
  49.4 22.3 %fine_product.1 = (bf16[2048,1024]{1,0:T(8,128)(2,1)S(1)}, bf16[2048,1024]{1,0:T(8,128)(2,1)S(1)}) custom-call(s32[32,16]{1,0:T(8,128)S(1)} %bitcast.6, s32[16]{0:T(128)S(1)} %pad_add_fusion.slot_c, bf16[32,64,1024]{2,1,0:T(8,128)(2,1)S(1)} %bitcast.7, bf16[2,272,256]{2,1,0:T(8,128)(2,1)S(1)} %constant_dynamic-update-slice_fusion.refs_0_, ...), custom_call_target="tpu_custom_call" | custom-call | flops 17179869184 | bytes 8388608 | tf_op jit(solution)/shard_map/fine_product/pallas_call | solution.py:195
  71.7 0.0 collective-permute-done.14.r3
  71.7 0.0 collective-permute-done.13.r2
  71.7 0.0 collective-permute-done.12.r1
  71.8 8.2 %other_half.1 = (bf16[2,512,2048]{2,1,0:T(8,128)(2,1)S(1)}, f32[64,64,128]{2,1,0:T(8,128)S(1)}) custom-call(s32[1]{0:T(128)} %bitcast.4.core_ref, s32[8]{0:T(128)S(1)} %get-tuple-element.37.slot_r, bf16[2048,1024]{1,0:T(8,128)(2,1)S(1)} %get-tuple-element.30.hi, bf16[2048,1024]{1,0:T(8,128)(2,1)S(1)} %get-tuple-element.31.lo, ...), custom_call_target="tpu_custom_call" | custom-call | flops 8589934592 | bytes 8388608 | tf_op jit(solution)/shard_map/other_half/pallas_call | solution.py:213
  80.0 0.1 collective-permute-start.15
  80.1 5.1 %own_half.1.a_ref = f32[64,64,128]{2,1,0:T(8,128)S(1)} custom-call(bf16[2048,1024]{1,0:T(8,128)(2,1)S(1)} %get-tuple-element.30.hi, bf16[2048,1024]{1,0:T(8,128)(2,1)S(1)} %get-tuple-element.31.lo, bf16[2,512,2048]{2,1,0:T(8,128)(2,1)S(1)} %get-tuple-element.33.turned), custom_call_target="tpu_custom_call" | custom-call | flops 8589934592 | bytes 8388608 | tf_op jit(solution)/shard_map/own_half/pallas_call | solution.py:225
  85.2 0.0 copy-start
  85.2 1.3 %copy-done = f32[64,64,128]{2,1,0:T(8,128)} copy-done((f32[64,64,128]{2,1,0:T(8,128)}, f32[64,64,128]{2,1,0:T(8,128)S(1)}, u32[]{:S(2)}) %copy-start) | copy-done | bytes 2097176
  86.5 0.0 collective-permute-done.15.b_ref
  86.5 0.0 copy-start.2
  86.5 1.3 %copy-done.2 = f32[64,64,128]{2,1,0:T(8,128)} copy-done((f32[64,64,128]{2,1,0:T(8,128)}, f32[64,64,128]{2,1,0:T(8,128)S(1)}, u32[]{:S(2)}) %copy-start.2) | copy-done | bytes 2097176
  87.8 5.7 %pack.1 = s16[64,72,128]{2,1,0:T(8,128)(2,1)} custom-call(f32[64,64,128]{2,1,0:T(8,128)} %copy-done, f32[64,64,128]{2,1,0:T(8,128)} %copy-done.2), custom_call_target="tpu_custom_call" | custom-call | tf_op jit(solution)/shard_map/pack/pallas_call | solution.py:283
  93.6 28.2 %all_to_all.5.in_ref = s16[64,72,128]{2,1,0:T(8,128)(2,1)} all-to-all(s16[64,72,128]{2,1,0:T(8,128)(2,1)} %pack.1), channel_id=1, replica_groups=mesh['x'=4,'yh'=2,'core'=2,'z'=4,'yl'=2] {'x','yh','z','yl'}, dimensions={0} | all-to-all | bytes 2359296 | tf_op jit(solution)/shard_map/all_to_all | solution.py:309
  121.7 2.3 %unpack.1 = f32[64,128]{1,0:T(8,128)} custom-call(s16[64,72,128]{2,1,0:T(8,128)(2,1)} %all_to_all.5.in_ref), custom_call_target="tpu_custom_call" | custom-call | tf_op jit(solution)/shard_map/unpack/pallas_call | solution.py:293
  (7 shorter events, 0.1 us)
Async XLA Ops:
  1.9 6.6 %collective-permute-start.2 = (bf16[1,272,256]{2,1,0:T(8,128)(2,1)S(1)}, bf16[1,272,256]{2,1,0:T(8,128)(2,1)S(1)}, u32[]{:S(2)}, u32[]{:S(2)}) collective-permute-start(bf16[1,272,256]{2,1,0:T(8,128)(2,1)S(1)} %maximum_bitcast_fusion), channel_id=1, source_target_pairs={{0,1},{1,0},{2,3},{3,2},{4,5},{5,4},{6,7},{7,6},{8,9},{9,8},{10,11... | collective-permute-start | bytes 417800 | tf_op jit(solution)/shard_map/ppermute | solution.py:55
  3.7 6.7 %collective-permute-start.1 = (bf16[1,272,256]{2,1,0:T(8,128)(2,1)S(1)}, bf16[1,272,256]{2,1,0:T(8,128)(2,1)S(1)}, u32[]{:S(2)}, u32[]{:S(2)}) collective-permute-start(bf16[1,272,256]{2,1,0:T(8,128)(2,1)S(1)} %maximum_bitcast_fusion), channel_id=1, source_target_pairs={{0,16},{1,0},{2,112},{3,96},{4,80},{5,64},{6,48},{7,32},{8,24},{9,... | collective-permute-start | bytes 417800 | tf_op jit(solution)/shard_map/ppermute | solution.py:55
  6.6 3.8 %collective-permute-start = (bf16[1,272,256]{2,1,0:T(8,128)(2,1)S(1)}, bf16[1,272,256]{2,1,0:T(8,128)(2,1)S(1)}, u32[]{:S(2)}, u32[]{:S(2)}) collective-permute-start(bf16[1,272,256]{2,1,0:T(8,128)(2,1)S(1)} %maximum_bitcast_fusion), channel_id=1, source_target_pairs={{0,0},{1,16},{2,96},{3,112},{4,64},{5,80},{6,32},{7,48},{8,8},{9,2... | collective-permute-start | bytes 417800 | tf_op jit(solution)/shard_map/ppermute | solution.py:55
  10.4 12.0 %collective-permute-start.5 = (bf16[2,272,256]{2,1,0:T(8,128)(2,1)S(1)}, bf16[2,272,256]{2,1,0:T(8,128)(2,1)S(1)}, u32[]{:S(2)}, u32[]{:S(2)}) collective-permute-start(bf16[2,272,256]{2,1,0:T(8,128)(2,1)S(1)} %constant_dynamic-update-slice_fusion.refs_0_), channel_id=1, source_target_pairs={{0,8},{1,9},{2,10},{3,11},{4,12},{5,13},{6,14},{7,15},{8,0},{9,1},... | collective-permute-start | bytes 835592 | tf_op jit(solution)/shard_map/ppermute | solution.py:55
  10.5 18.4 %collective-permute-start.4 = (bf16[2,272,256]{2,1,0:T(8,128)(2,1)S(1)}, bf16[2,272,256]{2,1,0:T(8,128)(2,1)S(1)}, u32[]{:S(2)}, u32[]{:S(2)}) collective-permute-start(bf16[2,272,256]{2,1,0:T(8,128)(2,1)S(1)} %constant_dynamic-update-slice_fusion.refs_0_), channel_id=1, source_target_pairs={{0,96},{1,97},{2,98},{3,99},{4,100},{5,101},{6,102},{7,103},{8,104... | collective-permute-start | bytes 835592 | tf_op jit(solution)/shard_map/ppermute | solution.py:55
  22.4 9.9 %collective-permute-start.3 = (bf16[2,272,256]{2,1,0:T(8,128)(2,1)S(1)}, bf16[2,272,256]{2,1,0:T(8,128)(2,1)S(1)}, u32[]{:S(2)}, u32[]{:S(2)}) collective-permute-start(bf16[2,272,256]{2,1,0:T(8,128)(2,1)S(1)} %constant_dynamic-update-slice_fusion.refs_0_), channel_id=1, source_target_pairs={{0,32},{1,33},{2,34},{3,35},{4,36},{5,37},{6,38},{7,39},{8,40},{9,... | collective-permute-start | bytes 835592 | tf_op jit(solution)/shard_map/ppermute | solution.py:55
  32.3 8.2 %collective-permute-start.8 = (bf16[2,272,256]{2,1,0:T(8,128)(2,1)S(1)}, bf16[2,272,256]{2,1,0:T(8,128)(2,1)S(1)}, u32[]{:S(2)}, u32[]{:S(2)}) collective-permute-start(bf16[2,272,256]{2,1,0:T(8,128)(2,1)S(1)} %collective-permute-done.3.refs_1_), channel_id=1, source_target_pairs={{0,8},{1,9},{2,10},{3,11},{4,12},{5,13},{6,14},{7,15},{8,0},{9,1},... | collective-permute-start | bytes 835592 | tf_op jit(solution)/shard_map/ppermute | solution.py:55
  32.4 8.1 %collective-permute-start.9 = (bf16[2,272,256]{2,1,0:T(8,128)(2,1)S(1)}, bf16[2,272,256]{2,1,0:T(8,128)(2,1)S(1)}, u32[]{:S(2)}, u32[]{:S(2)}) collective-permute-start(bf16[2,272,256]{2,1,0:T(8,128)(2,1)S(1)} %collective-permute-done.4.refs_2_), channel_id=1, source_target_pairs={{0,8},{1,9},{2,10},{3,11},{4,12},{5,13},{6,14},{7,15},{8,0},{9,1},... | collective-permute-start | bytes 835592 | tf_op jit(solution)/shard_map/ppermute | solution.py:55
  33.0 5.7 %collective-permute-start.7 = (bf16[1,272,256]{2,1,0:T(8,128)(2,1)S(1)}, bf16[1,272,256]{2,1,0:T(8,128)(2,1)S(1)}, u32[]{:S(2)}, u32[]{:S(2)}) collective-permute-start(bf16[1,272,256]{2,1,0:T(8,128)(2,1)S(1)} %slice.7), channel_id=1, source_target_pairs={{0,96},{1,97},{2,98},{3,99},{4,100},{5,101},{6,102},{7,103},{8,104... | collective-permute-start | bytes 417800 | tf_op jit(solution)/shard_map/ppermute | solution.py:55
  33.9 6.6 %collective-permute-start.6 = (bf16[1,272,256]{2,1,0:T(8,128)(2,1)S(1)}, bf16[1,272,256]{2,1,0:T(8,128)(2,1)S(1)}, u32[]{:S(2)}, u32[]{:S(2)}) collective-permute-start(bf16[1,272,256]{2,1,0:T(8,128)(2,1)S(1)} %slice.6), channel_id=1, source_target_pairs={{0,32},{1,33},{2,34},{3,35},{4,36},{5,37},{6,38},{7,39},{8,40},{9,... | collective-permute-start | bytes 417800 | tf_op jit(solution)/shard_map/ppermute | solution.py:55
  40.5 6.7 %collective-permute-start.10 = (bf16[1,272,256]{2,1,0:T(8,128)(2,1)S(1)}, bf16[1,272,256]{2,1,0:T(8,128)(2,1)S(1)}, u32[]{:S(2)}, u32[]{:S(2)}) collective-permute-start(bf16[1,272,256]{2,1,0:T(8,128)(2,1)S(1)} %collective-permute-done.6.refs_3_), channel_id=1, source_target_pairs={{0,8},{1,9},{2,10},{3,11},{4,12},{5,13},{6,14},{7,15},{8,0},{9,1},... | collective-permute-start | bytes 417800 | tf_op jit(solution)/shard_map/ppermute | solution.py:55
  40.5 6.7 %collective-permute-start.11 = (bf16[1,272,256]{2,1,0:T(8,128)(2,1)S(1)}, bf16[1,272,256]{2,1,0:T(8,128)(2,1)S(1)}, u32[]{:S(2)}, u32[]{:S(2)}) collective-permute-start(bf16[1,272,256]{2,1,0:T(8,128)(2,1)S(1)} %collective-permute-done.7.refs_4_), channel_id=1, source_target_pairs={{0,8},{1,9},{2,10},{3,11},{4,12},{5,13},{6,14},{7,15},{8,0},{9,1},... | collective-permute-start | bytes 417800 | tf_op jit(solution)/shard_map/ppermute | solution.py:55
  41.9 29.9 %collective-permute-start.14 = (bf16[2,272,256]{2,1,0:T(8,128)(2,1)S(1)}, bf16[2,272,256]{2,1,0:T(8,128)(2,1)S(1)}, u32[]{:S(2)}, u32[]{:S(2)}) collective-permute-start(bf16[2,272,256]{2,1,0:T(8,128)(2,1)S(1)} %pad_maximum_fusion.r0), channel_id=1, source_target_pairs={{0,4},{1,5},{2,6},{3,7},{4,0},{5,1},{6,2},{7,3},{8,12},{9,13},{10,... | collective-permute-start | bytes 835592 | tf_op jit(solution)/shard_map/ppermute | solution.py:55
  42.7 29.1 %collective-permute-start.13 = (bf16[2,272,256]{2,1,0:T(8,128)(2,1)S(1)}, bf16[2,272,256]{2,1,0:T(8,128)(2,1)S(1)}, u32[]{:S(2)}, u32[]{:S(2)}) collective-permute-start(bf16[2,272,256]{2,1,0:T(8,128)(2,1)S(1)} %pad_maximum_fusion.r0), channel_id=1, source_target_pairs={{0,6},{1,7},{2,0},{3,1},{4,2},{5,3},{6,4},{7,5},{8,14},{9,15},{10,... | collective-permute-start | bytes 835592 | tf_op jit(solution)/shard_map/ppermute | solution.py:55
  47.2 24.5 %collective-permute-start.12 = (bf16[2,272,256]{2,1,0:T(8,128)(2,1)S(1)}, bf16[2,272,256]{2,1,0:T(8,128)(2,1)S(1)}, u32[]{:S(2)}, u32[]{:S(2)}) collective-permute-start(bf16[2,272,256]{2,1,0:T(8,128)(2,1)S(1)} %pad_maximum_fusion.r0), channel_id=1, source_target_pairs={{0,2},{1,3},{2,4},{3,5},{4,6},{5,7},{6,0},{7,1},{8,10},{9,11},{10,... | collective-permute-start | bytes 835592 | tf_op jit(solution)/shard_map/ppermute | solution.py:55
  47.2 2.2 %copy-start.1 = (bf16[32,1,64,1024]{3,2,1,0:T(8,128)(2,1)S(1)}, bf16[32,1,64,1024]{3,2,1,0:T(8,128)(2,1)}, u32[]{:S(2)}) copy-start(bf16[32,1,64,1024]{3,2,1,0:T(8,128)(2,1)} %param.6) | copy-start | bytes 12582916
  80.0 6.5 %collective-permute-start.15 = (f32[64,64,128]{2,1,0:T(8,128)S(1)}, f32[64,64,128]{2,1,0:T(8,128)S(1)}, u32[]{:S(2)}, u32[]{:S(2)}) collective-permute-start(f32[64,64,128]{2,1,0:T(8,128)S(1)} %get-tuple-element.34), channel_id=1, source_target_pairs={{0,8},{1,9},{2,10},{3,11},{4,12},{5,13},{6,14},{7,15},{8,0},{9,1},... | collective-permute-start | bytes 6291464 | tf_op jit(solution)/shard_map/ppermute | solution.py:55
  85.2 1.3 %copy-start = (f32[64,64,128]{2,1,0:T(8,128)}, f32[64,64,128]{2,1,0:T(8,128)S(1)}, u32[]{:S(2)}) copy-start(f32[64,64,128]{2,1,0:T(8,128)S(1)} %own_half.1.a_ref) | copy-start | bytes 6291460
  86.5 1.3 %copy-start.2 = (f32[64,64,128]{2,1,0:T(8,128)}, f32[64,64,128]{2,1,0:T(8,128)S(1)}, u32[]{:S(2)}) copy-start(f32[64,64,128]{2,1,0:T(8,128)S(1)} %collective-permute-done.15.b_ref) | copy-start | bytes 6291460

commit v4 on v3

--- a/solution.py
+++ b/solution.py
@@ -92,29 +92,30 @@
 
 
 def fine_product(cols_ref, slot_c, a_hbm, *refs):
-    pc_in, (hi, lo, a_ref, pc_ref, dense, sems) = refs[:10], refs[10:]
-    copies, at = [], 0
+    pc_in, (hi, lo, a_ref, dense, sem) = refs[:10], refs[10:]
+    fetch = pltpu.make_async_copy(a_hbm, a_ref, sem)
+    fetch.start()
+
+    def place(ref, piece, at):
+        ids = ref[piece, pl.ds(4 * BS, PAD), :].astype(F32)
+        for b in range(4):
+
+            def store(g, out):
+                dense[4 * slot_c[at] + b, :, 128 * g : 128 * (g + 1)] = out
+
+            spread(ref[piece, pl.ds(BS * b, BS), :], ids[b : b + 1], store)
+
+    at = 0
     for ref in pc_in:
-        here = pc_ref.at[pl.ds(at, ref.shape[0])]
-        copies.append(pltpu.make_async_copy(ref, here, sems.at[len(copies)]))
+        if ref.shape[0] == 1:
+            place(ref, 0, at)
+        else:
+
+            @pl.loop(0, ref.shape[0])
+            def _(piece):
+                place(ref, piece, at + piece)
+
         at += ref.shape[0]
-    fetch = pltpu.make_async_copy(a_hbm, a_ref, sems.at[10])
-    fetch.start()
-    for copy in copies:
-        copy.start()
-    for copy in copies:
-        copy.wait()
-
-    @pl.loop(0, pc_ref.shape[0])
-    def _(piece):
-        ids = pc_ref[piece, pl.ds(4 * BS, PAD), :].astype(F32)
-        for b in range(4):
-
-            def store(g, out):
-                dense[4 * slot_c[piece] + b, :, 128 * g : 128 * (g + 1)] = out
-
-            spread(pc_ref[piece, pl.ds(BS * b, BS), :], ids[b : b + 1], store)
-
     fetch.wait()
 
     @pl.loop(0, a_ref.shape[0])
@@ -182,7 +183,7 @@
 
 VMEM = pl.BlockSpec(memory_space=pltpu.VMEM)
 SMEM = pl.BlockSpec(memory_space=pltpu.SMEM)
-ANY = pl.BlockSpec(memory_space=pl.ANY)
+HBM = pl.BlockSpec(memory_space=pltpu.HBM)
 HALF = jax.ShapeDtypeStruct((64, BS, 128), F32)
 
 
@@ -195,13 +196,12 @@
     return pl.pallas_call(
         fine_product,
         out_shape=(pltpu.VMEM((rows, 1024), BF16),) * 2,
-        in_specs=[SMEM] * 2 + [ANY] * 11,
+        in_specs=[SMEM] * 2 + [HBM] + [VMEM] * 10,
         out_specs=(VMEM, VMEM),
         scratch_shapes=[
             pltpu.VMEM(a.shape, BF16),
-            pltpu.VMEM((16,) + pc[0].shape[1:], BF16),
             pltpu.VMEM((64, BS, 1024), BF16),
-            pltpu.SemaphoreType.DMA((11,)),
+            pltpu.SemaphoreType.DMA,
         ],
         compiler_params=pltpu.CompilerParams(vmem_limit_bytes=28 << 20),
         cost_estimate=cost(2 << 33),
@@ -285,13 +285,19 @@
         out_shape=jax.ShapeDtypeStruct((64, ROWS, 128), jnp.int16),
         in_specs=[VMEM, VMEM],
         out_specs=VMEM,
+        compiler_params=pltpu.CompilerParams(vmem_limit_bytes=8 << 20),
         name="pack",
     )(a, b)
 
 
 def unpacked_sum(mixed):
     return pl.pallas_call(
-        unpack, out_shape=jax.ShapeDtypeStruct((BS, 128), F32), name="unpack"
+        unpack,
+        out_shape=jax.ShapeDtypeStruct((BS, 128), F32),
+        in_specs=[VMEM],
+        out_specs=VMEM,
+        compiler_params=pltpu.CompilerParams(vmem_limit_bytes=4 << 20),
+        name="unpack",
     )(mixed)
 
 
@@ -301,7 +307,8 @@
     piece = jnp.concatenate([p_vals.reshape(4 * BS, 4 * BS), ids, blank])
     pc, pr = gather_pieces(piece[None])
     core, slot_c, slot_r = slots()
-    hi, lo = run_fine_product(a_cols[:, 0], slot_c, a_vals[:, 0], pc)
+    a = pltpu.with_memory_space_constraint(a_vals[:, 0], pltpu.HBM)
+    hi, lo = run_fine_product(a_cols[:, 0], slot_c, a, pc)
     turned, other = run_other_half(core, slot_r, hi, lo, pr)
     met = send(other, OTHER_CORE)
     own = run_own_half(hi, lo, turned)

time: 124 us -> 113 us (0.911)
  Pallas kernels: 43.6 us -> 37.6 us
  local copies, waits for them, and re-layouts: 5.87 us -> 1.05 us
    unnamed x8 -> x2, local copies, waits for them, and re-layouts: 5.59 us -> 0.78 us
    pallas_call x1, Pallas kernels: 5.73 us -> 2.46 us  [packed_sum(): pl.pallas_call(pack, out_shape=jax.ShapeDtypeStruct((64, ROWS, 128), jnp....]
    pallas_call x1, Pallas kernels: 22.3 us -> 20.8 us  [run_fine_product(): pl.pallas_call(fine_product, out_shape=(pltpu.VMEM((rows, 1024), BF16),)...]
    pallas_call x1, Pallas kernels: 2.27 us -> 1 us  [unpacked_sum(): pl.pallas_call(unpack, out_shape=jax.ShapeDtypeStruct((BS, 128), F32), in...]
  transfers between devices with their start and end apart: 16 -> 16, of which waited for: 6 -> 6; matrix products, arithmetic and copies ran while one was open for 1% -> 1% of each run, Pallas kernels for 22% -> 23%
where the time goes in v4:
time: 113 us
  Pallas kernels  37.6 us (33%)
  blocking collectives  27.8 us (25%)
  starting transfers between devices  25.9 us (23%)
  waiting for transfers between devices  17.8 us (16%)
  other arithmetic  2.5 us (2%)
    all_to_all x1, blocking collectives, shards(): mixed = lax.all_to_all(packed, ('x', 'yh', 'z', 'yl'), 0, 0, tiled=True)  27.8 us
    ppermute x16, starting transfers between devices, send(): return lax.ppermute(value, AXES, pairs)  25.9 us
    pallas_call x1, Pallas kernels, run_fine_product(): pl.pallas_call(fine_product, out_shape=(pltpu.VMEM((rows, 1024), BF16),)...  20.8 us
    ppermute x16, waiting for transfers between devices, send(): return lax.ppermute(value, AXES, pairs)  17.8 us
    pallas_call x1, Pallas kernels, run_other_half(): pl.pallas_call(other_half, out_shape=(pltpu.VMEM((2, 512, hi.shape[0]), B...  8.21 us
    pallas_call x1, Pallas kernels, run_own_half(): pl.pallas_call(own_half, out_shape=HALF, in_specs=[VMEM] * 3, out_specs=V...  5.1 us
    pallas_call x1, Pallas kernels, packed_sum(): pl.pallas_call(pack, out_shape=jax.ShapeDtypeStruct((64, ROWS, 128), jnp....  2.46 us
  transfers between devices with their start and end apart: 16, of which 6 were waited for; matrix products, arithmetic and copies ran while one was open for 1% of the time, Pallas kernels for 23%

profile of v4, /device:TPU:0, one launch (start us, length us, event | category | flops | bytes accessed | tf_op | source)
XLA Modules:
  0.0 112.8 jit_solution(14214953661186736894)
XLA Ops:
  0.0 0.7 convert_element_type.3
  0.7 0.1 broadcast_in_dim.9
  0.8 0.1 reshape.10
  0.9 0.1 pad.4.clone
  0.9 1.0 maximum_bitcast_fusion
  1.9 1.8 %collective-permute-start.2 = (bf16[1,272,256]{2,1,0:T(8,128)(2,1)S(1)}, bf16[1,272,256]{2,1,0:T(8,128)(2,1)S(1)}, u32[]{:S(2)}, u32[]{:S(2)}) collective-permute-start(bf16[1,272,256]{2,1,0:T(8,128)(2,1)S(1)} %maximum_bitcast_fusion), channel_id=1, source_target_pairs={{0,1},{1,0},{2,3},{3,2},{4,5},{5,4},{6,7},{7,6},{8,9},{9,8},{10,11... | collective-permute-start | bytes 417800 | tf_op jit(solution)/shard_map/ppermute | solution.py:55
  3.7 2.9 %collective-permute-start.1 = (bf16[1,272,256]{2,1,0:T(8,128)(2,1)S(1)}, bf16[1,272,256]{2,1,0:T(8,128)(2,1)S(1)}, u32[]{:S(2)}, u32[]{:S(2)}) collective-permute-start(bf16[1,272,256]{2,1,0:T(8,128)(2,1)S(1)} %maximum_bitcast_fusion), channel_id=1, source_target_pairs={{0,16},{1,0},{2,112},{3,96},{4,80},{5,64},{6,48},{7,32},{8,24},{9,... | collective-permute-start | bytes 417800 | tf_op jit(solution)/shard_map/ppermute | solution.py:55
  6.6 0.7 collective-permute-start
  7.3 1.3 %collective-permute-done.2 = bf16[1,272,256]{2,1,0:T(8,128)(2,1)S(1)} collective-permute-done((bf16[1,272,256]{2,1,0:T(8,128)(2,1)S(1)}, bf16[1,272,256]{2,1,0:T(8,128)(2,1)S(1)}, u32[]{:S(2)}, u32[]{:S(2)}) %collective-permute-start.2) | collective-permute-done | bytes 139296 | tf_op jit(solution)/shard_map/ppermute | solution.py:55
  8.6 1.8 %collective-permute-done.1 = bf16[1,272,256]{2,1,0:T(8,128)(2,1)S(1)} collective-permute-done((bf16[1,272,256]{2,1,0:T(8,128)(2,1)S(1)}, bf16[1,272,256]{2,1,0:T(8,128)(2,1)S(1)}, u32[]{:S(2)}, u32[]{:S(2)}) %collective-permute-start.1) | collective-permute-done | bytes 139296 | tf_op jit(solution)/shard_map/ppermute | solution.py:55
  10.4 0.0 collective-permute-done
  10.4 0.1 collective-permute-start.5
  10.5 11.9 %collective-permute-start.4 = (bf16[2,272,256]{2,1,0:T(8,128)(2,1)S(1)}, bf16[2,272,256]{2,1,0:T(8,128)(2,1)S(1)}, u32[]{:S(2)}, u32[]{:S(2)}) collective-permute-start(bf16[2,272,256]{2,1,0:T(8,128)(2,1)S(1)} %constant_dynamic-update-slice_fusion.refs_0_), channel_id=1, source_target_pairs={{0,96},{1,97},{2,98},{3,99},{4,100},{5,101},{6,102},{7,103},{8,104... | collective-permute-start | bytes 835592 | tf_op jit(solution)/shard_map/ppermute | solution.py:55
  22.4 0.0 collective-permute-start.3
  22.4 0.0 collective-permute-done.5.refs_5_
  22.4 6.5 %collective-permute-done.4.refs_2_ = bf16[2,272,256]{2,1,0:T(8,128)(2,1)S(1)} collective-permute-done((bf16[2,272,256]{2,1,0:T(8,128)(2,1)S(1)}, bf16[2,272,256]{2,1,0:T(8,128)(2,1)S(1)}, u32[]{:S(2)}, u32[]{:S(2)}) %collective-permute-start.4) | collective-permute-done | bytes 278560 | tf_op jit(solution)/shard_map/ppermute | solution.py:55
  28.9 3.4 %collective-permute-done.3.refs_1_ = bf16[2,272,256]{2,1,0:T(8,128)(2,1)S(1)} collective-permute-done((bf16[2,272,256]{2,1,0:T(8,128)(2,1)S(1)}, bf16[2,272,256]{2,1,0:T(8,128)(2,1)S(1)}, u32[]{:S(2)}, u32[]{:S(2)}) %collective-permute-start.3) | collective-permute-done | bytes 278560 | tf_op jit(solution)/shard_map/ppermute | solution.py:55
  32.3 0.1 collective-permute-start.8
  32.4 0.6 collective-permute-start.9
  33.0 0.9 collective-permute-start.7
  33.9 1.1 collective-permute-start.6
  35.0 0.7 broadcast_add_fusion.1
  35.7 2.9 %collective-permute-done.7.refs_4_ = bf16[1,272,256]{2,1,0:T(8,128)(2,1)S(1)} collective-permute-done((bf16[1,272,256]{2,1,0:T(8,128)(2,1)S(1)}, bf16[1,272,256]{2,1,0:T(8,128)(2,1)S(1)}, u32[]{:S(2)}, u32[]{:S(2)}) %collective-permute-start.7) | collective-permute-done | bytes 139296 | tf_op jit(solution)/shard_map/ppermute | solution.py:55
  38.6 1.9 %collective-permute-done.6.refs_3_ = bf16[1,272,256]{2,1,0:T(8,128)(2,1)S(1)} collective-permute-done((bf16[1,272,256]{2,1,0:T(8,128)(2,1)S(1)}, bf16[1,272,256]{2,1,0:T(8,128)(2,1)S(1)}, u32[]{:S(2)}, u32[]{:S(2)}) %collective-permute-start.6) | collective-permute-done | bytes 139296 | tf_op jit(solution)/shard_map/ppermute | solution.py:55
  40.5 0.0 collective-permute-done.8.refs_6_
  40.5 0.0 collective-permute-done.9.refs_7_
  40.5 0.0 collective-permute-start.10
  40.5 0.5 collective-permute-start.11
  41.0 0.8 copy.7
  41.8 0.1 pad_add_fusion.slot_c
  41.9 0.8 collective-permute-start.14
  42.7 4.5 %collective-permute-start.13 = (bf16[2,272,256]{2,1,0:T(8,128)(2,1)S(1)}, bf16[2,272,256]{2,1,0:T(8,128)(2,1)S(1)}, u32[]{:S(2)}, u32[]{:S(2)}) collective-permute-start(bf16[2,272,256]{2,1,0:T(8,128)(2,1)S(1)} %pad_maximum_fusion.r0), channel_id=1, source_target_pairs={{0,6},{1,7},{2,0},{3,1},{4,2},{5,3},{6,4},{7,5},{8,14},{9,15},{10,... | collective-permute-start | bytes 835592 | tf_op jit(solution)/shard_map/ppermute | solution.py:55
  47.2 0.0 collective-permute-start.12
  47.2 0.0 collective-permute-done.10.refs_8_
  47.2 0.0 collective-permute-done.11.refs_9_
  47.2 20.8 %fine_product.1 = (bf16[2048,1024]{1,0:T(8,128)(2,1)S(1)}, bf16[2048,1024]{1,0:T(8,128)(2,1)S(1)}) custom-call(s32[32,16]{1,0:T(8,128)S(1)} %bitcast.6, s32[16]{0:T(128)S(1)} %pad_add_fusion.slot_c, bf16[32,64,1024]{2,1,0:T(8,128)(2,1)} %bitcast.8, bf16[2,272,256]{2,1,0:T(8,128)(2,1)S(1)} %constant_dynamic-update-slice_fusion.refs_0_, ...), custom_call_target="tpu_custom_call" | custom-call | flops 17179869184 | bytes 8388608 | tf_op jit(solution)/shard_map/fine_product/pallas_call | solution.py:196
  68.0 0.0 collective-permute-done.14.r3
  68.1 0.0 collective-permute-done.13.r2
  68.1 0.0 collective-permute-done.12.r1
  68.1 8.2 %other_half.1 = (bf16[2,512,2048]{2,1,0:T(8,128)(2,1)S(1)}, f32[64,64,128]{2,1,0:T(8,128)S(1)}) custom-call(s32[1]{0:T(128)} %bitcast.4.core_ref, s32[8]{0:T(128)S(1)} %get-tuple-element.37.slot_r, bf16[2048,1024]{1,0:T(8,128)(2,1)S(1)} %get-tuple-element.30.hi, bf16[2048,1024]{1,0:T(8,128)(2,1)S(1)} %get-tuple-element.31.lo, ...), custom_call_target="tpu_custom_call" | custom-call | flops 8589934592 | bytes 8388608 | tf_op jit(solution)/shard_map/other_half/pallas_call | solution.py:213
  76.3 0.1 collective-permute-start.15
  76.4 5.1 %own_half.1.a_ref = f32[64,64,128]{2,1,0:T(8,128)S(1)} custom-call(bf16[2048,1024]{1,0:T(8,128)(2,1)S(1)} %get-tuple-element.30.hi, bf16[2048,1024]{1,0:T(8,128)(2,1)S(1)} %get-tuple-element.31.lo, bf16[2,512,2048]{2,1,0:T(8,128)(2,1)S(1)} %get-tuple-element.33.turned), custom_call_target="tpu_custom_call" | custom-call | flops 8589934592 | bytes 8388608 | tf_op jit(solution)/shard_map/own_half/pallas_call | solution.py:225
  81.5 0.0 collective-permute-done.15.b_ref
  81.5 2.5 %pack.1 = s16[64,72,128]{2,1,0:T(8,128)(2,1)S(1)} custom-call(f32[64,64,128]{2,1,0:T(8,128)S(1)} %own_half.1.a_ref, f32[64,64,128]{2,1,0:T(8,128)S(1)} %collective-permute-done.15.b_ref), custom_call_target="tpu_custom_call" | custom-call | tf_op jit(solution)/shard_map/pack/pallas_call | solution.py:283
  84.0 27.8 %all_to_all.5.in_ref = s16[64,72,128]{2,1,0:T(8,128)(2,1)S(1)} all-to-all(s16[64,72,128]{2,1,0:T(8,128)(2,1)S(1)} %pack.1), channel_id=1, replica_groups=mesh['x'=4,'yh'=2,'core'=2,'z'=4,'yl'=2] {'x','yh','z','yl'}, dimensions={0} | all-to-all | bytes 2359296 | tf_op jit(solution)/shard_map/all_to_all | solution.py:316
  111.8 1.0 unpack.1
  (7 shorter events, 0.1 us)
Async XLA Ops:
  1.9 6.6 %collective-permute-start.2 = (bf16[1,272,256]{2,1,0:T(8,128)(2,1)S(1)}, bf16[1,272,256]{2,1,0:T(8,128)(2,1)S(1)}, u32[]{:S(2)}, u32[]{:S(2)}) collective-permute-start(bf16[1,272,256]{2,1,0:T(8,128)(2,1)S(1)} %maximum_bitcast_fusion), channel_id=1, source_target_pairs={{0,1},{1,0},{2,3},{3,2},{4,5},{5,4},{6,7},{7,6},{8,9},{9,8},{10,11... | collective-permute-start | bytes 417800 | tf_op jit(solution)/shard_map/ppermute | solution.py:55
  3.7 6.7 %collective-permute-start.1 = (bf16[1,272,256]{2,1,0:T(8,128)(2,1)S(1)}, bf16[1,272,256]{2,1,0:T(8,128)(2,1)S(1)}, u32[]{:S(2)}, u32[]{:S(2)}) collective-permute-start(bf16[1,272,256]{2,1,0:T(8,128)(2,1)S(1)} %maximum_bitcast_fusion), channel_id=1, source_target_pairs={{0,16},{1,0},{2,112},{3,96},{4,80},{5,64},{6,48},{7,32},{8,24},{9,... | collective-permute-start | bytes 417800 | tf_op jit(solution)/shard_map/ppermute | solution.py:55
  6.6 3.8 %collective-permute-start = (bf16[1,272,256]{2,1,0:T(8,128)(2,1)S(1)}, bf16[1,272,256]{2,1,0:T(8,128)(2,1)S(1)}, u32[]{:S(2)}, u32[]{:S(2)}) collective-permute-start(bf16[1,272,256]{2,1,0:T(8,128)(2,1)S(1)} %maximum_bitcast_fusion), channel_id=1, source_target_pairs={{0,0},{1,16},{2,96},{3,112},{4,64},{5,80},{6,32},{7,48},{8,8},{9,2... | collective-permute-start | bytes 417800 | tf_op jit(solution)/shard_map/ppermute | solution.py:55
  10.4 12.0 %collective-permute-start.5 = (bf16[2,272,256]{2,1,0:T(8,128)(2,1)S(1)}, bf16[2,272,256]{2,1,0:T(8,128)(2,1)S(1)}, u32[]{:S(2)}, u32[]{:S(2)}) collective-permute-start(bf16[2,272,256]{2,1,0:T(8,128)(2,1)S(1)} %constant_dynamic-update-slice_fusion.refs_0_), channel_id=1, source_target_pairs={{0,8},{1,9},{2,10},{3,11},{4,12},{5,13},{6,14},{7,15},{8,0},{9,1},... | collective-permute-start | bytes 835592 | tf_op jit(solution)/shard_map/ppermute | solution.py:55
  10.5 18.4 %collective-permute-start.4 = (bf16[2,272,256]{2,1,0:T(8,128)(2,1)S(1)}, bf16[2,272,256]{2,1,0:T(8,128)(2,1)S(1)}, u32[]{:S(2)}, u32[]{:S(2)}) collective-permute-start(bf16[2,272,256]{2,1,0:T(8,128)(2,1)S(1)} %constant_dynamic-update-slice_fusion.refs_0_), channel_id=1, source_target_pairs={{0,96},{1,97},{2,98},{3,99},{4,100},{5,101},{6,102},{7,103},{8,104... | collective-permute-start | bytes 835592 | tf_op jit(solution)/shard_map/ppermute | solution.py:55
  22.4 9.9 %collective-permute-start.3 = (bf16[2,272,256]{2,1,0:T(8,128)(2,1)S(1)}, bf16[2,272,256]{2,1,0:T(8,128)(2,1)S(1)}, u32[]{:S(2)}, u32[]{:S(2)}) collective-permute-start(bf16[2,272,256]{2,1,0:T(8,128)(2,1)S(1)} %constant_dynamic-update-slice_fusion.refs_0_), channel_id=1, source_target_pairs={{0,32},{1,33},{2,34},{3,35},{4,36},{5,37},{6,38},{7,39},{8,40},{9,... | collective-permute-start | bytes 835592 | tf_op jit(solution)/shard_map/ppermute | solution.py:55
  32.3 8.2 %collective-permute-start.8 = (bf16[2,272,256]{2,1,0:T(8,128)(2,1)S(1)}, bf16[2,272,256]{2,1,0:T(8,128)(2,1)S(1)}, u32[]{:S(2)}, u32[]{:S(2)}) collective-permute-start(bf16[2,272,256]{2,1,0:T(8,128)(2,1)S(1)} %collective-permute-done.3.refs_1_), channel_id=1, source_target_pairs={{0,8},{1,9},{2,10},{3,11},{4,12},{5,13},{6,14},{7,15},{8,0},{9,1},... | collective-permute-start | bytes 835592 | tf_op jit(solution)/shard_map/ppermute | solution.py:55
  32.4 8.1 %collective-permute-start.9 = (bf16[2,272,256]{2,1,0:T(8,128)(2,1)S(1)}, bf16[2,272,256]{2,1,0:T(8,128)(2,1)S(1)}, u32[]{:S(2)}, u32[]{:S(2)}) collective-permute-start(bf16[2,272,256]{2,1,0:T(8,128)(2,1)S(1)} %collective-permute-done.4.refs_2_), channel_id=1, source_target_pairs={{0,8},{1,9},{2,10},{3,11},{4,12},{5,13},{6,14},{7,15},{8,0},{9,1},... | collective-permute-start | bytes 835592 | tf_op jit(solution)/shard_map/ppermute | solution.py:55
  33.0 5.7 %collective-permute-start.7 = (bf16[1,272,256]{2,1,0:T(8,128)(2,1)S(1)}, bf16[1,272,256]{2,1,0:T(8,128)(2,1)S(1)}, u32[]{:S(2)}, u32[]{:S(2)}) collective-permute-start(bf16[1,272,256]{2,1,0:T(8,128)(2,1)S(1)} %slice.7), channel_id=1, source_target_pairs={{0,96},{1,97},{2,98},{3,99},{4,100},{5,101},{6,102},{7,103},{8,104... | collective-permute-start | bytes 417800 | tf_op jit(solution)/shard_map/ppermute | solution.py:55
  33.9 6.6 %collective-permute-start.6 = (bf16[1,272,256]{2,1,0:T(8,128)(2,1)S(1)}, bf16[1,272,256]{2,1,0:T(8,128)(2,1)S(1)}, u32[]{:S(2)}, u32[]{:S(2)}) collective-permute-start(bf16[1,272,256]{2,1,0:T(8,128)(2,1)S(1)} %slice.6), channel_id=1, source_target_pairs={{0,32},{1,33},{2,34},{3,35},{4,36},{5,37},{6,38},{7,39},{8,40},{9,... | collective-permute-start | bytes 417800 | tf_op jit(solution)/shard_map/ppermute | solution.py:55
  40.5 6.7 %collective-permute-start.10 = (bf16[1,272,256]{2,1,0:T(8,128)(2,1)S(1)}, bf16[1,272,256]{2,1,0:T(8,128)(2,1)S(1)}, u32[]{:S(2)}, u32[]{:S(2)}) collective-permute-start(bf16[1,272,256]{2,1,0:T(8,128)(2,1)S(1)} %collective-permute-done.6.refs_3_), channel_id=1, source_target_pairs={{0,8},{1,9},{2,10},{3,11},{4,12},{5,13},{6,14},{7,15},{8,0},{9,1},... | collective-permute-start | bytes 417800 | tf_op jit(solution)/shard_map/ppermute | solution.py:55
  40.5 6.7 %collective-permute-start.11 = (bf16[1,272,256]{2,1,0:T(8,128)(2,1)S(1)}, bf16[1,272,256]{2,1,0:T(8,128)(2,1)S(1)}, u32[]{:S(2)}, u32[]{:S(2)}) collective-permute-start(bf16[1,272,256]{2,1,0:T(8,128)(2,1)S(1)} %collective-permute-done.7.refs_4_), channel_id=1, source_target_pairs={{0,8},{1,9},{2,10},{3,11},{4,12},{5,13},{6,14},{7,15},{8,0},{9,1},... | collective-permute-start | bytes 417800 | tf_op jit(solution)/shard_map/ppermute | solution.py:55
  41.9 26.2 %collective-permute-start.14 = (bf16[2,272,256]{2,1,0:T(8,128)(2,1)S(1)}, bf16[2,272,256]{2,1,0:T(8,128)(2,1)S(1)}, u32[]{:S(2)}, u32[]{:S(2)}) collective-permute-start(bf16[2,272,256]{2,1,0:T(8,128)(2,1)S(1)} %pad_maximum_fusion.r0), channel_id=1, source_target_pairs={{0,4},{1,5},{2,6},{3,7},{4,0},{5,1},{6,2},{7,3},{8,12},{9,13},{10,... | collective-permute-start | bytes 835592 | tf_op jit(solution)/shard_map/ppermute | solution.py:55
  42.7 25.4 %collective-permute-start.13 = (bf16[2,272,256]{2,1,0:T(8,128)(2,1)S(1)}, bf16[2,272,256]{2,1,0:T(8,128)(2,1)S(1)}, u32[]{:S(2)}, u32[]{:S(2)}) collective-permute-start(bf16[2,272,256]{2,1,0:T(8,128)(2,1)S(1)} %pad_maximum_fusion.r0), channel_id=1, source_target_pairs={{0,6},{1,7},{2,0},{3,1},{4,2},{5,3},{6,4},{7,5},{8,14},{9,15},{10,... | collective-permute-start | bytes 835592 | tf_op jit(solution)/shard_map/ppermute | solution.py:55
  47.2 20.8 %collective-permute-start.12 = (bf16[2,272,256]{2,1,0:T(8,128)(2,1)S(1)}, bf16[2,272,256]{2,1,0:T(8,128)(2,1)S(1)}, u32[]{:S(2)}, u32[]{:S(2)}) collective-permute-start(bf16[2,272,256]{2,1,0:T(8,128)(2,1)S(1)} %pad_maximum_fusion.r0), channel_id=1, source_target_pairs={{0,2},{1,3},{2,4},{3,5},{4,6},{5,7},{6,0},{7,1},{8,10},{9,11},{10,... | collective-permute-start | bytes 835592 | tf_op jit(solution)/shard_map/ppermute | solution.py:55
  76.3 5.2 %collective-permute-start.15 = (f32[64,64,128]{2,1,0:T(8,128)S(1)}, f32[64,64,128]{2,1,0:T(8,128)S(1)}, u32[]{:S(2)}, u32[]{:S(2)}) collective-permute-start(f32[64,64,128]{2,1,0:T(8,128)S(1)} %get-tuple-element.34), channel_id=1, source_target_pairs={{0,8},{1,9},{2,10},{3,11},{4,12},{5,13},{6,14},{7,15},{8,0},{9,1},... | collective-permute-start | bytes 6291464 | tf_op jit(solution)/shard_map/ppermute | solution.py:55

commit v5 on v4

--- a/solution.py
+++ b/solution.py
@@ -1,3 +1,5 @@
+import functools
+
 import jax
 import jax.numpy as jnp
 from jax import lax
@@ -12,7 +14,7 @@
 F32 = jnp.float32
 BS = 64
 ROWS = 72
-PAD = 16
+HALF_ROWS = 136
 
 
 def linear(place):
@@ -40,8 +42,8 @@
     return (y % 2) * 2 + y // 2
 
 
-REFLECT = route(lambda x, y, c, z: (2 * x - z, swap_y(y), c, x))
-REFLECT_FAR = route(lambda x, y, c, z: (2 * x - z, swap_y(y) + 2, c, x))
+REFLECT = route(lambda x, y, c, z: (2 * x - z + 2, swap_y(y), c, x))
+ACROSS_Y = route(lambda x, y, c, z: (x, y + 2, c, z))
 OTHER_CORE = route(lambda x, y, c, z: (x, y, 1 - c, z))
 NEXT_X = route(lambda x, y, c, z: (x + 1, y, c, z))
 LAST_X = route(lambda x, y, c, z: (x - 1, y, c, z))
@@ -91,31 +93,54 @@
         store(g, choose(where, jnp.asarray(2.0 * g, BF16), values))
 
 
-def fine_product(cols_ref, slot_c, a_hbm, *refs):
-    pc_in, (hi, lo, a_ref, dense, sem) = refs[:10], refs[10:]
+def position(name):
+    return lax.axis_index(name).astype(jnp.int32)
+
+
+def flip(bit, number):
+    return bit if number == 0 else 1 - bit
+
+
+NEAR = ((0, 0, 0, 2),)
+BEHIND, AHEAD, ACROSS = ((-1, 0, 0, 2),), ((1, 0, 0, 2),), ((0, 1, 0, 2),)
+BEHIND2, AHEAD2 = ((-1, 1, 0, 2), (2, 0, 0, 1)), ((1, 1, 0, 2), (2, 0, 1, 1))
+BEHIND3, AHEAD3 = ((2, 1, 0, 1),), ((2, 1, 1, 1),)
+
+
+def place(ref, halves, other, dense):
+    x, yh, core, z = (position(name) for name in ("x", "yh", "core", "z"))
+    owner = 1 - core if other else core
+    base = 0
+    for step, side, first, count in halves:
+        piece = 2 * jnp.bitwise_and(2 * z + 10 - x - step, 3) + flip(yh, side)
+        at = 32 * owner + 4 * piece + 2 * first
+
+        def one(h, base=base, at=at):
+            ids = ref[base + h, pl.ds(2 * BS, 8), :].astype(F32)
+            for b in range(2):
+
+                def store(g, out):
+                    dense[at + 2 * h + b, :, 128 * g : 128 * (g + 1)] = out
+
+                spread(ref[base + h, pl.ds(BS * b, BS), :], ids[b : b + 1], store)
+
+        if count == 1:
+            one(0)
+        else:
+            pl.loop(0, count)(one)
+        base += count
+
+
+def place_all(what, *refs):
+    for (halves, other), ref in zip(what, refs):
+        place(ref, halves, other, refs[-1])
+
+
+def fine_product(what, cols_ref, a_hbm, *refs):
+    arrays, (dense_in, hi, lo, dense, a_ref, sem) = refs[: len(what)], refs[len(what) :]
     fetch = pltpu.make_async_copy(a_hbm, a_ref, sem)
     fetch.start()
-
-    def place(ref, piece, at):
-        ids = ref[piece, pl.ds(4 * BS, PAD), :].astype(F32)
-        for b in range(4):
-
-            def store(g, out):
-                dense[4 * slot_c[at] + b, :, 128 * g : 128 * (g + 1)] = out
-
-            spread(ref[piece, pl.ds(BS * b, BS), :], ids[b : b + 1], store)
-
-    at = 0
-    for ref in pc_in:
-        if ref.shape[0] == 1:
-            place(ref, 0, at)
-        else:
-
-            @pl.loop(0, ref.shape[0])
-            def _(piece):
-                place(ref, piece, at + piece)
-
-        at += ref.shape[0]
+    place_all(what, *arrays, dense)
     fetch.wait()
 
     @pl.loop(0, a_ref.shape[0])
@@ -124,7 +149,7 @@
             total = None
             for k in range(4):
                 tiles = [
-                    dense[cols_ref[i, 4 * k + j], :, 256 * n : 256 * (n + 1)] for j in range(4)
+                    dense[cols_ref[4 * k + j, i], :, 256 * n : 256 * (n + 1)] for j in range(4)
                 ]
                 weights = jnp.concatenate(tiles, axis=0)
                 left = a_ref[i, :, 256 * k : 256 * (k + 1)]
@@ -136,21 +161,19 @@
             lo[rows, 256 * n : 256 * (n + 1)] = (total - top.astype(F32)).astype(BF16)
 
 
-def turn(pr_ref, piece, turned, core, at):
-    ids4 = pr_ref[piece, pl.ds(4 * BS, PAD), :].astype(F32)
-    for pair in range(2):
-        flipped = pr_ref[piece, pl.ds(128 * pair, 128), :].astype(F32).T.astype(BF16)
-        where, values = [], []
-        for m in range(4):
-            a = ids4[2 * pair : 2 * pair + 1, BS * m : BS * (m + 1)]
-            b = ids4[2 * pair + 1 : 2 * pair + 2, BS * m : BS * (m + 1)]
-            where.append(rows16(jnp.concatenate([a, b], axis=1)))
-            values.append(flipped[BS * m : BS * (m + 1)])
-        for n in range(16):
-            out = choose(where, jnp.asarray(float(n), BF16), values)
-            slot = core if n % 2 == 0 else 1 - core
-            to = pl.ds(pl.multiple_of(at + 128 * pair, 128), 128)
-            turned[slot, pl.ds(BS * (n // 2), BS), to] = out
+def turn(ref, h, turned, core, at):
+    ids = ref[h, pl.ds(2 * BS, 8), :].astype(F32)
+    flipped = ref[h, pl.ds(0, 128), :].astype(F32).T.astype(BF16)
+    where, values = [], []
+    for m in range(4):
+        a = ids[0:1, BS * m : BS * (m + 1)]
+        b = ids[1:2, BS * m : BS * (m + 1)]
+        where.append(rows16(jnp.concatenate([a, b], axis=1)))
+        values.append(flipped[BS * m : BS * (m + 1)])
+    for n in range(16):
+        out = choose(where, jnp.asarray(float(n), BF16), values)
+        slot = core if n % 2 == 0 else 1 - core
+        turned[slot, pl.ds(BS * (n // 2), BS), pl.ds(pl.multiple_of(at, 128), 128)] = out
 
 
 def half_product(turned, slot, hi, lo, out_ref):
@@ -165,15 +188,16 @@
                 out_ref[8 * q + 2 * n + j] = c[BS * q : BS * (q + 1), 128 * j : 128 * (j + 1)]
 
 
-def other_half(core_ref, slot_r, hi, lo, r0, r1, r2, r3, turned, out_ref):
-    at = 0
-    for ref in (r0, r1, r2, r3):
-
-        @pl.loop(0, 2)
-        def _(side):
-            turn(ref, side, turned, core_ref[0], 256 * slot_r[at + side])
-
-        at += 2
+def other_half(hi, lo, r0, r1, r2, r3, turned, out_ref):
+    core, z, yl = (position(name) for name in ("core", "z", "yl"))
+    for ref, step in ((r0, 0), (r1, -1), (r2, 1), (r3, 2)):
+        for side in range(2):
+            at = 256 * (2 * jnp.bitwise_and(z + step + 4, 3) + flip(yl, side))
+
+            @pl.loop(0, 2)
+            def _(h):
+                turn(ref, 2 * side + h, turned, core, at + 128 * h)
+
     half_product(turned, 1, hi, lo, out_ref)
 
 
@@ -191,34 +215,49 @@
     return pl.CostEstimate(flops=flops, bytes_accessed=1 << 23, transcendentals=0)
 
 
-def run_fine_product(cols, slot_c, a, pc):
+DENSE = pltpu.VMEM((64, BS, 1024), BF16)
+
+
+def run_place(what, arrays, dense):
+    given = () if dense is None else (dense,)
+    body = lambda *refs: place_all(what, *refs[: len(what)], refs[-1])
+    return pl.pallas_call(
+        body,
+        out_shape=DENSE,
+        in_specs=[VMEM] * (len(arrays) + len(given)),
+        out_specs=VMEM,
+        input_output_aliases={len(arrays): 0} if given else {},
+        compiler_params=pltpu.CompilerParams(vmem_limit_bytes=16 << 20),
+        cost_estimate=cost(1 << 30),
+        name="place",
+    )(*arrays, *given)
+
+
+def run_fine_product(what, cols, a, arrays, dense):
     rows = a.shape[0] * BS
     return pl.pallas_call(
-        fine_product,
-        out_shape=(pltpu.VMEM((rows, 1024), BF16),) * 2,
-        in_specs=[SMEM] * 2 + [HBM] + [VMEM] * 10,
-        out_specs=(VMEM, VMEM),
-        scratch_shapes=[
-            pltpu.VMEM(a.shape, BF16),
-            pltpu.VMEM((64, BS, 1024), BF16),
-            pltpu.SemaphoreType.DMA,
-        ],
-        compiler_params=pltpu.CompilerParams(vmem_limit_bytes=28 << 20),
+        functools.partial(fine_product, what),
+        out_shape=(pltpu.VMEM((rows, 1024), BF16),) * 2 + (DENSE,),
+        in_specs=[SMEM, HBM] + [VMEM] * (len(arrays) + 1),
+        out_specs=(VMEM,) * 3,
+        scratch_shapes=[pltpu.VMEM(a.shape, BF16), pltpu.SemaphoreType.DMA],
+        input_output_aliases={2 + len(arrays): 2},
+        compiler_params=pltpu.CompilerParams(vmem_limit_bytes=24 << 20),
         cost_estimate=cost(2 << 33),
         name="fine_product",
-    )(cols, slot_c, a, *pc)
-
-
-def run_other_half(core, slot_r, hi, lo, pr):
+    )(cols, a, *arrays, dense)
+
+
+def run_other_half(hi, lo, pr):
     return pl.pallas_call(
         other_half,
         out_shape=(pltpu.VMEM((2, 512, hi.shape[0]), BF16), HALF),
-        in_specs=[SMEM] * 2 + [VMEM] * 6,
+        in_specs=[VMEM] * 6,
         out_specs=(VMEM, VMEM),
         compiler_params=pltpu.CompilerParams(vmem_limit_bytes=28 << 20),
         cost_estimate=cost(1 << 33),
         name="other_half",
-    )(core, slot_r, hi, lo, *pr)
+    )(hi, lo, *pr)
 
 
 def run_own_half(hi, lo, turned):
@@ -233,29 +272,66 @@
     )(hi, lo, turned)
 
 
-def gather_pieces(piece):
-    near, far, beside = together(
-        send(piece, REFLECT), send(piece, REFLECT_FAR), send(piece, BESIDE)
+def stamp(cols_ref, vals_ref, out_ref):
+    block = lax.broadcasted_iota(jnp.int32, (1, 4 * BS), 1) // BS
+    for h in range(2):
+        out_ref[h, :BS, :] = vals_ref[2 * h]
+        out_ref[h, BS : 2 * BS, :] = vals_ref[2 * h + 1]
+        rows = []
+        for b in range(2):
+            row = jnp.zeros((1, 4 * BS), jnp.int32)
+            for m in range(4):
+                row = jnp.where(block == m, cols_ref[2 * h + b, m], row)
+            rows.append(row)
+        rows.append(jnp.zeros((6, 4 * BS), jnp.int32))
+        out_ref[h, 2 * BS :, :] = jnp.concatenate(rows).astype(F32).astype(BF16)
+
+
+def run_stamp(cols, vals):
+    return pl.pallas_call(
+        stamp,
+        out_shape=jax.ShapeDtypeStruct((2, HALF_ROWS, 4 * BS), BF16),
+        in_specs=[SMEM, VMEM],
+        out_specs=VMEM,
+        compiler_params=pltpu.CompilerParams(vmem_limit_bytes=2 << 20),
+        name="stamp",
+    )(cols, vals)
+
+
+def fetch_and_multiply(piece, cols, a):
+    near, beside = together(send(piece, REFLECT), send(piece, BESIDE))
+    b1, a1, f, e0, r0, dense = together(
+        send(near, NEXT_X),
+        send(near, LAST_X),
+        send(near, ACROSS_Y),
+        send(near, OTHER_CORE),
+        jnp.concatenate([piece, beside]),
+        run_place(((NEAR, False),), (near,), None),
     )
-    c0 = jnp.concatenate([near, far])
-    r0 = jnp.concatenate([piece, beside])
-    c1, c2, d0 = together(send(c0, NEXT_X), send(c0, LAST_X), send(c0, OTHER_CORE))
-    c3, c4, d1, d2, r0 = together(
-        send(c1[:1], NEXT_X), send(c2[1:], LAST_X), send(c1, OTHER_CORE), send(c2, OTHER_CORE), r0
+    what = ((BEHIND, False), (AHEAD, False), (ACROSS, False), (NEAR, True))
+    b2, a2, e1, e2, e3, dense = together(
+        send(jnp.concatenate([f, b1[:1]]), NEXT_X),
+        send(jnp.concatenate([f, a1[1:]]), LAST_X),
+        send(b1, OTHER_CORE),
+        send(a1, OTHER_CORE),
+        send(f, OTHER_CORE),
+        run_place(what, (b1, a1, f, e0), dense),
     )
-    d3, d4 = send(c3, OTHER_CORE), send(c4, OTHER_CORE)
+    what = ((BEHIND2, False), (AHEAD2, False), (BEHIND, True), (AHEAD, True), (ACROSS, True))
+    b3, a3, e4, e5, dense = together(
+        send(b2[:1], NEXT_X),
+        send(a2[1:2], LAST_X),
+        send(b2, OTHER_CORE),
+        send(a2, OTHER_CORE),
+        run_place(what, (b2, a2, e1, e2, e3), dense),
+    )
+    what = ((BEHIND3, False), (AHEAD3, False), (BEHIND2, True), (AHEAD2, True))
+    e6, e7 = send(b3, OTHER_CORE), send(a3, OTHER_CORE)
     r1, r2, r3 = send(r0, NEXT_Z), send(r0, LAST_Z), send(r0, ACROSS_Z)
-    return (c0, c1, c2, c3, c4, d0, d1, d2, d3, d4), (r0, r1, r2, r3)
-
-
-def slots():
-    x, yh, core, z, yl = (lax.axis_index(name).astype(jnp.int32) for name in AXES)
-    step = jnp.array([0, 0, -1, -1, 1, 1, 2, 2], jnp.int32)
-    side = jnp.array([0, 1, 0, 1, 0, 1, 0, 1], jnp.int32)
-    mine = 2 * ((2 * z - x - step) % 4) + (yh ^ side)
-    slot_c = jnp.concatenate([mine + 8 * core, mine + 8 * (1 - core)])
-    slot_r = 2 * ((z + step) % 4) + (yl ^ side)
-    return core.reshape(1), slot_c, slot_r
+    dense = run_place(what, (b3, a3, e4, e5), dense)
+    what = ((BEHIND3, True), (AHEAD3, True))
+    hi, lo, dense = run_fine_product(what, cols, a, (e6, e7), dense)
+    return hi, lo, (r0, r1, r2, r3)
 
 
 def pack(a_ref, b_ref, out_ref):
@@ -302,14 +378,10 @@
 
 
 def shards(a_vals, a_cols, p_vals, p_cols):
-    ids = jnp.repeat(p_cols.astype(BF16), BS, axis=1)
-    blank = jnp.zeros((PAD - 4, 4 * BS), BF16)
-    piece = jnp.concatenate([p_vals.reshape(4 * BS, 4 * BS), ids, blank])
-    pc, pr = gather_pieces(piece[None])
-    core, slot_c, slot_r = slots()
     a = pltpu.with_memory_space_constraint(a_vals[:, 0], pltpu.HBM)
-    hi, lo = run_fine_product(a_cols[:, 0], slot_c, a, pc)
-    turned, other = run_other_half(core, slot_r, hi, lo, pr)
+    piece = run_stamp(p_cols, p_vals)
+    hi, lo, pr = fetch_and_multiply(piece, a_cols[:, 0].T, a)
+    turned, other = run_other_half(hi, lo, pr)
     met = send(other, OTHER_CORE)
     own = run_own_half(hi, lo, turned)
     packed = packed_sum(own, met)

time: 113 us -> 108 us (0.956)
  waiting for transfers between devices: 17.8 us -> 8.03 us
  Pallas kernels: 37.6 us -> 41.2 us
  starting transfers between devices: 25.9 us -> 28.4 us
  other arithmetic: 2.5 us -> 0.06 us
    ppermute x16 -> x21, waiting for transfers between devices: 17.8 us -> 8.03 us  [send(): return lax.ppermute(value, AXES, pairs)]
    pallas_call x1 -> x6, Pallas kernels: 20.8 us -> 24.4 us  [the longest x1 18.6 us: run_fine_product(): pl.pallas_call(functools.partial(fine_product, what), out_shape=(pltpu.VM...]
    ppermute x16 -> x21, starting transfers between devices: 25.9 us -> 28.4 us  [send(): return lax.ppermute(value, AXES, pairs)]
  transfers between devices with their start and end apart: 16 -> 21, of which waited for: 6 -> 5; matrix products, arithmetic and copies ran while one was open for 1% -> 0% of each run, Pallas kernels for 23% -> 27%
where the time goes in v5:
time: 108 us
  Pallas kernels  41.2 us (38%)
  blocking collectives  28.6 us (26%)
  starting transfers between devices  28.4 us (26%)
  waiting for transfers between devices  8.03 us (7%)
  local copies, waits for them, and re-layouts  1.62 us (2%)
    all_to_all x1, blocking collectives, shards(): mixed = lax.all_to_all(packed, ('x', 'yh', 'z', 'yl'), 0, 0, tiled=True)  28.6 us
    ppermute x21, starting transfers between devices, send(): return lax.ppermute(value, AXES, pairs)  28.4 us
    pallas_call x1, Pallas kernels, run_fine_product(): pl.pallas_call(functools.partial(fine_product, what), out_shape=(pltpu.VM...  18.6 us
    pallas_call x1, Pallas kernels, run_other_half(): pl.pallas_call(other_half, out_shape=(pltpu.VMEM((2, 512, hi.shape[0]), B...  8.31 us
    ppermute x21, waiting for transfers between devices, send(): return lax.ppermute(value, AXES, pairs)  8.03 us
    pallas_call x4, Pallas kernels, run_place(): pl.pallas_call(body, out_shape=DENSE, in_specs=[VMEM] * (len(arrays) + le...  5.16 us
    pallas_call x1, Pallas kernels, run_own_half(): pl.pallas_call(own_half, out_shape=HALF, in_specs=[VMEM] * 3, out_specs=V...  5.11 us
    pallas_call x1, Pallas kernels, packed_sum(): pl.pallas_call(pack, out_shape=jax.ShapeDtypeStruct((64, ROWS, 128), jnp....  2.46 us
  transfers between devices with their start and end apart: 21, of which 5 were waited for; matrix products, arithmetic and copies ran while one was open for 0% of the time, Pallas kernels for 27%

profile of v5, /device:TPU:0, one launch (start us, length us, event | category | flops | bytes accessed | tf_op | source)
XLA Modules:
  0.0 108.2 jit_solution(6399936847712152774)
XLA Ops:
  0.0 0.0 copy-start
  0.0 0.9 copy-done
  0.9 0.0 copy-start.1
  0.9 0.7 copy-done.1
  1.6 0.6 stamp.1
  2.2 3.2 %collective-permute-start = (bf16[2,136,256]{2,1,0:T(8,128)(2,1)S(1)}, bf16[2,136,256]{2,1,0:T(8,128)(2,1)S(1)}, u32[]{:S(2)}, u32[]{:S(2)}) collective-permute-start(bf16[2,136,256]{2,1,0:T(8,128)(2,1)S(1)} %stamp.1), channel_id=1, source_target_pairs={{0,64},{1,80},{2,32},{3,48},{4,0},{5,16},{6,96},{7,112},{8,72},{9,... | collective-permute-start | bytes 417800 | tf_op jit(solution)/shard_map/ppermute | solution.py:57
  5.4 2.6 %collective-permute-start.1 = (bf16[2,136,256]{2,1,0:T(8,128)(2,1)S(1)}, bf16[2,136,256]{2,1,0:T(8,128)(2,1)S(1)}, u32[]{:S(2)}, u32[]{:S(2)}) collective-permute-start(bf16[2,136,256]{2,1,0:T(8,128)(2,1)S(1)} %stamp.1), channel_id=1, source_target_pairs={{0,1},{1,0},{2,3},{3,2},{4,5},{5,4},{6,7},{7,6},{8,9},{9,8},{10,11... | collective-permute-start | bytes 417800 | tf_op jit(solution)/shard_map/ppermute | solution.py:57
  8.0 1.9 %collective-permute-done.refs_0_ = bf16[2,136,256]{2,1,0:T(8,128)(2,1)S(1)} collective-permute-done((bf16[2,136,256]{2,1,0:T(8,128)(2,1)S(1)}, bf16[2,136,256]{2,1,0:T(8,128)(2,1)S(1)}, u32[]{:S(2)}, u32[]{:S(2)}) %collective-permute-start) | collective-permute-done | bytes 139296 | tf_op jit(solution)/shard_map/ppermute | solution.py:57
  9.9 1.5 %collective-permute-done.1 = bf16[2,136,256]{2,1,0:T(8,128)(2,1)S(1)} collective-permute-done((bf16[2,136,256]{2,1,0:T(8,128)(2,1)S(1)}, bf16[2,136,256]{2,1,0:T(8,128)(2,1)S(1)}, u32[]{:S(2)}, u32[]{:S(2)}) %collective-permute-start.1) | collective-permute-done | bytes 139296 | tf_op jit(solution)/shard_map/ppermute | solution.py:57
  11.4 0.4 collective-permute-start.2
  11.7 3.3 %collective-permute-start.3 = (bf16[2,136,256]{2,1,0:T(8,128)(2,1)S(1)}, bf16[2,136,256]{2,1,0:T(8,128)(2,1)S(1)}, u32[]{:S(2)}, u32[]{:S(2)}) collective-permute-start(bf16[2,136,256]{2,1,0:T(8,128)(2,1)S(1)} %collective-permute-done.refs_0_), channel_id=1, source_target_pairs={{0,96},{1,97},{2,98},{3,99},{4,100},{5,101},{6,102},{7,103},{8,104... | collective-permute-start | bytes 417800 | tf_op jit(solution)/shard_map/ppermute | solution.py:57
  15.0 5.1 %collective-permute-start.4 = (bf16[2,136,256]{2,1,0:T(8,128)(2,1)S(1)}, bf16[2,136,256]{2,1,0:T(8,128)(2,1)S(1)}, u32[]{:S(2)}, u32[]{:S(2)}) collective-permute-start(bf16[2,136,256]{2,1,0:T(8,128)(2,1)S(1)} %collective-permute-done.refs_0_), channel_id=1, source_target_pairs={{0,16},{1,17},{2,18},{3,19},{4,20},{5,21},{6,22},{7,23},{8,24},{9,... | collective-permute-start | bytes 417800 | tf_op jit(solution)/shard_map/ppermute | solution.py:57
  20.2 0.0 collective-permute-start.5
  20.2 0.3 place.4.refs_4_
  20.6 0.0 collective-permute-done.2.refs_0_
  20.6 0.0 collective-permute-done.3.refs_1_
  20.6 2.6 %collective-permute-done.4.refs_2_ = bf16[2,136,256]{2,1,0:T(8,128)(2,1)S(1)} collective-permute-done((bf16[2,136,256]{2,1,0:T(8,128)(2,1)S(1)}, bf16[2,136,256]{2,1,0:T(8,128)(2,1)S(1)}, u32[]{:S(2)}, u32[]{:S(2)}) %collective-permute-start.4) | collective-permute-done | bytes 139296 | tf_op jit(solution)/shard_map/ppermute | solution.py:57
  23.2 0.0 collective-permute-done.5.refs_3_
  23.3 0.1 collective-permute-start.6
  23.4 3.2 %collective-permute-start.7 = (bf16[3,136,256]{2,1,0:T(8,128)(2,1)S(1)}, bf16[3,136,256]{2,1,0:T(8,128)(2,1)S(1)}, u32[]{:S(2)}, u32[]{:S(2)}) collective-permute-start(bf16[3,136,256]{2,1,0:T(8,128)(2,1)S(1)} %get-tuple-element.51), channel_id=1, source_target_pairs={{0,96},{1,97},{2,98},{3,99},{4,100},{5,101},{6,102},{7,103},{8,104... | collective-permute-start | bytes 626696 | tf_op jit(solution)/shard_map/ppermute | solution.py:57
  26.6 0.0 collective-permute-start.10
  26.6 0.5 collective-permute-start.8
  27.1 0.0 collective-permute-start.9
  27.1 1.4 %place.5.refs_5_ = bf16[64,64,1024]{2,1,0:T(8,128)(2,1)S(1)} custom-call(bf16[2,136,256]{2,1,0:T(8,128)(2,1)S(1)} %collective-permute-done.2.refs_0_, bf16[2,136,256]{2,1,0:T(8,128)(2,1)S(1)} %collective-permute-done.3.refs_1_, bf16[2,136,256]{2,1,0:T(8,128)(2,1)S(1)} %collective-permute-done.4.refs_2_, ...), custom_call_target="tpu_custom_call", output_to_operand_aliasing={{}: (4, {})} | custom-call | flops 1073741824 | bytes 8388608 | tf_op jit(solution)/shard_map/place/pallas_call | solution.py:224
  28.5 0.0 collective-permute-done.10.refs_4_
  28.5 0.0 collective-permute-done.8.refs_2_
  28.5 0.0 collective-permute-done.9.refs_3_
  28.6 1.8 %collective-permute-done.6.refs_0_ = bf16[3,136,256]{2,1,0:T(8,128)(2,1)S(1)} collective-permute-done((bf16[3,136,256]{2,1,0:T(8,128)(2,1)S(1)}, bf16[3,136,256]{2,1,0:T(8,128)(2,1)S(1)}, u32[]{:S(2)}, u32[]{:S(2)}) %collective-permute-start.6) | collective-permute-done | bytes 208928 | tf_op jit(solution)/shard_map/ppermute | solution.py:57
  30.4 0.0 collective-permute-done.7.refs_1_
  30.4 0.0 collective-permute-start.13
  30.4 0.5 collective-permute-start.14
  30.9 0.4 collective-permute-start.17
  31.3 0.2 collective-permute-start.11
  31.4 3.2 %collective-permute-start.12 = (bf16[1,136,256]{2,1,0:T(8,128)(2,1)S(1)}, bf16[1,136,256]{2,1,0:T(8,128)(2,1)S(1)}, u32[]{:S(2)}, u32[]{:S(2)}) collective-permute-start(bf16[1,136,256]{2,1,0:T(8,128)(2,1)S(1)} %slice.15), channel_id=1, source_target_pairs={{0,96},{1,97},{2,98},{3,99},{4,100},{5,101},{6,102},{7,103},{8,104... | collective-permute-start | bytes 208904 | tf_op jit(solution)/shard_map/ppermute | solution.py:57
  34.6 2.1 %place.6.refs_4_ = bf16[64,64,1024]{2,1,0:T(8,128)(2,1)S(1)} custom-call(bf16[3,136,256]{2,1,0:T(8,128)(2,1)S(1)} %collective-permute-done.6.refs_0_, bf16[3,136,256]{2,1,0:T(8,128)(2,1)S(1)} %collective-permute-done.7.refs_1_, bf16[2,136,256]{2,1,0:T(8,128)(2,1)S(1)} %collective-permute-done.8.refs_2_, ...), custom_call_target="tpu_custom_call", output_to_operand_aliasing={{}: (5, {})} | custom-call | flops 1073741824 | bytes 8388608 | tf_op jit(solution)/shard_map/place/pallas_call | solution.py:224
  36.7 0.0 copy-start.2
  36.7 0.2 collective-permute-done.11.refs_0_
  36.9 3.5 %collective-permute-start.18 = (bf16[4,136,256]{2,1,0:T(8,128)(2,1)S(1)}, bf16[4,136,256]{2,1,0:T(8,128)(2,1)S(1)}, u32[]{:S(2)}, u32[]{:S(2)}) collective-permute-start(bf16[4,136,256]{2,1,0:T(8,128)(2,1)S(1)} %pad_maximum_fusion.r0), channel_id=1, source_target_pairs={{0,6},{1,7},{2,0},{3,1},{4,2},{5,3},{6,4},{7,5},{8,14},{9,15},{10,... | collective-permute-start | bytes 835592 | tf_op jit(solution)/shard_map/ppermute | solution.py:57
  40.4 0.0 collective-permute-done.12.refs_1_
  40.4 1.5 %collective-permute-start.19 = (bf16[4,136,256]{2,1,0:T(8,128)(2,1)S(1)}, bf16[4,136,256]{2,1,0:T(8,128)(2,1)S(1)}, u32[]{:S(2)}, u32[]{:S(2)}) collective-permute-start(bf16[4,136,256]{2,1,0:T(8,128)(2,1)S(1)} %pad_maximum_fusion.r0), channel_id=1, source_target_pairs={{0,4},{1,5},{2,6},{3,7},{4,0},{5,1},{6,2},{7,3},{8,12},{9,13},{10,... | collective-permute-start | bytes 835592 | tf_op jit(solution)/shard_map/ppermute | solution.py:57
  41.9 0.0 collective-permute-done.13.refs_2_
  41.9 0.0 collective-permute-done.14.refs_3_
  41.9 0.0 collective-permute-start.15
  41.9 0.5 collective-permute-start.16
  42.4 1.3 %place.7.refs_2_ = bf16[64,64,1024]{2,1,0:T(8,128)(2,1)S(1)} custom-call(bf16[1,136,256]{2,1,0:T(8,128)(2,1)S(1)} %collective-permute-done.11.refs_0_, bf16[1,136,256]{2,1,0:T(8,128)(2,1)S(1)} %collective-permute-done.12.refs_1_, bf16[3,136,256]{2,1,0:T(8,128)(2,1)S(1)} %collective-permute-done.13.refs_2_, ...), custom_call_target="tpu_custom_call", output_to_operand_aliasing={{}: (4, {})} | custom-call | flops 1073741824 | bytes 8388608 | tf_op jit(solution)/shard_map/place/pallas_call | solution.py:224
  43.8 0.0 collective-permute-done.15.refs_0_
  43.8 0.0 collective-permute-done.16.refs_1_
  43.8 0.0 copy-done.2
  43.8 18.6 %fine_product.1 = (bf16[2048,1024]{1,0:T(8,128)(2,1)S(1)}, bf16[2048,1024]{1,0:T(8,128)(2,1)S(1)}, bf16[64,64,1024]{2,1,0:T(8,128)(2,1)S(1)}) custom-call(s32[16,32]{1,0:T(8,128)S(1)} %bitcast.4, bf16[32,64,1024]{2,1,0:T(8,128)(2,1)} %bitcast.5, bf16[1,136,256]{2,1,0:T(8,128)(2,1)S(1)} %collective-permute-done.15.refs_0_, ...), custom_call_target="tpu_custom_call", output_to_operand_aliasing={{2}: (4, {})} | custom-call | flops 17179869184 | bytes 8388608 | tf_op jit(solution)/shard_map/fine_product/pallas_call | solution.py:238
  62.4 0.0 collective-permute-done.17.r1
  62.4 0.0 collective-permute-done.18.r2
  62.4 0.0 collective-permute-done.19.r3
  62.4 8.3 %other_half.1 = (bf16[2,512,2048]{2,1,0:T(8,128)(2,1)S(1)}, f32[64,64,128]{2,1,0:T(8,128)S(1)}) custom-call(bf16[2048,1024]{1,0:T(8,128)(2,1)S(1)} %get-tuple-element.46.hi, bf16[2048,1024]{1,0:T(8,128)(2,1)S(1)} %get-tuple-element.47.lo, bf16[4,136,256]{2,1,0:T(8,128)(2,1)S(1)} %pad_maximum_fusion.r0, bf16[4,136,256]{2,1,0:T(8,128)(2,1)S(1)} %collective-permute-done.17.r1, ...), custom_call_target="tpu_custom_call" | custom-call | flops 8589934592 | bytes 8388608 | tf_op jit(solution)/shard_map/other_half/pallas_call | solution.py:252
  70.8 0.2 collective-permute-start.20
  70.9 5.1 %own_half.1.a_ref = f32[64,64,128]{2,1,0:T(8,128)S(1)} custom-call(bf16[2048,1024]{1,0:T(8,128)(2,1)S(1)} %get-tuple-element.46.hi, bf16[2048,1024]{1,0:T(8,128)(2,1)S(1)} %get-tuple-element.47.lo, bf16[2,512,2048]{2,1,0:T(8,128)(2,1)S(1)} %get-tuple-element.49.turned), custom_call_target="tpu_custom_call" | custom-call | flops 8589934592 | bytes 8388608 | tf_op jit(solution)/shard_map/own_half/pallas_call | solution.py:264
  76.1 0.0 collective-permute-done.20.b_ref
  76.1 2.5 %pack.1 = s16[64,72,128]{2,1,0:T(8,128)(2,1)S(1)} custom-call(f32[64,64,128]{2,1,0:T(8,128)S(1)} %own_half.1.a_ref, f32[64,64,128]{2,1,0:T(8,128)S(1)} %collective-permute-done.20.b_ref), custom_call_target="tpu_custom_call" | custom-call | tf_op jit(solution)/shard_map/pack/pallas_call | solution.py:359
  78.5 28.6 %all_to_all.5.in_ref = s16[64,72,128]{2,1,0:T(8,128)(2,1)S(1)} all-to-all(s16[64,72,128]{2,1,0:T(8,128)(2,1)S(1)} %pack.1), channel_id=1, replica_groups=mesh['x'=4,'yh'=2,'core'=2,'z'=4,'yl'=2] {'x','yh','z','yl'}, dimensions={0} | all-to-all | bytes 2359296 | tf_op jit(solution)/shard_map/all_to_all | solution.py:388
  107.2 1.0 unpack.1
  (6 shorter events, 0.1 us)
Async XLA Ops:
  0.0 0.9 copy-start
  0.9 0.7 copy-start.1
  2.2 7.7 %collective-permute-start = (bf16[2,136,256]{2,1,0:T(8,128)(2,1)S(1)}, bf16[2,136,256]{2,1,0:T(8,128)(2,1)S(1)}, u32[]{:S(2)}, u32[]{:S(2)}) collective-permute-start(bf16[2,136,256]{2,1,0:T(8,128)(2,1)S(1)} %stamp.1), channel_id=1, source_target_pairs={{0,64},{1,80},{2,32},{3,48},{4,0},{5,16},{6,96},{7,112},{8,72},{9,... | collective-permute-start | bytes 417800 | tf_op jit(solution)/shard_map/ppermute | solution.py:57
  5.4 6.0 %collective-permute-start.1 = (bf16[2,136,256]{2,1,0:T(8,128)(2,1)S(1)}, bf16[2,136,256]{2,1,0:T(8,128)(2,1)S(1)}, u32[]{:S(2)}, u32[]{:S(2)}) collective-permute-start(bf16[2,136,256]{2,1,0:T(8,128)(2,1)S(1)} %stamp.1), channel_id=1, source_target_pairs={{0,1},{1,0},{2,3},{3,2},{4,5},{5,4},{6,7},{7,6},{8,9},{9,8},{10,11... | collective-permute-start | bytes 417800 | tf_op jit(solution)/shard_map/ppermute | solution.py:57
  11.4 9.2 %collective-permute-start.2 = (bf16[2,136,256]{2,1,0:T(8,128)(2,1)S(1)}, bf16[2,136,256]{2,1,0:T(8,128)(2,1)S(1)}, u32[]{:S(2)}, u32[]{:S(2)}) collective-permute-start(bf16[2,136,256]{2,1,0:T(8,128)(2,1)S(1)} %collective-permute-done.refs_0_), channel_id=1, source_target_pairs={{0,32},{1,33},{2,34},{3,35},{4,36},{5,37},{6,38},{7,39},{8,40},{9,... | collective-permute-start | bytes 417800 | tf_op jit(solution)/shard_map/ppermute | solution.py:57
  11.7 8.9 %collective-permute-start.3 = (bf16[2,136,256]{2,1,0:T(8,128)(2,1)S(1)}, bf16[2,136,256]{2,1,0:T(8,128)(2,1)S(1)}, u32[]{:S(2)}, u32[]{:S(2)}) collective-permute-start(bf16[2,136,256]{2,1,0:T(8,128)(2,1)S(1)} %collective-permute-done.refs_0_), channel_id=1, source_target_pairs={{0,96},{1,97},{2,98},{3,99},{4,100},{5,101},{6,102},{7,103},{8,104... | collective-permute-start | bytes 417800 | tf_op jit(solution)/shard_map/ppermute | solution.py:57
  15.0 8.2 %collective-permute-start.4 = (bf16[2,136,256]{2,1,0:T(8,128)(2,1)S(1)}, bf16[2,136,256]{2,1,0:T(8,128)(2,1)S(1)}, u32[]{:S(2)}, u32[]{:S(2)}) collective-permute-start(bf16[2,136,256]{2,1,0:T(8,128)(2,1)S(1)} %collective-permute-done.refs_0_), channel_id=1, source_target_pairs={{0,16},{1,17},{2,18},{3,19},{4,20},{5,21},{6,22},{7,23},{8,24},{9,... | collective-permute-start | bytes 417800 | tf_op jit(solution)/shard_map/ppermute | solution.py:57
  20.2 3.0 %collective-permute-start.5 = (bf16[2,136,256]{2,1,0:T(8,128)(2,1)S(1)}, bf16[2,136,256]{2,1,0:T(8,128)(2,1)S(1)}, u32[]{:S(2)}, u32[]{:S(2)}) collective-permute-start(bf16[2,136,256]{2,1,0:T(8,128)(2,1)S(1)} %collective-permute-done.refs_0_), channel_id=1, source_target_pairs={{0,8},{1,9},{2,10},{3,11},{4,12},{5,13},{6,14},{7,15},{8,0},{9,1},... | collective-permute-start | bytes 417800 | tf_op jit(solution)/shard_map/ppermute | solution.py:57
  23.3 7.1 %collective-permute-start.6 = (bf16[3,136,256]{2,1,0:T(8,128)(2,1)S(1)}, bf16[3,136,256]{2,1,0:T(8,128)(2,1)S(1)}, u32[]{:S(2)}, u32[]{:S(2)}) collective-permute-start(bf16[3,136,256]{2,1,0:T(8,128)(2,1)S(1)} %get-tuple-element.52), channel_id=1, source_target_pairs={{0,32},{1,33},{2,34},{3,35},{4,36},{5,37},{6,38},{7,39},{8,40},{9,... | collective-permute-start | bytes 626696 | tf_op jit(solution)/shard_map/ppermute | solution.py:57
  23.4 7.0 %collective-permute-start.7 = (bf16[3,136,256]{2,1,0:T(8,128)(2,1)S(1)}, bf16[3,136,256]{2,1,0:T(8,128)(2,1)S(1)}, u32[]{:S(2)}, u32[]{:S(2)}) collective-permute-start(bf16[3,136,256]{2,1,0:T(8,128)(2,1)S(1)} %get-tuple-element.51), channel_id=1, source_target_pairs={{0,96},{1,97},{2,98},{3,99},{4,100},{5,101},{6,102},{7,103},{8,104... | collective-permute-start | bytes 626696 | tf_op jit(solution)/shard_map/ppermute | solution.py:57
  26.6 1.9 %collective-permute-start.10 = (bf16[2,136,256]{2,1,0:T(8,128)(2,1)S(1)}, bf16[2,136,256]{2,1,0:T(8,128)(2,1)S(1)}, u32[]{:S(2)}, u32[]{:S(2)}) collective-permute-start(bf16[2,136,256]{2,1,0:T(8,128)(2,1)S(1)} %collective-permute-done.4.refs_2_), channel_id=1, source_target_pairs={{0,8},{1,9},{2,10},{3,11},{4,12},{5,13},{6,14},{7,15},{8,0},{9,1},... | collective-permute-start | bytes 417800 | tf_op jit(solution)/shard_map/ppermute | solution.py:57
  26.6 1.9 %collective-permute-start.8 = (bf16[2,136,256]{2,1,0:T(8,128)(2,1)S(1)}, bf16[2,136,256]{2,1,0:T(8,128)(2,1)S(1)}, u32[]{:S(2)}, u32[]{:S(2)}) collective-permute-start(bf16[2,136,256]{2,1,0:T(8,128)(2,1)S(1)} %collective-permute-done.2.refs_0_), channel_id=1, source_target_pairs={{0,8},{1,9},{2,10},{3,11},{4,12},{5,13},{6,14},{7,15},{8,0},{9,1},... | collective-permute-start | bytes 417800 | tf_op jit(solution)/shard_map/ppermute | solution.py:57
  27.1 1.4 %collective-permute-start.9 = (bf16[2,136,256]{2,1,0:T(8,128)(2,1)S(1)}, bf16[2,136,256]{2,1,0:T(8,128)(2,1)S(1)}, u32[]{:S(2)}, u32[]{:S(2)}) collective-permute-start(bf16[2,136,256]{2,1,0:T(8,128)(2,1)S(1)} %collective-permute-done.3.refs_1_), channel_id=1, source_target_pairs={{0,8},{1,9},{2,10},{3,11},{4,12},{5,13},{6,14},{7,15},{8,0},{9,1},... | collective-permute-start | bytes 417800 | tf_op jit(solution)/shard_map/ppermute | solution.py:57
  30.4 11.6 %collective-permute-start.13 = (bf16[3,136,256]{2,1,0:T(8,128)(2,1)S(1)}, bf16[3,136,256]{2,1,0:T(8,128)(2,1)S(1)}, u32[]{:S(2)}, u32[]{:S(2)}) collective-permute-start(bf16[3,136,256]{2,1,0:T(8,128)(2,1)S(1)} %collective-permute-done.6.refs_0_), channel_id=1, source_target_pairs={{0,8},{1,9},{2,10},{3,11},{4,12},{5,13},{6,14},{7,15},{8,0},{9,1},... | collective-permute-start | bytes 626696 | tf_op jit(solution)/shard_map/ppermute | solution.py:57
  30.4 11.6 %collective-permute-start.14 = (bf16[3,136,256]{2,1,0:T(8,128)(2,1)S(1)}, bf16[3,136,256]{2,1,0:T(8,128)(2,1)S(1)}, u32[]{:S(2)}, u32[]{:S(2)}) collective-permute-start(bf16[3,136,256]{2,1,0:T(8,128)(2,1)S(1)} %collective-permute-done.7.refs_1_), channel_id=1, source_target_pairs={{0,8},{1,9},{2,10},{3,11},{4,12},{5,13},{6,14},{7,15},{8,0},{9,1},... | collective-permute-start | bytes 626696 | tf_op jit(solution)/shard_map/ppermute | solution.py:57
  30.9 31.5 %collective-permute-start.17 = (bf16[4,136,256]{2,1,0:T(8,128)(2,1)S(1)}, bf16[4,136,256]{2,1,0:T(8,128)(2,1)S(1)}, u32[]{:S(2)}, u32[]{:S(2)}) collective-permute-start(bf16[4,136,256]{2,1,0:T(8,128)(2,1)S(1)} %pad_maximum_fusion.r0), channel_id=1, source_target_pairs={{0,2},{1,3},{2,4},{3,5},{4,6},{5,7},{6,0},{7,1},{8,10},{9,11},{10,... | collective-permute-start | bytes 835592 | tf_op jit(solution)/shard_map/ppermute | solution.py:57
  31.3 5.6 %collective-permute-start.11 = (bf16[1,136,256]{2,1,0:T(8,128)(2,1)S(1)}, bf16[1,136,256]{2,1,0:T(8,128)(2,1)S(1)}, u32[]{:S(2)}, u32[]{:S(2)}) collective-permute-start(bf16[1,136,256]{2,1,0:T(8,128)(2,1)S(1)} %slice.14), channel_id=1, source_target_pairs={{0,32},{1,33},{2,34},{3,35},{4,36},{5,37},{6,38},{7,39},{8,40},{9,... | collective-permute-start | bytes 208904 | tf_op jit(solution)/shard_map/ppermute | solution.py:57
  31.4 9.0 %collective-permute-start.12 = (bf16[1,136,256]{2,1,0:T(8,128)(2,1)S(1)}, bf16[1,136,256]{2,1,0:T(8,128)(2,1)S(1)}, u32[]{:S(2)}, u32[]{:S(2)}) collective-permute-start(bf16[1,136,256]{2,1,0:T(8,128)(2,1)S(1)} %slice.15), channel_id=1, source_target_pairs={{0,96},{1,97},{2,98},{3,99},{4,100},{5,101},{6,102},{7,103},{8,104... | collective-permute-start | bytes 208904 | tf_op jit(solution)/shard_map/ppermute | solution.py:57
  36.7 7.1 %copy-start.2 = (s32[32,1,16]{0,2,1:T(8,128)S(1)}, s32[32,1,16]{0,2,1:T(8,128)}, u32[]{:S(2)}) copy-start(s32[32,1,16]{0,2,1:T(8,128)} %param.5) | copy-start | bytes 6148
  36.9 25.5 %collective-permute-start.18 = (bf16[4,136,256]{2,1,0:T(8,128)(2,1)S(1)}, bf16[4,136,256]{2,1,0:T(8,128)(2,1)S(1)}, u32[]{:S(2)}, u32[]{:S(2)}) collective-permute-start(bf16[4,136,256]{2,1,0:T(8,128)(2,1)S(1)} %pad_maximum_fusion.r0), channel_id=1, source_target_pairs={{0,6},{1,7},{2,0},{3,1},{4,2},{5,3},{6,4},{7,5},{8,14},{9,15},{10,... | collective-permute-start | bytes 835592 | tf_op jit(solution)/shard_map/ppermute | solution.py:57
  40.4 22.0 %collective-permute-start.19 = (bf16[4,136,256]{2,1,0:T(8,128)(2,1)S(1)}, bf16[4,136,256]{2,1,0:T(8,128)(2,1)S(1)}, u32[]{:S(2)}, u32[]{:S(2)}) collective-permute-start(bf16[4,136,256]{2,1,0:T(8,128)(2,1)S(1)} %pad_maximum_fusion.r0), channel_id=1, source_target_pairs={{0,4},{1,5},{2,6},{3,7},{4,0},{5,1},{6,2},{7,3},{8,12},{9,13},{10,... | collective-permute-start | bytes 835592 | tf_op jit(solution)/shard_map/ppermute | solution.py:57
  41.9 1.8 %collective-permute-start.15 = (bf16[1,136,256]{2,1,0:T(8,128)(2,1)S(1)}, bf16[1,136,256]{2,1,0:T(8,128)(2,1)S(1)}, u32[]{:S(2)}, u32[]{:S(2)}) collective-permute-start(bf16[1,136,256]{2,1,0:T(8,128)(2,1)S(1)} %collective-permute-done.11.refs_0_), channel_id=1, source_target_pairs={{0,8},{1,9},{2,10},{3,11},{4,12},{5,13},{6,14},{7,15},{8,0},{9,1},... | collective-permute-start | bytes 208904 | tf_op jit(solution)/shard_map/ppermute | solution.py:57
  41.9 1.8 %collective-permute-start.16 = (bf16[1,136,256]{2,1,0:T(8,128)(2,1)S(1)}, bf16[1,136,256]{2,1,0:T(8,128)(2,1)S(1)}, u32[]{:S(2)}, u32[]{:S(2)}) collective-permute-start(bf16[1,136,256]{2,1,0:T(8,128)(2,1)S(1)} %collective-permute-done.12.refs_1_), channel_id=1, source_target_pairs={{0,8},{1,9},{2,10},{3,11},{4,12},{5,13},{6,14},{7,15},{8,0},{9,1},... | collective-permute-start | bytes 208904 | tf_op jit(solution)/shard_map/ppermute | solution.py:57
  70.8 5.3 %collective-permute-start.20 = (f32[64,64,128]{2,1,0:T(8,128)S(1)}, f32[64,64,128]{2,1,0:T(8,128)S(1)}, u32[]{:S(2)}, u32[]{:S(2)}) collective-permute-start(f32[64,64,128]{2,1,0:T(8,128)S(1)} %get-tuple-element.50), channel_id=1, source_target_pairs={{0,8},{1,9},{2,10},{3,11},{4,12},{5,13},{6,14},{7,15},{8,0},{9,1},... | collective-permute-start | bytes 6291464 | tf_op jit(solution)/shard_map/ppermute | solution.py:57

commit v6 on v5

--- a/solution.py
+++ b/solution.py
@@ -136,12 +136,9 @@
         place(ref, halves, other, refs[-1])
 
 
-def fine_product(what, cols_ref, a_hbm, *refs):
-    arrays, (dense_in, hi, lo, dense, a_ref, sem) = refs[: len(what)], refs[len(what) :]
-    fetch = pltpu.make_async_copy(a_hbm, a_ref, sem)
-    fetch.start()
+def fine_product(what, cols_ref, a_ref, *refs):
+    arrays, (dense_in, hi, lo, dense) = refs[: len(what)], refs[len(what) :]
     place_all(what, *arrays, dense)
-    fetch.wait()
 
     @pl.loop(0, a_ref.shape[0])
     def _(i):
@@ -205,6 +202,10 @@
     half_product(turned, 0, hi, lo, out_ref)
 
 
+def in_hbm(v):
+    return pltpu.with_memory_space_constraint(v, pltpu.HBM)
+
+
 VMEM = pl.BlockSpec(memory_space=pltpu.VMEM)
 SMEM = pl.BlockSpec(memory_space=pltpu.SMEM)
 HBM = pl.BlockSpec(memory_space=pltpu.HBM)
@@ -218,19 +219,32 @@
 DENSE = pltpu.VMEM((64, BS, 1024), BF16)
 
 
-def run_place(what, arrays, dense):
+def run_place(what, arrays, dense, a=None):
     given = () if dense is None else (dense,)
-    body = lambda *refs: place_all(what, *refs[: len(what)], refs[-1])
-    return pl.pallas_call(
+    fetched = () if a is None else (a,)
+    count = len(arrays) + len(given)
+
+    def body(*refs):
+        if a is None:
+            place_all(what, *refs[: len(what)], refs[-1])
+        else:
+            fetch = pltpu.make_async_copy(refs[count], refs[count + 2], refs[-1])
+            fetch.start()
+            place_all(what, *refs[: len(what)], refs[count + 1])
+            fetch.wait()
+
+    out = pl.pallas_call(
         body,
-        out_shape=DENSE,
-        in_specs=[VMEM] * (len(arrays) + len(given)),
-        out_specs=VMEM,
+        out_shape=(DENSE,) + tuple(pltpu.VMEM(v.shape, v.dtype) for v in fetched),
+        in_specs=[VMEM] * count + [HBM] * len(fetched),
+        out_specs=(VMEM,) * (1 + len(fetched)),
+        scratch_shapes=[pltpu.SemaphoreType.DMA] * len(fetched),
         input_output_aliases={len(arrays): 0} if given else {},
         compiler_params=pltpu.CompilerParams(vmem_limit_bytes=16 << 20),
         cost_estimate=cost(1 << 30),
         name="place",
-    )(*arrays, *given)
+    )(*arrays, *given, *fetched)
+    return out if fetched else out[0]
 
 
 def run_fine_product(what, cols, a, arrays, dense):
@@ -238,11 +252,10 @@
     return pl.pallas_call(
         functools.partial(fine_product, what),
         out_shape=(pltpu.VMEM((rows, 1024), BF16),) * 2 + (DENSE,),
-        in_specs=[SMEM, HBM] + [VMEM] * (len(arrays) + 1),
+        in_specs=[SMEM] + [VMEM] * (len(arrays) + 2),
         out_specs=(VMEM,) * 3,
-        scratch_shapes=[pltpu.VMEM(a.shape, BF16), pltpu.SemaphoreType.DMA],
         input_output_aliases={2 + len(arrays): 2},
-        compiler_params=pltpu.CompilerParams(vmem_limit_bytes=24 << 20),
+        compiler_params=pltpu.CompilerParams(vmem_limit_bytes=16 << 20),
         cost_estimate=cost(2 << 33),
         name="fine_product",
     )(cols, a, *arrays, dense)
@@ -272,11 +285,14 @@
     )(hi, lo, turned)
 
 
-def stamp(cols_ref, vals_ref, out_ref):
+def stamp(cols_ref, vals_ref, out_ref, sems):
+    copies = []
+    for b in range(4):
+        to = out_ref.at[b // 2, pl.ds(BS * (b % 2), BS)]
+        copies.append(pltpu.make_async_copy(vals_ref.at[b], to, sems.at[b]))
+        copies[b].start()
     block = lax.broadcasted_iota(jnp.int32, (1, 4 * BS), 1) // BS
     for h in range(2):
-        out_ref[h, :BS, :] = vals_ref[2 * h]
-        out_ref[h, BS : 2 * BS, :] = vals_ref[2 * h + 1]
         rows = []
         for b in range(2):
             row = jnp.zeros((1, 4 * BS), jnp.int32)
@@ -285,52 +301,53 @@
             rows.append(row)
         rows.append(jnp.zeros((6, 4 * BS), jnp.int32))
         out_ref[h, 2 * BS :, :] = jnp.concatenate(rows).astype(F32).astype(BF16)
+    for copy in copies:
+        copy.wait()
 
 
 def run_stamp(cols, vals):
     return pl.pallas_call(
         stamp,
         out_shape=jax.ShapeDtypeStruct((2, HALF_ROWS, 4 * BS), BF16),
-        in_specs=[SMEM, VMEM],
+        in_specs=[SMEM, HBM],
         out_specs=VMEM,
+        scratch_shapes=[pltpu.SemaphoreType.DMA((4,))],
         compiler_params=pltpu.CompilerParams(vmem_limit_bytes=2 << 20),
         name="stamp",
-    )(cols, vals)
+    )(in_hbm(cols), in_hbm(vals))
 
 
 def fetch_and_multiply(piece, cols, a):
     near, beside = together(send(piece, REFLECT), send(piece, BESIDE))
-    b1, a1, f, e0, r0, dense = together(
+    b1, a1, f, r0, dense = together(
         send(near, NEXT_X),
         send(near, LAST_X),
         send(near, ACROSS_Y),
-        send(near, OTHER_CORE),
         jnp.concatenate([piece, beside]),
         run_place(((NEAR, False),), (near,), None),
     )
-    what = ((BEHIND, False), (AHEAD, False), (ACROSS, False), (NEAR, True))
-    b2, a2, e1, e2, e3, dense = together(
+    what = ((BEHIND, False), (AHEAD, False), (ACROSS, False))
+    b2, a2, e1, r0, dense = together(
         send(jnp.concatenate([f, b1[:1]]), NEXT_X),
         send(jnp.concatenate([f, a1[1:]]), LAST_X),
-        send(b1, OTHER_CORE),
-        send(a1, OTHER_CORE),
-        send(f, OTHER_CORE),
-        run_place(what, (b1, a1, f, e0), dense),
+        send(jnp.concatenate([near, b1, a1, f]), OTHER_CORE),
+        r0,
+        run_place(what, (b1, a1, f), dense),
     )
-    what = ((BEHIND2, False), (AHEAD2, False), (BEHIND, True), (AHEAD, True), (ACROSS, True))
-    b3, a3, e4, e5, dense = together(
+    what = ((BEHIND2, False), (AHEAD2, False), (NEAR + BEHIND + AHEAD + ACROSS, True))
+    b3, a3, e2, r0, (dense, a) = together(
         send(b2[:1], NEXT_X),
         send(a2[1:2], LAST_X),
-        send(b2, OTHER_CORE),
-        send(a2, OTHER_CORE),
-        run_place(what, (b2, a2, e1, e2, e3), dense),
+        send(jnp.concatenate([b2, a2]), OTHER_CORE),
+        r0,
+        run_place(what, (b2, a2, e1), dense, a),
     )
-    what = ((BEHIND3, False), (AHEAD3, False), (BEHIND2, True), (AHEAD2, True))
-    e6, e7 = send(b3, OTHER_CORE), send(a3, OTHER_CORE)
+    e3 = send(jnp.concatenate([b3, a3]), OTHER_CORE)
     r1, r2, r3 = send(r0, NEXT_Z), send(r0, LAST_Z), send(r0, ACROSS_Z)
-    dense = run_place(what, (b3, a3, e4, e5), dense)
-    what = ((BEHIND3, True), (AHEAD3, True))
-    hi, lo, dense = run_fine_product(what, cols, a, (e6, e7), dense)
+    what = ((BEHIND3, False), (AHEAD3, False), (BEHIND2 + AHEAD2, True))
+    dense = run_place(what, (b3, a3, e2), dense)
+    what = ((BEHIND3 + AHEAD3, True),)
+    hi, lo, dense = run_fine_product(what, cols, a, (e3,), dense)
     return hi, lo, (r0, r1, r2, r3)
 
 
@@ -378,7 +395,7 @@
 
 
 def shards(a_vals, a_cols, p_vals, p_cols):
-    a = pltpu.with_memory_space_constraint(a_vals[:, 0], pltpu.HBM)
+    a = in_hbm(a_vals[:, 0])
     piece = run_stamp(p_cols, p_vals)
     hi, lo, pr = fetch_and_multiply(piece, a_cols[:, 0].T, a)
     turned, other = run_other_half(hi, lo, pr)

time: 108 us -> 108 us (level)
  waiting for transfers between devices: 8.03 us -> 10.6 us
  starting transfers between devices: 28.4 us -> 26.6 us
  blocking collectives: 28.6 us -> 30.2 us
  local copies, waits for them, and re-layouts: 1.62 us -> 0.03 us
    ppermute x21 -> x16, waiting for transfers between devices: 8.03 us -> 10.6 us  [send(): return lax.ppermute(value, AXES, pairs)]
    pallas_call x1, Pallas kernels: 18.6 us -> 16.6 us  [run_fine_product(): pl.pallas_call(functools.partial(fine_product, what), out_shape=(pltpu.VM...]
    ppermute x21 -> x16, starting transfers between devices: 28.4 us -> 26.6 us  [send(): return lax.ppermute(value, AXES, pairs)]
    all_to_all x1, blocking collectives: 28.6 us -> 30.2 us  [shards(): mixed = lax.all_to_all(packed, ('x', 'yh', 'z', 'yl'), 0, 0, tiled=True)]
    unnamed x6 -> x2, local copies, waits for them, and re-layouts: 1.59 us -> 0.01 us
  transfers between devices with their start and end apart: 21 -> 16, of which waited for: 5 -> 5; matrix products, arithmetic and copies ran while one was open for 0% -> 0% of each run, Pallas kernels for 27% -> 25%
where the time goes in v6:
time: 108 us
  Pallas kernels  40.2 us (37%)
  blocking collectives  30.2 us (28%)
  starting transfers between devices  26.6 us (25%)
  waiting for transfers between devices  10.6 us (10%)
    all_to_all x1, blocking collectives, shards(): mixed = lax.all_to_all(packed, ('x', 'yh', 'z', 'yl'), 0, 0, tiled=True)  30.2 us
    ppermute x16, starting transfers between devices, send(): return lax.ppermute(value, AXES, pairs)  26.6 us
    pallas_call x1, Pallas kernels, run_fine_product(): pl.pallas_call(functools.partial(fine_product, what), out_shape=(pltpu.VM...  16.6 us
    ppermute x16, waiting for transfers between devices, send(): return lax.ppermute(value, AXES, pairs)  10.6 us
    pallas_call x1, Pallas kernels, run_other_half(): pl.pallas_call(other_half, out_shape=(pltpu.VMEM((2, 512, hi.shape[0]), B...  8.31 us
    pallas_call x4, Pallas kernels, run_place(): pl.pallas_call(body, out_shape=(DENSE,) + tuple((pltpu.VMEM(v.shape, v.dt...  5.18 us
    pallas_call x1, Pallas kernels, run_own_half(): pl.pallas_call(own_half, out_shape=HALF, in_specs=[VMEM] * 3, out_specs=V...  5.1 us
    pallas_call x1, Pallas kernels, packed_sum(): pl.pallas_call(pack, out_shape=jax.ShapeDtypeStruct((64, ROWS, 128), jnp....  2.46 us
  transfers between devices with their start and end apart: 16, of which 5 were waited for; matrix products, arithmetic and copies ran while one was open for 0% of the time, Pallas kernels for 25%

profile of v6, /device:TPU:0, one launch (start us, length us, event | category | flops | bytes accessed | tf_op | source)
XLA Modules:
  0.0 108.1 jit_solution(3655105363718162231)
XLA Ops:
  0.0 1.5 %stamp.1 = bf16[2,136,256]{2,1,0:T(8,128)(2,1)S(1)} custom-call(s32[4,4]{1,0:T(4,128)} %cols_ref.1, bf16[4,64,256]{2,1,0:T(8,128)(2,1)} %vals_ref.1), custom_call_target="tpu_custom_call" | custom-call | tf_op jit(solution)/shard_map/stamp/pallas_call | solution.py:309
  1.5 3.2 %collective-permute-start = (bf16[2,136,256]{2,1,0:T(8,128)(2,1)S(1)}, bf16[2,136,256]{2,1,0:T(8,128)(2,1)S(1)}, u32[]{:S(2)}, u32[]{:S(2)}) collective-permute-start(bf16[2,136,256]{2,1,0:T(8,128)(2,1)S(1)} %stamp.1), channel_id=1, source_target_pairs={{0,64},{1,80},{2,32},{3,48},{4,0},{5,16},{6,96},{7,112},{8,72},{9,... | collective-permute-start | bytes 417800 | tf_op jit(solution)/shard_map/ppermute | solution.py:57
  4.7 2.6 %collective-permute-start.1 = (bf16[2,136,256]{2,1,0:T(8,128)(2,1)S(1)}, bf16[2,136,256]{2,1,0:T(8,128)(2,1)S(1)}, u32[]{:S(2)}, u32[]{:S(2)}) collective-permute-start(bf16[2,136,256]{2,1,0:T(8,128)(2,1)S(1)} %stamp.1), channel_id=1, source_target_pairs={{0,1},{1,0},{2,3},{3,2},{4,5},{5,4},{6,7},{7,6},{8,9},{9,8},{10,11... | collective-permute-start | bytes 417800 | tf_op jit(solution)/shard_map/ppermute | solution.py:57
  7.3 1.9 %collective-permute-done.refs_0_ = bf16[2,136,256]{2,1,0:T(8,128)(2,1)S(1)} collective-permute-done((bf16[2,136,256]{2,1,0:T(8,128)(2,1)S(1)}, bf16[2,136,256]{2,1,0:T(8,128)(2,1)S(1)}, u32[]{:S(2)}, u32[]{:S(2)}) %collective-permute-start) | collective-permute-done | bytes 139296 | tf_op jit(solution)/shard_map/ppermute | solution.py:57
  9.3 1.5 %collective-permute-done.1 = bf16[2,136,256]{2,1,0:T(8,128)(2,1)S(1)} collective-permute-done((bf16[2,136,256]{2,1,0:T(8,128)(2,1)S(1)}, bf16[2,136,256]{2,1,0:T(8,128)(2,1)S(1)}, u32[]{:S(2)}, u32[]{:S(2)}) %collective-permute-start.1) | collective-permute-done | bytes 139296 | tf_op jit(solution)/shard_map/ppermute | solution.py:57
  10.7 0.4 collective-permute-start.2
  11.1 3.3 %collective-permute-start.3 = (bf16[2,136,256]{2,1,0:T(8,128)(2,1)S(1)}, bf16[2,136,256]{2,1,0:T(8,128)(2,1)S(1)}, u32[]{:S(2)}, u32[]{:S(2)}) collective-permute-start(bf16[2,136,256]{2,1,0:T(8,128)(2,1)S(1)} %collective-permute-done.refs_0_), channel_id=1, source_target_pairs={{0,96},{1,97},{2,98},{3,99},{4,100},{5,101},{6,102},{7,103},{8,104... | collective-permute-start | bytes 417800 | tf_op jit(solution)/shard_map/ppermute | solution.py:57
  14.4 5.1 %collective-permute-start.4 = (bf16[2,136,256]{2,1,0:T(8,128)(2,1)S(1)}, bf16[2,136,256]{2,1,0:T(8,128)(2,1)S(1)}, u32[]{:S(2)}, u32[]{:S(2)}) collective-permute-start(bf16[2,136,256]{2,1,0:T(8,128)(2,1)S(1)} %collective-permute-done.refs_0_), channel_id=1, source_target_pairs={{0,16},{1,17},{2,18},{3,19},{4,20},{5,21},{6,22},{7,23},{8,24},{9,... | collective-permute-start | bytes 417800 | tf_op jit(solution)/shard_map/ppermute | solution.py:57
  19.5 0.3 place.4.refs_3_
  19.9 0.0 collective-permute-done.2.refs_0_
  19.9 0.0 collective-permute-done.3.refs_1_
  20.0 2.6 %collective-permute-done.4.refs_2_ = bf16[2,136,256]{2,1,0:T(8,128)(2,1)S(1)} collective-permute-done((bf16[2,136,256]{2,1,0:T(8,128)(2,1)S(1)}, bf16[2,136,256]{2,1,0:T(8,128)(2,1)S(1)}, u32[]{:S(2)}, u32[]{:S(2)}) %collective-permute-start.4) | collective-permute-done | bytes 139296 | tf_op jit(solution)/shard_map/ppermute | solution.py:57
  22.6 0.1 pad_maximum_fusion
  22.7 0.1 collective-permute-start.7
  22.8 0.1 collective-permute-start.5
  22.9 3.2 %collective-permute-start.6 = (bf16[3,136,256]{2,1,0:T(8,128)(2,1)S(1)}, bf16[3,136,256]{2,1,0:T(8,128)(2,1)S(1)}, u32[]{:S(2)}, u32[]{:S(2)}) collective-permute-start(bf16[3,136,256]{2,1,0:T(8,128)(2,1)S(1)} %get-tuple-element.53), channel_id=1, source_target_pairs={{0,96},{1,97},{2,98},{3,99},{4,100},{5,101},{6,102},{7,103},{8,104... | collective-permute-start | bytes 626696 | tf_op jit(solution)/shard_map/ppermute | solution.py:57
  26.1 1.1 place.5.refs_3_
  27.2 4.5 %collective-permute-done.5.refs_0_ = bf16[3,136,256]{2,1,0:T(8,128)(2,1)S(1)} collective-permute-done((bf16[3,136,256]{2,1,0:T(8,128)(2,1)S(1)}, bf16[3,136,256]{2,1,0:T(8,128)(2,1)S(1)}, u32[]{:S(2)}, u32[]{:S(2)}) %collective-permute-start.5) | collective-permute-done | bytes 208928 | tf_op jit(solution)/shard_map/ppermute | solution.py:57
  31.7 0.0 collective-permute-done.6.refs_1_
  31.7 0.0 collective-permute-done.7.refs_2_
  31.7 0.1 collective-permute-start.10
  31.8 0.3 collective-permute-start.8
  32.1 3.0 %collective-permute-start.9 = (bf16[1,136,256]{2,1,0:T(8,128)(2,1)S(1)}, bf16[1,136,256]{2,1,0:T(8,128)(2,1)S(1)}, u32[]{:S(2)}, u32[]{:S(2)}) collective-permute-start(bf16[1,136,256]{2,1,0:T(8,128)(2,1)S(1)} %slice.15), channel_id=1, source_target_pairs={{0,96},{1,97},{2,98},{3,99},{4,100},{5,101},{6,102},{7,103},{8,104... | collective-permute-start | bytes 208904 | tf_op jit(solution)/shard_map/ppermute | solution.py:57
  35.1 2.5 %place.6 = (bf16[64,64,1024]{2,1,0:T(8,128)(2,1)S(1)}, bf16[32,64,1024]{2,1,0:T(8,128)(2,1)S(1)}) custom-call(bf16[3,136,256]{2,1,0:T(8,128)(2,1)S(1)} %collective-permute-done.5.refs_0_, bf16[3,136,256]{2,1,0:T(8,128)(2,1)S(1)} %collective-permute-done.6.refs_1_, ...), custom_call_target="tpu_custom_call", output_to_operand_aliasing={{0}: (3, {})} | custom-call | flops 1073741824 | bytes 8388608 | tf_op jit(solution)/shard_map/place/pallas_call | solution.py:236
  37.6 0.1 collective-permute-done.8.refs_0_
  37.7 0.0 collective-permute-done.9.refs_1_
  37.7 0.0 collective-permute-done.10.refs_2_
  37.7 0.0 copy-start
  37.7 0.1 collective-permute-start.11
  37.8 0.2 collective-permute-start.12
  38.0 3.5 %collective-permute-start.13 = (bf16[4,136,256]{2,1,0:T(8,128)(2,1)S(1)}, bf16[4,136,256]{2,1,0:T(8,128)(2,1)S(1)}, u32[]{:S(2)}, u32[]{:S(2)}) collective-permute-start(bf16[4,136,256]{2,1,0:T(8,128)(2,1)S(1)} %pad_maximum_fusion.2.r0), channel_id=1, source_target_pairs={{0,6},{1,7},{2,0},{3,1},{4,2},{5,3},{6,4},{7,5},{8,14},{9,15},{10,... | collective-permute-start | bytes 835592 | tf_op jit(solution)/shard_map/ppermute | solution.py:57
  41.5 1.4 %collective-permute-start.14 = (bf16[4,136,256]{2,1,0:T(8,128)(2,1)S(1)}, bf16[4,136,256]{2,1,0:T(8,128)(2,1)S(1)}, u32[]{:S(2)}, u32[]{:S(2)}) collective-permute-start(bf16[4,136,256]{2,1,0:T(8,128)(2,1)S(1)} %pad_maximum_fusion.2.r0), channel_id=1, source_target_pairs={{0,4},{1,5},{2,6},{3,7},{4,0},{5,1},{6,2},{7,3},{8,12},{9,13},{10,... | collective-permute-start | bytes 835592 | tf_op jit(solution)/shard_map/ppermute | solution.py:57
  42.8 1.3 %place.7.refs_1_ = bf16[64,64,1024]{2,1,0:T(8,128)(2,1)S(1)} custom-call(bf16[1,136,256]{2,1,0:T(8,128)(2,1)S(1)} %collective-permute-done.8.refs_0_, bf16[1,136,256]{2,1,0:T(8,128)(2,1)S(1)} %collective-permute-done.9.refs_1_, bf16[6,136,256]{2,1,0:T(8,128)(2,1)S(1)} %collective-permute-done.10.refs_2_, ...), custom_call_target="tpu_custom_call", output_to_operand_aliasing={{}: (3, {})} | custom-call | flops 1073741824 | bytes 8388608 | tf_op jit(solution)/shard_map/place/pallas_call | solution.py:236
  44.2 0.0 collective-permute-done.11.refs_0_
  44.2 0.0 copy-done
  44.2 16.6 %fine_product.1 = (bf16[2048,1024]{1,0:T(8,128)(2,1)S(1)}, bf16[2048,1024]{1,0:T(8,128)(2,1)S(1)}, bf16[64,64,1024]{2,1,0:T(8,128)(2,1)S(1)}) custom-call(s32[16,32]{1,0:T(8,128)S(1)} %bitcast.4, bf16[32,64,1024]{2,1,0:T(8,128)(2,1)S(1)} %get-tuple-element.43.a_ref, ...), custom_call_target="tpu_custom_call", output_to_operand_aliasing={{2}: (3, {})} | custom-call | flops 17179869184 | bytes 8388608 | tf_op jit(solution)/shard_map/fine_product/pallas_call | solution.py:252
  60.8 0.0 collective-permute-done.12.r1
  60.8 0.0 collective-permute-done.13.r2
  60.8 0.0 collective-permute-done.14.r3
  60.8 8.3 %other_half.1 = (bf16[2,512,2048]{2,1,0:T(8,128)(2,1)S(1)}, f32[64,64,128]{2,1,0:T(8,128)S(1)}) custom-call(bf16[2048,1024]{1,0:T(8,128)(2,1)S(1)} %get-tuple-element.48.hi, bf16[2048,1024]{1,0:T(8,128)(2,1)S(1)} %get-tuple-element.49.lo, bf16[4,136,256]{2,1,0:T(8,128)(2,1)S(1)} %pad_maximum_fusion.2.r0, ...), custom_call_target="tpu_custom_call" | custom-call | flops 8589934592 | bytes 8388608 | tf_op jit(solution)/shard_map/other_half/pallas_call | solution.py:265
  69.2 0.1 collective-permute-start.15
  69.3 5.1 %own_half.1.a_ref = f32[64,64,128]{2,1,0:T(8,128)S(1)} custom-call(bf16[2048,1024]{1,0:T(8,128)(2,1)S(1)} %get-tuple-element.48.hi, bf16[2048,1024]{1,0:T(8,128)(2,1)S(1)} %get-tuple-element.49.lo, bf16[2,512,2048]{2,1,0:T(8,128)(2,1)S(1)} %get-tuple-element.51.turned), custom_call_target="tpu_custom_call" | custom-call | flops 8589934592 | bytes 8388608 | tf_op jit(solution)/shard_map/own_half/pallas_call | solution.py:277
  74.4 0.0 collective-permute-done.15.b_ref
  74.4 2.5 %pack.1 = s16[64,72,128]{2,1,0:T(8,128)(2,1)S(1)} custom-call(f32[64,64,128]{2,1,0:T(8,128)S(1)} %own_half.1.a_ref, f32[64,64,128]{2,1,0:T(8,128)S(1)} %collective-permute-done.15.b_ref), custom_call_target="tpu_custom_call" | custom-call | tf_op jit(solution)/shard_map/pack/pallas_call | solution.py:376
  76.8 30.2 %all_to_all.5.in_ref = s16[64,72,128]{2,1,0:T(8,128)(2,1)S(1)} all-to-all(s16[64,72,128]{2,1,0:T(8,128)(2,1)S(1)} %pack.1), channel_id=1, replica_groups=mesh['x'=4,'yh'=2,'core'=2,'z'=4,'yl'=2] {'x','yh','z','yl'}, dimensions={0} | all-to-all | bytes 2359296 | tf_op jit(solution)/shard_map/all_to_all | solution.py:405
  107.1 1.0 unpack.1
  (8 shorter events, 0.1 us)
Async XLA Ops:
  1.5 7.7 %collective-permute-start = (bf16[2,136,256]{2,1,0:T(8,128)(2,1)S(1)}, bf16[2,136,256]{2,1,0:T(8,128)(2,1)S(1)}, u32[]{:S(2)}, u32[]{:S(2)}) collective-permute-start(bf16[2,136,256]{2,1,0:T(8,128)(2,1)S(1)} %stamp.1), channel_id=1, source_target_pairs={{0,64},{1,80},{2,32},{3,48},{4,0},{5,16},{6,96},{7,112},{8,72},{9,... | collective-permute-start | bytes 417800 | tf_op jit(solution)/shard_map/ppermute | solution.py:57
  4.7 6.0 %collective-permute-start.1 = (bf16[2,136,256]{2,1,0:T(8,128)(2,1)S(1)}, bf16[2,136,256]{2,1,0:T(8,128)(2,1)S(1)}, u32[]{:S(2)}, u32[]{:S(2)}) collective-permute-start(bf16[2,136,256]{2,1,0:T(8,128)(2,1)S(1)} %stamp.1), channel_id=1, source_target_pairs={{0,1},{1,0},{2,3},{3,2},{4,5},{5,4},{6,7},{7,6},{8,9},{9,8},{10,11... | collective-permute-start | bytes 417800 | tf_op jit(solution)/shard_map/ppermute | solution.py:57
  10.7 9.2 %collective-permute-start.2 = (bf16[2,136,256]{2,1,0:T(8,128)(2,1)S(1)}, bf16[2,136,256]{2,1,0:T(8,128)(2,1)S(1)}, u32[]{:S(2)}, u32[]{:S(2)}) collective-permute-start(bf16[2,136,256]{2,1,0:T(8,128)(2,1)S(1)} %collective-permute-done.refs_0_), channel_id=1, source_target_pairs={{0,32},{1,33},{2,34},{3,35},{4,36},{5,37},{6,38},{7,39},{8,40},{9,... | collective-permute-start | bytes 417800 | tf_op jit(solution)/shard_map/ppermute | solution.py:57
  11.1 8.9 %collective-permute-start.3 = (bf16[2,136,256]{2,1,0:T(8,128)(2,1)S(1)}, bf16[2,136,256]{2,1,0:T(8,128)(2,1)S(1)}, u32[]{:S(2)}, u32[]{:S(2)}) collective-permute-start(bf16[2,136,256]{2,1,0:T(8,128)(2,1)S(1)} %collective-permute-done.refs_0_), channel_id=1, source_target_pairs={{0,96},{1,97},{2,98},{3,99},{4,100},{5,101},{6,102},{7,103},{8,104... | collective-permute-start | bytes 417800 | tf_op jit(solution)/shard_map/ppermute | solution.py:57
  14.4 8.2 %collective-permute-start.4 = (bf16[2,136,256]{2,1,0:T(8,128)(2,1)S(1)}, bf16[2,136,256]{2,1,0:T(8,128)(2,1)S(1)}, u32[]{:S(2)}, u32[]{:S(2)}) collective-permute-start(bf16[2,136,256]{2,1,0:T(8,128)(2,1)S(1)} %collective-permute-done.refs_0_), channel_id=1, source_target_pairs={{0,16},{1,17},{2,18},{3,19},{4,20},{5,21},{6,22},{7,23},{8,24},{9,... | collective-permute-start | bytes 417800 | tf_op jit(solution)/shard_map/ppermute | solution.py:57
  22.7 9.0 %collective-permute-start.7 = (bf16[8,136,256]{2,1,0:T(8,128)(2,1)S(1)}, bf16[8,136,256]{2,1,0:T(8,128)(2,1)S(1)}, u32[]{:S(2)}, u32[]{:S(2)}) collective-permute-start(bf16[8,136,256]{2,1,0:T(8,128)(2,1)S(1)} %pad_maximum_fusion), channel_id=1, source_target_pairs={{0,8},{1,9},{2,10},{3,11},{4,12},{5,13},{6,14},{7,15},{8,0},{9,1},... | collective-permute-start | bytes 1671176 | tf_op jit(solution)/shard_map/ppermute | solution.py:57
  22.8 8.8 %collective-permute-start.5 = (bf16[3,136,256]{2,1,0:T(8,128)(2,1)S(1)}, bf16[3,136,256]{2,1,0:T(8,128)(2,1)S(1)}, u32[]{:S(2)}, u32[]{:S(2)}) collective-permute-start(bf16[3,136,256]{2,1,0:T(8,128)(2,1)S(1)} %get-tuple-element.54), channel_id=1, source_target_pairs={{0,32},{1,33},{2,34},{3,35},{4,36},{5,37},{6,38},{7,39},{8,40},{9,... | collective-permute-start | bytes 626696 | tf_op jit(solution)/shard_map/ppermute | solution.py:57
  22.9 8.8 %collective-permute-start.6 = (bf16[3,136,256]{2,1,0:T(8,128)(2,1)S(1)}, bf16[3,136,256]{2,1,0:T(8,128)(2,1)S(1)}, u32[]{:S(2)}, u32[]{:S(2)}) collective-permute-start(bf16[3,136,256]{2,1,0:T(8,128)(2,1)S(1)} %get-tuple-element.53), channel_id=1, source_target_pairs={{0,96},{1,97},{2,98},{3,99},{4,100},{5,101},{6,102},{7,103},{8,104... | collective-permute-start | bytes 626696 | tf_op jit(solution)/shard_map/ppermute | solution.py:57
  31.7 6.0 %collective-permute-start.10 = (bf16[6,136,256]{2,1,0:T(8,128)(2,1)S(1)}, bf16[6,136,256]{2,1,0:T(8,128)(2,1)S(1)}, u32[]{:S(2)}, u32[]{:S(2)}) collective-permute-start(bf16[6,136,256]{2,1,0:T(8,128)(2,1)S(1)} %pad_maximum_fusion.1), channel_id=1, source_target_pairs={{0,8},{1,9},{2,10},{3,11},{4,12},{5,13},{6,14},{7,15},{8,0},{9,1},... | collective-permute-start | bytes 1253384 | tf_op jit(solution)/shard_map/ppermute | solution.py:57
  31.8 5.8 %collective-permute-start.8 = (bf16[1,136,256]{2,1,0:T(8,128)(2,1)S(1)}, bf16[1,136,256]{2,1,0:T(8,128)(2,1)S(1)}, u32[]{:S(2)}, u32[]{:S(2)}) collective-permute-start(bf16[1,136,256]{2,1,0:T(8,128)(2,1)S(1)} %slice.14), channel_id=1, source_target_pairs={{0,32},{1,33},{2,34},{3,35},{4,36},{5,37},{6,38},{7,39},{8,40},{9,... | collective-permute-start | bytes 208904 | tf_op jit(solution)/shard_map/ppermute | solution.py:57
  32.1 5.6 %collective-permute-start.9 = (bf16[1,136,256]{2,1,0:T(8,128)(2,1)S(1)}, bf16[1,136,256]{2,1,0:T(8,128)(2,1)S(1)}, u32[]{:S(2)}, u32[]{:S(2)}) collective-permute-start(bf16[1,136,256]{2,1,0:T(8,128)(2,1)S(1)} %slice.15), channel_id=1, source_target_pairs={{0,96},{1,97},{2,98},{3,99},{4,100},{5,101},{6,102},{7,103},{8,104... | collective-permute-start | bytes 208904 | tf_op jit(solution)/shard_map/ppermute | solution.py:57
  37.7 6.5 %copy-start = (s32[32,1,16]{0,2,1:T(8,128)S(1)}, s32[32,1,16]{0,2,1:T(8,128)}, u32[]{:S(2)}) copy-start(s32[32,1,16]{0,2,1:T(8,128)} %param.5) | copy-start | bytes 6148
  37.7 6.4 %collective-permute-start.11 = (bf16[2,136,256]{2,1,0:T(8,128)(2,1)S(1)}, bf16[2,136,256]{2,1,0:T(8,128)(2,1)S(1)}, u32[]{:S(2)}, u32[]{:S(2)}) collective-permute-start(bf16[2,136,256]{2,1,0:T(8,128)(2,1)S(1)} %pad_maximum_fusion.5), channel_id=1, source_target_pairs={{0,8},{1,9},{2,10},{3,11},{4,12},{5,13},{6,14},{7,15},{8,0},{9,1},... | collective-permute-start | bytes 417800 | tf_op jit(solution)/shard_map/ppermute | solution.py:57
  37.8 23.0 %collective-permute-start.12 = (bf16[4,136,256]{2,1,0:T(8,128)(2,1)S(1)}, bf16[4,136,256]{2,1,0:T(8,128)(2,1)S(1)}, u32[]{:S(2)}, u32[]{:S(2)}) collective-permute-start(bf16[4,136,256]{2,1,0:T(8,128)(2,1)S(1)} %pad_maximum_fusion.2.r0), channel_id=1, source_target_pairs={{0,2},{1,3},{2,4},{3,5},{4,6},{5,7},{6,0},{7,1},{8,10},{9,11},{10,... | collective-permute-start | bytes 835592 | tf_op jit(solution)/shard_map/ppermute | solution.py:57
  38.0 22.8 %collective-permute-start.13 = (bf16[4,136,256]{2,1,0:T(8,128)(2,1)S(1)}, bf16[4,136,256]{2,1,0:T(8,128)(2,1)S(1)}, u32[]{:S(2)}, u32[]{:S(2)}) collective-permute-start(bf16[4,136,256]{2,1,0:T(8,128)(2,1)S(1)} %pad_maximum_fusion.2.r0), channel_id=1, source_target_pairs={{0,6},{1,7},{2,0},{3,1},{4,2},{5,3},{6,4},{7,5},{8,14},{9,15},{10,... | collective-permute-start | bytes 835592 | tf_op jit(solution)/shard_map/ppermute | solution.py:57
  41.5 19.4 %collective-permute-start.14 = (bf16[4,136,256]{2,1,0:T(8,128)(2,1)S(1)}, bf16[4,136,256]{2,1,0:T(8,128)(2,1)S(1)}, u32[]{:S(2)}, u32[]{:S(2)}) collective-permute-start(bf16[4,136,256]{2,1,0:T(8,128)(2,1)S(1)} %pad_maximum_fusion.2.r0), channel_id=1, source_target_pairs={{0,4},{1,5},{2,6},{3,7},{4,0},{5,1},{6,2},{7,3},{8,12},{9,13},{10,... | collective-permute-start | bytes 835592 | tf_op jit(solution)/shard_map/ppermute | solution.py:57
  69.2 5.2 %collective-permute-start.15 = (f32[64,64,128]{2,1,0:T(8,128)S(1)}, f32[64,64,128]{2,1,0:T(8,128)S(1)}, u32[]{:S(2)}, u32[]{:S(2)}) collective-permute-start(f32[64,64,128]{2,1,0:T(8,128)S(1)} %get-tuple-element.52), channel_id=1, source_target_pairs={{0,8},{1,9},{2,10},{3,11},{4,12},{5,13},{6,14},{7,15},{8,0},{9,1},... | collective-permute-start | bytes 6291464 | tf_op jit(solution)/shard_map/ppermute | solution.py:57

commit v7 on v6

--- a/solution.py
+++ b/solution.py
@@ -7,6 +7,7 @@
 from jax.experimental.pallas import tpu as pltpu
 from jax.sharding import Mesh
 from jax.sharding import PartitionSpec as P
+
 
 AXES = ("x", "yh", "core", "z", "yl")
 SIZES = (4, 2, 2, 4, 2)
@@ -75,6 +76,11 @@
 
 def swap_halves(v):
     return jnp.concatenate([v[:, BS:], v[:, :BS]], axis=1)
+
+
+def meet(first, free, last):
+    fixed = together(*first, *last)
+    return fixed[: len(first)] + free + fixed[len(first) :]
 
 
 def spread(tile, ids, store):
@@ -185,16 +191,22 @@
                 out_ref[8 * q + 2 * n + j] = c[BS * q : BS * (q + 1), 128 * j : 128 * (j + 1)]
 
 
-def other_half(hi, lo, r0, r1, r2, r3, turned, out_ref):
+def turn_line(ref, side, turned):
     core, z, yl = (position(name) for name in ("core", "z", "yl"))
-    for ref, step in ((r0, 0), (r1, -1), (r2, 1), (r3, 2)):
-        for side in range(2):
-            at = 256 * (2 * jnp.bitwise_and(z + step + 4, 3) + flip(yl, side))
-
-            @pl.loop(0, 2)
-            def _(h):
-                turn(ref, 2 * side + h, turned, core, at + 128 * h)
-
+    for ring, step in enumerate((0, -1, 1, 2)):
+        at = 256 * (2 * jnp.bitwise_and(z + step + 4, 3) + flip(yl, side))
+
+        @pl.loop(0, 2)
+        def _(h):
+            turn(ref, 2 * ring + h, turned, core, at + 128 * h)
+
+
+def turn_own(line, turned):
+    turn_line(line, 0, turned)
+
+
+def other_half(hi, lo, beside, turned_in, turned, out_ref):
+    turn_line(beside, 1, turned)
     half_product(turned, 1, hi, lo, out_ref)
 
 
@@ -233,7 +245,7 @@
             place_all(what, *refs[: len(what)], refs[count + 1])
             fetch.wait()
 
-    out = pl.pallas_call(
+    call = pl.pallas_call(
         body,
         out_shape=(DENSE,) + tuple(pltpu.VMEM(v.shape, v.dtype) for v in fetched),
         in_specs=[VMEM] * count + [HBM] * len(fetched),
@@ -242,8 +254,8 @@
         input_output_aliases={len(arrays): 0} if given else {},
         compiler_params=pltpu.CompilerParams(vmem_limit_bytes=16 << 20),
         cost_estimate=cost(1 << 30),
-        name="place",
-    )(*arrays, *given, *fetched)
+    )
+    out = call(*arrays, *given, *fetched)
     return out if fetched else out[0]
 
 
@@ -261,16 +273,29 @@
     )(cols, a, *arrays, dense)
 
 
-def run_other_half(hi, lo, pr):
+def run_turn(line):
+    return pl.pallas_call(
+        turn_own,
+        out_shape=pltpu.VMEM((2, 512, 2048), BF16),
+        in_specs=[VMEM],
+        out_specs=VMEM,
+        compiler_params=pltpu.CompilerParams(vmem_limit_bytes=8 << 20),
+        cost_estimate=cost(1 << 30),
+        name="turn",
+    )(line)
+
+
+def run_other_half(hi, lo, beside, turned):
     return pl.pallas_call(
         other_half,
-        out_shape=(pltpu.VMEM((2, 512, hi.shape[0]), BF16), HALF),
-        in_specs=[VMEM] * 6,
+        out_shape=(pltpu.VMEM(turned.shape, BF16), HALF),
+        in_specs=[VMEM] * 4,
         out_specs=(VMEM, VMEM),
-        compiler_params=pltpu.CompilerParams(vmem_limit_bytes=28 << 20),
+        input_output_aliases={3: 0},
+        compiler_params=pltpu.CompilerParams(vmem_limit_bytes=16 << 20),
         cost_estimate=cost(1 << 33),
         name="other_half",
-    )(hi, lo, *pr)
+    )(hi, lo, beside, turned)
 
 
 def run_own_half(hi, lo, turned):
@@ -279,7 +304,7 @@
         out_shape=HALF,
         in_specs=[VMEM] * 3,
         out_specs=VMEM,
-        compiler_params=pltpu.CompilerParams(vmem_limit_bytes=28 << 20),
+        compiler_params=pltpu.CompilerParams(vmem_limit_bytes=16 << 20),
         cost_estimate=cost(1 << 33),
         name="own_half",
     )(hi, lo, turned)
@@ -318,37 +343,36 @@
 
 
 def fetch_and_multiply(piece, cols, a):
-    near, beside = together(send(piece, REFLECT), send(piece, BESIDE))
-    b1, a1, f, r0, dense = together(
-        send(near, NEXT_X),
-        send(near, LAST_X),
-        send(near, ACROSS_Y),
-        jnp.concatenate([piece, beside]),
-        run_place(((NEAR, False),), (near,), None),
+    (near,) = together(send(piece, REFLECT))
+    b1, a1, f, z1, z2, z3, dense = meet(
+        (send(near, NEXT_X), send(near, LAST_X), send(near, ACROSS_Y)),
+        (send(piece, NEXT_Z), send(piece, LAST_Z), send(piece, ACROSS_Z)),
+        (run_place(((NEAR, False),), (near,), None),),
     )
     what = ((BEHIND, False), (AHEAD, False), (ACROSS, False))
-    b2, a2, e1, r0, dense = together(
+    line = jnp.concatenate([piece, z1, z2, z3])
+    b2, a2, e1, line, dense, turned = together(
         send(jnp.concatenate([f, b1[:1]]), NEXT_X),
         send(jnp.concatenate([f, a1[1:]]), LAST_X),
         send(jnp.concatenate([near, b1, a1, f]), OTHER_CORE),
-        r0,
+        line,
         run_place(what, (b1, a1, f), dense),
+        run_turn(line),
     )
     what = ((BEHIND2, False), (AHEAD2, False), (NEAR + BEHIND + AHEAD + ACROSS, True))
-    b3, a3, e2, r0, (dense, a) = together(
+    beside = send(line, BESIDE)
+    b3, a3, e2, (dense, a) = together(
         send(b2[:1], NEXT_X),
         send(a2[1:2], LAST_X),
         send(jnp.concatenate([b2, a2]), OTHER_CORE),
-        r0,
         run_place(what, (b2, a2, e1), dense, a),
     )
     e3 = send(jnp.concatenate([b3, a3]), OTHER_CORE)
-    r1, r2, r3 = send(r0, NEXT_Z), send(r0, LAST_Z), send(r0, ACROSS_Z)
     what = ((BEHIND3, False), (AHEAD3, False), (BEHIND2 + AHEAD2, True))
     dense = run_place(what, (b3, a3, e2), dense)
     what = ((BEHIND3 + AHEAD3, True),)
     hi, lo, dense = run_fine_product(what, cols, a, (e3,), dense)
-    return hi, lo, (r0, r1, r2, r3)
+    return hi, lo, turned, beside
 
 
 def pack(a_ref, b_ref, out_ref):
@@ -397,8 +421,8 @@
 def shards(a_vals, a_cols, p_vals, p_cols):
     a = in_hbm(a_vals[:, 0])
     piece = run_stamp(p_cols, p_vals)
-    hi, lo, pr = fetch_and_multiply(piece, a_cols[:, 0].T, a)
-    turned, other = run_other_half(hi, lo, pr)
+    hi, lo, turned, beside = fetch_and_multiply(piece, a_cols[:, 0].T, a)
+    turned, other = run_other_half(hi, lo, beside, turned)
     met = send(other, OTHER_CORE)
     own = run_own_half(hi, lo, turned)
     packed = packed_sum(own, met)

time: 108 us -> 109 us (level)
  waiting for transfers between devices: 10.6 us -> 20 us
  starting transfers between devices: 26.6 us -> 20.8 us
  blocking collectives: 30.2 us -> 27.7 us
    ppermute x16, waiting for transfers between devices: 10.6 us -> 20 us  [send(): return lax.ppermute(value, AXES, pairs)]
    ppermute x16, starting transfers between devices: 26.6 us -> 20.8 us  [send(): return lax.ppermute(value, AXES, pairs)]
    all_to_all x1, blocking collectives: 30.2 us -> 27.7 us  [shards(): mixed = lax.all_to_all(packed, ('x', 'yh', 'z', 'yl'), 0, 0, tiled=True)]
    pallas_call x5 -> x6, Pallas kernels: 13.5 us -> 13.5 us  [the longest x1 6.71 us: run_other_half(): pl.pallas_call(other_half, out_shape=(pltpu.VMEM(turned.shape, BF16), HAL...]
  transfers between devices with their start and end apart: 16 -> 16, of which waited for: 5 -> 8; matrix products, arithmetic and copies ran while one was open for 0% -> 0% of each run, Pallas kernels for 25% -> 26%
where the time goes in v7:
time: 109 us
  Pallas kernels  40.2 us (37%)
  blocking collectives  27.7 us (25%)
  starting transfers between devices  20.8 us (19%)
  waiting for transfers between devices  20 us (18%)
    all_to_all x1, blocking collectives, shards(): mixed = lax.all_to_all(packed, ('x', 'yh', 'z', 'yl'), 0, 0, tiled=True)  27.7 us
    ppermute x16, starting transfers between devices, send(): return lax.ppermute(value, AXES, pairs)  20.8 us
    ppermute x16, waiting for transfers between devices, send(): return lax.ppermute(value, AXES, pairs)  20 us
    pallas_call x1, Pallas kernels, run_fine_product(): pl.pallas_call(functools.partial(fine_product, what), out_shape=(pltpu.VM...  16.6 us
    pallas_call x1, Pallas kernels, run_other_half(): pl.pallas_call(other_half, out_shape=(pltpu.VMEM(turned.shape, BF16), HAL...  6.71 us
    pallas_call x4, Pallas kernels, run_place(): out = call(*arrays, *given, *fetched)  5.2 us
    pallas_call x1, Pallas kernels, run_own_half(): pl.pallas_call(own_half, out_shape=HALF, in_specs=[VMEM] * 3, out_specs=V...  5.1 us
    pallas_call x1, Pallas kernels, packed_sum(): pl.pallas_call(pack, out_shape=jax.ShapeDtypeStruct((64, ROWS, 128), jnp....  2.46 us
  transfers between devices with their start and end apart: 16, of which 8 were waited for; matrix products, arithmetic and copies ran while one was open for 0% of the time, Pallas kernels for 26%

profile of v7, /device:TPU:0, one launch (start us, length us, event | category | flops | bytes accessed | tf_op | source)
XLA Modules:
  0.0 109.2 jit_solution(11556550240202525543)
XLA Ops:
  0.0 1.5 %stamp.1 = bf16[2,136,256]{2,1,0:T(8,128)(2,1)S(1)} custom-call(s32[4,4]{1,0:T(4,128)} %cols_ref.1, bf16[4,64,256]{2,1,0:T(8,128)(2,1)} %vals_ref.1), custom_call_target="tpu_custom_call" | custom-call | tf_op jit(solution)/shard_map/stamp/pallas_call | solution.py:334
  1.5 3.2 %collective-permute-start = (bf16[2,136,256]{2,1,0:T(8,128)(2,1)S(1)}, bf16[2,136,256]{2,1,0:T(8,128)(2,1)S(1)}, u32[]{:S(2)}, u32[]{:S(2)}) collective-permute-start(bf16[2,136,256]{2,1,0:T(8,128)(2,1)S(1)} %stamp.1), channel_id=1, source_target_pairs={{0,64},{1,80},{2,32},{3,48},{4,0},{5,16},{6,96},{7,112},{8,72},{9,... | collective-permute-start | bytes 417800 | tf_op jit(solution)/shard_map/ppermute | solution.py:58
  4.7 4.5 %collective-permute-done.refs_0_ = bf16[2,136,256]{2,1,0:T(8,128)(2,1)S(1)} collective-permute-done((bf16[2,136,256]{2,1,0:T(8,128)(2,1)S(1)}, bf16[2,136,256]{2,1,0:T(8,128)(2,1)S(1)}, u32[]{:S(2)}, u32[]{:S(2)}) %collective-permute-start) | collective-permute-done | bytes 139296 | tf_op jit(solution)/shard_map/ppermute | solution.py:58
  9.3 3.5 %collective-permute-start.3 = (bf16[2,136,256]{2,1,0:T(8,128)(2,1)S(1)}, bf16[2,136,256]{2,1,0:T(8,128)(2,1)S(1)}, u32[]{:S(2)}, u32[]{:S(2)}) collective-permute-start(bf16[2,136,256]{2,1,0:T(8,128)(2,1)S(1)} %collective-permute-done.refs_0_), channel_id=1, source_target_pairs={{0,16},{1,17},{2,18},{3,19},{4,20},{5,21},{6,22},{7,23},{8,24},{9,... | collective-permute-start | bytes 417800 | tf_op jit(solution)/shard_map/ppermute | solution.py:58
  12.7 6.8 %collective-permute-start.2 = (bf16[2,136,256]{2,1,0:T(8,128)(2,1)S(1)}, bf16[2,136,256]{2,1,0:T(8,128)(2,1)S(1)}, u32[]{:S(2)}, u32[]{:S(2)}) collective-permute-start(bf16[2,136,256]{2,1,0:T(8,128)(2,1)S(1)} %collective-permute-done.refs_0_), channel_id=1, source_target_pairs={{0,96},{1,97},{2,98},{3,99},{4,100},{5,101},{6,102},{7,103},{8,104... | collective-permute-start | bytes 417800 | tf_op jit(solution)/shard_map/ppermute | solution.py:58
  19.5 0.0 collective-permute-start.1
  19.5 0.3 shard_map.46.refs_3_
  19.9 0.0 collective-permute-done.3.refs_2_
  19.9 2.2 %collective-permute-done.2.refs_1_ = bf16[2,136,256]{2,1,0:T(8,128)(2,1)S(1)} collective-permute-done((bf16[2,136,256]{2,1,0:T(8,128)(2,1)S(1)}, bf16[2,136,256]{2,1,0:T(8,128)(2,1)S(1)}, u32[]{:S(2)}, u32[]{:S(2)}) %collective-permute-start.2) | collective-permute-done | bytes 139296 | tf_op jit(solution)/shard_map/ppermute | solution.py:58
  22.1 3.7 %collective-permute-done.1.refs_0_ = bf16[2,136,256]{2,1,0:T(8,128)(2,1)S(1)} collective-permute-done((bf16[2,136,256]{2,1,0:T(8,128)(2,1)S(1)}, bf16[2,136,256]{2,1,0:T(8,128)(2,1)S(1)}, u32[]{:S(2)}, u32[]{:S(2)}) %collective-permute-start.1) | collective-permute-done | bytes 139296 | tf_op jit(solution)/shard_map/ppermute | solution.py:58
  25.8 0.1 pad_maximum_fusion
  25.9 0.1 collective-permute-start.6
  26.0 2.3 %collective-permute-start.9 = (bf16[2,136,256]{2,1,0:T(8,128)(2,1)S(1)}, bf16[2,136,256]{2,1,0:T(8,128)(2,1)S(1)}, u32[]{:S(2)}, u32[]{:S(2)}) collective-permute-start(bf16[2,136,256]{2,1,0:T(8,128)(2,1)S(1)} %stamp.1), channel_id=1, source_target_pairs={{0,4},{1,5},{2,6},{3,7},{4,0},{5,1},{6,2},{7,3},{8,12},{9,13},{10,... | collective-permute-start | bytes 417800 | tf_op jit(solution)/shard_map/ppermute | solution.py:58
  28.3 0.8 collective-permute-start.8
  29.1 1.2 %collective-permute-start.7 = (bf16[2,136,256]{2,1,0:T(8,128)(2,1)S(1)}, bf16[2,136,256]{2,1,0:T(8,128)(2,1)S(1)}, u32[]{:S(2)}, u32[]{:S(2)}) collective-permute-start(bf16[2,136,256]{2,1,0:T(8,128)(2,1)S(1)} %stamp.1), channel_id=1, source_target_pairs={{0,2},{1,3},{2,4},{3,5},{4,6},{5,7},{6,0},{7,1},{8,10},{9,11},{10,... | collective-permute-start | bytes 417800 | tf_op jit(solution)/shard_map/ppermute | solution.py:58
  30.3 0.1 collective-permute-start.5
  30.4 3.7 %collective-permute-done.9 = bf16[2,136,256]{2,1,0:T(8,128)(2,1)S(1)} collective-permute-done((bf16[2,136,256]{2,1,0:T(8,128)(2,1)S(1)}, bf16[2,136,256]{2,1,0:T(8,128)(2,1)S(1)}, u32[]{:S(2)}, u32[]{:S(2)}) %collective-permute-start.9) | collective-permute-done | bytes 139296 | tf_op jit(solution)/shard_map/ppermute | solution.py:58
  34.1 0.0 collective-permute-start.4
  34.1 2.8 %collective-permute-done.8 = bf16[2,136,256]{2,1,0:T(8,128)(2,1)S(1)} collective-permute-done((bf16[2,136,256]{2,1,0:T(8,128)(2,1)S(1)}, bf16[2,136,256]{2,1,0:T(8,128)(2,1)S(1)}, u32[]{:S(2)}, u32[]{:S(2)}) %collective-permute-start.8) | collective-permute-done | bytes 139296 | tf_op jit(solution)/shard_map/ppermute | solution.py:58
  36.9 0.0 collective-permute-done.7
  36.9 0.1 pad_maximum_fusion.1.line
  36.9 1.6 %turn.1.turned_in = bf16[2,512,2048]{2,1,0:T(8,128)(2,1)S(1)} custom-call(bf16[8,136,256]{2,1,0:T(8,128)(2,1)S(1)} %pad_maximum_fusion.1.line), custom_call_target="tpu_custom_call" | custom-call | flops 1073741824 | bytes 8388608 | tf_op jit(solution)/shard_map/turn/pallas_call | solution.py:277
  38.6 1.1 shard_map.47.refs_3_
  39.6 0.0 collective-permute-done.5.refs_1_
  39.7 1.7 %collective-permute-done.4.refs_0_ = bf16[3,136,256]{2,1,0:T(8,128)(2,1)S(1)} collective-permute-done((bf16[3,136,256]{2,1,0:T(8,128)(2,1)S(1)}, bf16[3,136,256]{2,1,0:T(8,128)(2,1)S(1)}, u32[]{:S(2)}, u32[]{:S(2)}) %collective-permute-start.4) | collective-permute-done | bytes 208928 | tf_op jit(solution)/shard_map/ppermute | solution.py:58
  41.4 0.0 collective-permute-done.6.refs_2_
  41.4 0.1 collective-permute-start.12
  41.6 0.1 collective-permute-start.11
  41.6 2.0 %collective-permute-start.10 = (bf16[1,136,256]{2,1,0:T(8,128)(2,1)S(1)}, bf16[1,136,256]{2,1,0:T(8,128)(2,1)S(1)}, u32[]{:S(2)}, u32[]{:S(2)}) collective-permute-start(bf16[1,136,256]{2,1,0:T(8,128)(2,1)S(1)} %slice.14), channel_id=1, source_target_pairs={{0,32},{1,33},{2,34},{3,35},{4,36},{5,37},{6,38},{7,39},{8,40},{9,... | collective-permute-start | bytes 208904 | tf_op jit(solution)/shard_map/ppermute | solution.py:58
  43.7 2.5 %shard_map.48 = (bf16[64,64,1024]{2,1,0:T(8,128)(2,1)S(1)}, bf16[32,64,1024]{2,1,0:T(8,128)(2,1)S(1)}) custom-call(bf16[3,136,256]{2,1,0:T(8,128)(2,1)S(1)} %collective-permute-done.4.refs_0_, bf16[3,136,256]{2,1,0:T(8,128)(2,1)S(1)} %collective-permute-done.5.refs_1_, ...), custom_call_target="tpu_custom_call", output_to_operand_aliasing={{0}: (3, {})} | custom-call | flops 1073741824 | bytes 8388608 | tf_op jit(solution)/shard_map/pallas_call | solution.py:258
  46.1 0.1 collective-permute-done.11.refs_1_
  46.2 1.3 %collective-permute-done.10.refs_0_ = bf16[1,136,256]{2,1,0:T(8,128)(2,1)S(1)} collective-permute-done((bf16[1,136,256]{2,1,0:T(8,128)(2,1)S(1)}, bf16[1,136,256]{2,1,0:T(8,128)(2,1)S(1)}, u32[]{:S(2)}, u32[]{:S(2)}) %collective-permute-start.10) | collective-permute-done | bytes 69664 | tf_op jit(solution)/shard_map/ppermute | solution.py:58
  47.5 0.0 collective-permute-done.12.refs_2_
  47.5 0.0 copy-start
  47.5 0.1 collective-permute-start.13
  47.6 0.1 collective-permute-start.14
  47.7 1.3 %shard_map.49.refs_1_ = bf16[64,64,1024]{2,1,0:T(8,128)(2,1)S(1)} custom-call(bf16[1,136,256]{2,1,0:T(8,128)(2,1)S(1)} %collective-permute-done.10.refs_0_, bf16[1,136,256]{2,1,0:T(8,128)(2,1)S(1)} %collective-permute-done.11.refs_1_, bf16[6,136,256]{2,1,0:T(8,128)(2,1)S(1)} %collective-permute-done.12.refs_2_, ...), custom_call_target="tpu_custom_call", output_to_operand_aliasing={{}: (3, {})} | custom-call | flops 1073741824 | bytes 8388608 | tf_op jit(solution)/shard_map/pallas_call | solution.py:258
  49.0 0.0 collective-permute-done.13.refs_0_
  49.0 0.0 copy-done
  49.1 16.6 %fine_product.1 = (bf16[2048,1024]{1,0:T(8,128)(2,1)S(1)}, bf16[2048,1024]{1,0:T(8,128)(2,1)S(1)}, bf16[64,64,1024]{2,1,0:T(8,128)(2,1)S(1)}) custom-call(s32[16,32]{1,0:T(8,128)S(1)} %bitcast.4, bf16[32,64,1024]{2,1,0:T(8,128)(2,1)S(1)} %get-tuple-element.36.a_ref, ...), custom_call_target="tpu_custom_call", output_to_operand_aliasing={{2}: (3, {})} | custom-call | flops 17179869184 | bytes 8388608 | tf_op jit(solution)/shard_map/fine_product/pallas_call | solution.py:264
  65.7 0.0 collective-permute-done.14.beside
  65.7 6.7 %other_half.1 = (bf16[2,512,2048]{2,1,0:T(8,128)(2,1)S(1)}, f32[64,64,128]{2,1,0:T(8,128)S(1)}) custom-call(bf16[2048,1024]{1,0:T(8,128)(2,1)S(1)} %get-tuple-element.41.hi, bf16[2048,1024]{1,0:T(8,128)(2,1)S(1)} %get-tuple-element.42.lo, bf16[8,136,256]{2,1,0:T(8,128)(2,1)S(1)} %collective-permute-done.14.beside, ...), custom_call_target="tpu_custom_call", output_to_operand_aliasing={{0}: (3, {})} | custom-call | flops 8589934592 | bytes 8388608 | tf_op jit(solution)/shard_map/other_half/pallas_call | solution.py:289
  72.4 0.5 collective-permute-start.15
  72.9 5.1 %own_half.1.a_ref = f32[64,64,128]{2,1,0:T(8,128)S(1)} custom-call(bf16[2048,1024]{1,0:T(8,128)(2,1)S(1)} %get-tuple-element.41.hi, bf16[2048,1024]{1,0:T(8,128)(2,1)S(1)} %get-tuple-element.42.lo, bf16[2,512,2048]{2,1,0:T(8,128)(2,1)S(1)} %get-tuple-element.45.turned), custom_call_target="tpu_custom_call" | custom-call | flops 8589934592 | bytes 8388608 | tf_op jit(solution)/shard_map/own_half/pallas_call | solution.py:302
  78.0 0.0 collective-permute-done.15.b_ref
  78.0 2.5 %pack.1 = s16[64,72,128]{2,1,0:T(8,128)(2,1)S(1)} custom-call(f32[64,64,128]{2,1,0:T(8,128)S(1)} %own_half.1.a_ref, f32[64,64,128]{2,1,0:T(8,128)S(1)} %collective-permute-done.15.b_ref), custom_call_target="tpu_custom_call" | custom-call | tf_op jit(solution)/shard_map/pack/pallas_call | solution.py:400
  80.5 27.7 %all_to_all.5.in_ref = s16[64,72,128]{2,1,0:T(8,128)(2,1)S(1)} all-to-all(s16[64,72,128]{2,1,0:T(8,128)(2,1)S(1)} %pack.1), channel_id=1, replica_groups=mesh['x'=4,'yh'=2,'core'=2,'z'=4,'yl'=2] {'x','yh','z','yl'}, dimensions={0} | all-to-all | bytes 2359296 | tf_op jit(solution)/shard_map/all_to_all | solution.py:429
  108.2 1.0 unpack.1
  (7 shorter events, 0.1 us)
Async XLA Ops:
  1.5 7.7 %collective-permute-start = (bf16[2,136,256]{2,1,0:T(8,128)(2,1)S(1)}, bf16[2,136,256]{2,1,0:T(8,128)(2,1)S(1)}, u32[]{:S(2)}, u32[]{:S(2)}) collective-permute-start(bf16[2,136,256]{2,1,0:T(8,128)(2,1)S(1)} %stamp.1), channel_id=1, source_target_pairs={{0,64},{1,80},{2,32},{3,48},{4,0},{5,16},{6,96},{7,112},{8,72},{9,... | collective-permute-start | bytes 417800 | tf_op jit(solution)/shard_map/ppermute | solution.py:58
  9.3 10.6 %collective-permute-start.3 = (bf16[2,136,256]{2,1,0:T(8,128)(2,1)S(1)}, bf16[2,136,256]{2,1,0:T(8,128)(2,1)S(1)}, u32[]{:S(2)}, u32[]{:S(2)}) collective-permute-start(bf16[2,136,256]{2,1,0:T(8,128)(2,1)S(1)} %collective-permute-done.refs_0_), channel_id=1, source_target_pairs={{0,16},{1,17},{2,18},{3,19},{4,20},{5,21},{6,22},{7,23},{8,24},{9,... | collective-permute-start | bytes 417800 | tf_op jit(solution)/shard_map/ppermute | solution.py:58
  12.7 9.4 %collective-permute-start.2 = (bf16[2,136,256]{2,1,0:T(8,128)(2,1)S(1)}, bf16[2,136,256]{2,1,0:T(8,128)(2,1)S(1)}, u32[]{:S(2)}, u32[]{:S(2)}) collective-permute-start(bf16[2,136,256]{2,1,0:T(8,128)(2,1)S(1)} %collective-permute-done.refs_0_), channel_id=1, source_target_pairs={{0,96},{1,97},{2,98},{3,99},{4,100},{5,101},{6,102},{7,103},{8,104... | collective-permute-start | bytes 417800 | tf_op jit(solution)/shard_map/ppermute | solution.py:58
  19.5 6.3 %collective-permute-start.1 = (bf16[2,136,256]{2,1,0:T(8,128)(2,1)S(1)}, bf16[2,136,256]{2,1,0:T(8,128)(2,1)S(1)}, u32[]{:S(2)}, u32[]{:S(2)}) collective-permute-start(bf16[2,136,256]{2,1,0:T(8,128)(2,1)S(1)} %collective-permute-done.refs_0_), channel_id=1, source_target_pairs={{0,32},{1,33},{2,34},{3,35},{4,36},{5,37},{6,38},{7,39},{8,40},{9,... | collective-permute-start | bytes 417800 | tf_op jit(solution)/shard_map/ppermute | solution.py:58
  25.9 15.5 %collective-permute-start.6 = (bf16[8,136,256]{2,1,0:T(8,128)(2,1)S(1)}, bf16[8,136,256]{2,1,0:T(8,128)(2,1)S(1)}, u32[]{:S(2)}, u32[]{:S(2)}) collective-permute-start(bf16[8,136,256]{2,1,0:T(8,128)(2,1)S(1)} %pad_maximum_fusion), channel_id=1, source_target_pairs={{0,8},{1,9},{2,10},{3,11},{4,12},{5,13},{6,14},{7,15},{8,0},{9,1},... | collective-permute-start | bytes 1671176 | tf_op jit(solution)/shard_map/ppermute | solution.py:58
  26.0 8.1 %collective-permute-start.9 = (bf16[2,136,256]{2,1,0:T(8,128)(2,1)S(1)}, bf16[2,136,256]{2,1,0:T(8,128)(2,1)S(1)}, u32[]{:S(2)}, u32[]{:S(2)}) collective-permute-start(bf16[2,136,256]{2,1,0:T(8,128)(2,1)S(1)} %stamp.1), channel_id=1, source_target_pairs={{0,4},{1,5},{2,6},{3,7},{4,0},{5,1},{6,2},{7,3},{8,12},{9,13},{10,... | collective-permute-start | bytes 417800 | tf_op jit(solution)/shard_map/ppermute | solution.py:58
  28.3 8.6 %collective-permute-start.8 = (bf16[2,136,256]{2,1,0:T(8,128)(2,1)S(1)}, bf16[2,136,256]{2,1,0:T(8,128)(2,1)S(1)}, u32[]{:S(2)}, u32[]{:S(2)}) collective-permute-start(bf16[2,136,256]{2,1,0:T(8,128)(2,1)S(1)} %stamp.1), channel_id=1, source_target_pairs={{0,6},{1,7},{2,0},{3,1},{4,2},{5,3},{6,4},{7,5},{8,14},{9,15},{10,... | collective-permute-start | bytes 417800 | tf_op jit(solution)/shard_map/ppermute | solution.py:58
  29.1 7.8 %collective-permute-start.7 = (bf16[2,136,256]{2,1,0:T(8,128)(2,1)S(1)}, bf16[2,136,256]{2,1,0:T(8,128)(2,1)S(1)}, u32[]{:S(2)}, u32[]{:S(2)}) collective-permute-start(bf16[2,136,256]{2,1,0:T(8,128)(2,1)S(1)} %stamp.1), channel_id=1, source_target_pairs={{0,2},{1,3},{2,4},{3,5},{4,6},{5,7},{6,0},{7,1},{8,10},{9,11},{10,... | collective-permute-start | bytes 417800 | tf_op jit(solution)/shard_map/ppermute | solution.py:58
  30.3 9.3 %collective-permute-start.5 = (bf16[3,136,256]{2,1,0:T(8,128)(2,1)S(1)}, bf16[3,136,256]{2,1,0:T(8,128)(2,1)S(1)}, u32[]{:S(2)}, u32[]{:S(2)}) collective-permute-start(bf16[3,136,256]{2,1,0:T(8,128)(2,1)S(1)} %get-tuple-element.47), channel_id=1, source_target_pairs={{0,96},{1,97},{2,98},{3,99},{4,100},{5,101},{6,102},{7,103},{8,104... | collective-permute-start | bytes 626696 | tf_op jit(solution)/shard_map/ppermute | solution.py:58
  34.1 7.3 %collective-permute-start.4 = (bf16[3,136,256]{2,1,0:T(8,128)(2,1)S(1)}, bf16[3,136,256]{2,1,0:T(8,128)(2,1)S(1)}, u32[]{:S(2)}, u32[]{:S(2)}) collective-permute-start(bf16[3,136,256]{2,1,0:T(8,128)(2,1)S(1)} %get-tuple-element.48), channel_id=1, source_target_pairs={{0,32},{1,33},{2,34},{3,35},{4,36},{5,37},{6,38},{7,39},{8,40},{9,... | collective-permute-start | bytes 626696 | tf_op jit(solution)/shard_map/ppermute | solution.py:58
  41.4 6.1 %collective-permute-start.12 = (bf16[6,136,256]{2,1,0:T(8,128)(2,1)S(1)}, bf16[6,136,256]{2,1,0:T(8,128)(2,1)S(1)}, u32[]{:S(2)}, u32[]{:S(2)}) collective-permute-start(bf16[6,136,256]{2,1,0:T(8,128)(2,1)S(1)} %pad_maximum_fusion.2), channel_id=1, source_target_pairs={{0,8},{1,9},{2,10},{3,11},{4,12},{5,13},{6,14},{7,15},{8,0},{9,1},... | collective-permute-start | bytes 1253384 | tf_op jit(solution)/shard_map/ppermute | solution.py:58
  41.6 4.6 %collective-permute-start.11 = (bf16[1,136,256]{2,1,0:T(8,128)(2,1)S(1)}, bf16[1,136,256]{2,1,0:T(8,128)(2,1)S(1)}, u32[]{:S(2)}, u32[]{:S(2)}) collective-permute-start(bf16[1,136,256]{2,1,0:T(8,128)(2,1)S(1)} %slice.15), channel_id=1, source_target_pairs={{0,96},{1,97},{2,98},{3,99},{4,100},{5,101},{6,102},{7,103},{8,104... | collective-permute-start | bytes 208904 | tf_op jit(solution)/shard_map/ppermute | solution.py:58
  41.6 5.8 %collective-permute-start.10 = (bf16[1,136,256]{2,1,0:T(8,128)(2,1)S(1)}, bf16[1,136,256]{2,1,0:T(8,128)(2,1)S(1)}, u32[]{:S(2)}, u32[]{:S(2)}) collective-permute-start(bf16[1,136,256]{2,1,0:T(8,128)(2,1)S(1)} %slice.14), channel_id=1, source_target_pairs={{0,32},{1,33},{2,34},{3,35},{4,36},{5,37},{6,38},{7,39},{8,40},{9,... | collective-permute-start | bytes 208904 | tf_op jit(solution)/shard_map/ppermute | solution.py:58
  47.5 1.5 %copy-start = (s32[32,1,16]{0,2,1:T(8,128)S(1)}, s32[32,1,16]{0,2,1:T(8,128)}, u32[]{:S(2)}) copy-start(s32[32,1,16]{0,2,1:T(8,128)} %param.5) | copy-start | bytes 6148
  47.5 1.5 %collective-permute-start.13 = (bf16[2,136,256]{2,1,0:T(8,128)(2,1)S(1)}, bf16[2,136,256]{2,1,0:T(8,128)(2,1)S(1)}, u32[]{:S(2)}, u32[]{:S(2)}) collective-permute-start(bf16[2,136,256]{2,1,0:T(8,128)(2,1)S(1)} %pad_maximum_fusion.5), channel_id=1, source_target_pairs={{0,8},{1,9},{2,10},{3,11},{4,12},{5,13},{6,14},{7,15},{8,0},{9,1},... | collective-permute-start | bytes 417800 | tf_op jit(solution)/shard_map/ppermute | solution.py:58
  47.6 18.1 %collective-permute-start.14 = (bf16[8,136,256]{2,1,0:T(8,128)(2,1)S(1)}, bf16[8,136,256]{2,1,0:T(8,128)(2,1)S(1)}, u32[]{:S(2)}, u32[]{:S(2)}) collective-permute-start(bf16[8,136,256]{2,1,0:T(8,128)(2,1)S(1)} %pad_maximum_fusion.1.line), channel_id=1, source_target_pairs={{0,1},{1,0},{2,3},{3,2},{4,5},{5,4},{6,7},{7,6},{8,9},{9,8},{10,11... | collective-permute-start | bytes 1671176 | tf_op jit(solution)/shard_map/ppermute | solution.py:58
  72.4 5.6 %collective-permute-start.15 = (f32[64,64,128]{2,1,0:T(8,128)S(1)}, f32[64,64,128]{2,1,0:T(8,128)S(1)}, u32[]{:S(2)}, u32[]{:S(2)}) collective-permute-start(f32[64,64,128]{2,1,0:T(8,128)S(1)} %get-tuple-element.46), channel_id=1, source_target_pairs={{0,8},{1,9},{2,10},{3,11},{4,12},{5,13},{6,14},{7,15},{8,0},{9,1},... | collective-permute-start | bytes 6291464 | tf_op jit(solution)/shard_map/ppermute | solution.py:58

commit v8 on v7

--- a/solution.py
+++ b/solution.py
@@ -183,12 +183,9 @@
     @pl.loop(0, 4)
     def _(n):
         at = pl.ds(pl.multiple_of(256 * n, 256), 256)
-        left = turned[slot]
-        c = jnp.dot(left, hi[:, at], preferred_element_type=F32)
-        c = c + jnp.dot(left, lo[:, at], preferred_element_type=F32)
-        for q in range(8):
-            for j in range(2):
-                out_ref[8 * q + 2 * n + j] = c[BS * q : BS * (q + 1), 128 * j : 128 * (j + 1)]
+        left = jnp.concatenate([turned[slot], turned[slot]], axis=1)
+        c = jnp.dot(left, jnp.concatenate([hi[:, at], lo[:, at]]), preferred_element_type=F32)
+        store_blocks(c, n, out_ref)
 
 
 def turn_line(ref, side, turned):
@@ -203,6 +200,12 @@
 
 def turn_own(line, turned):
     turn_line(line, 0, turned)
+
+
+def store_blocks(c, n, out_ref):
+    for q in range(8):
+        for j in range(2):
+            out_ref[16 * (q // 2) + 4 * n + 2 * (q % 2) + j] = c[BS * q : BS * (q + 1), 128 * j : 128 * (j + 1)]
 
 
 def other_half(hi, lo, beside, turned_in, turned, out_ref):
@@ -292,7 +295,7 @@
         in_specs=[VMEM] * 4,
         out_specs=(VMEM, VMEM),
         input_output_aliases={3: 0},
-        compiler_params=pltpu.CompilerParams(vmem_limit_bytes=16 << 20),
+        compiler_params=pltpu.CompilerParams(vmem_limit_bytes=20 << 20),
         cost_estimate=cost(1 << 33),
         name="other_half",
     )(hi, lo, beside, turned)
@@ -376,16 +379,18 @@
 
 
 def pack(a_ref, b_ref, out_ref):
-    @pl.loop(0, a_ref.shape[0])
-    def _(i):
-        total = a_ref[i] + b_ref[i]
-        largest = jnp.max(jnp.abs(total), axis=0, keepdims=True)
-        power = jnp.clip(jnp.ceil(jnp.log2(jnp.maximum(largest, 1e-36))), -110.0, 60.0)
-        scaled = jnp.floor(total * jnp.exp2(15.0 - power) + 0.5)
-        scaled = jnp.minimum(scaled, 32767.0)
-        out_ref[i, :BS, :] = scaled.astype(jnp.int32).astype(jnp.int16)
-        power = jnp.broadcast_to(power, (ROWS - BS, 128))
-        out_ref[i, BS:, :] = power.astype(jnp.int32).astype(jnp.int16)
+    @pl.loop(0, a_ref.shape[0] // 4)
+    def _(four):
+        for i in range(4):
+            at = 4 * four + i
+            total = a_ref[at] + b_ref[at]
+            largest = jnp.max(jnp.abs(total), axis=0, keepdims=True)
+            power = jnp.clip(jnp.ceil(jnp.log2(jnp.maximum(largest, 1e-36))), -110.0, 60.0)
+            scaled = jnp.floor(total * jnp.exp2(15.0 - power) + 0.5)
+            scaled = jnp.minimum(scaled, 32767.0)
+            out_ref[at, :BS, :] = scaled.astype(jnp.int32).astype(jnp.int16)
+            power = jnp.broadcast_to(power, (ROWS - BS, 128))
+            out_ref[at, BS:, :] = power.astype(jnp.int32).astype(jnp.int16)
 
 
 def unpack(in_ref, out_ref):
@@ -426,7 +431,7 @@
     met = send(other, OTHER_CORE)
     own = run_own_half(hi, lo, turned)
     packed = packed_sum(own, met)
-    mixed = lax.all_to_all(packed, ("x", "yh", "z", "yl"), 0, 0, tiled=True)
+    mixed = lax.all_to_all(packed, ("x", "z", "yh", "yl"), 0, 0, tiled=True)
     return unpacked_sum(mixed)
 
 

time: 109 us -> 108 us (level)
  Pallas kernels: 40.2 us -> 38.8 us
    pallas_call x1, Pallas kernels: 2.46 us -> 1.07 us  [packed_sum(): pl.pallas_call(pack, out_shape=jax.ShapeDtypeStruct((64, ROWS, 128), jnp....]
where the time goes in v8:
time: 108 us
  Pallas kernels  38.8 us (36%)
  blocking collectives  27.6 us (26%)
  starting transfers between devices  20.8 us (19%)
  waiting for transfers between devices  20 us (19%)
    all_to_all x1, blocking collectives, shards(): mixed = lax.all_to_all(packed, ('x', 'z', 'yh', 'yl'), 0, 0, tiled=True)  27.6 us
    ppermute x16, starting transfers between devices, send(): return lax.ppermute(value, AXES, pairs)  20.8 us
    ppermute x16, waiting for transfers between devices, send(): return lax.ppermute(value, AXES, pairs)  20 us
    pallas_call x1, Pallas kernels, run_fine_product(): pl.pallas_call(functools.partial(fine_product, what), out_shape=(pltpu.VM...  16.6 us
    pallas_call x1, Pallas kernels, run_other_half(): pl.pallas_call(other_half, out_shape=(pltpu.VMEM(turned.shape, BF16), HAL...  6.71 us
    pallas_call x4, Pallas kernels, run_place(): out = call(*arrays, *given, *fetched)  5.2 us
    pallas_call x1, Pallas kernels, run_own_half(): pl.pallas_call(own_half, out_shape=HALF, in_specs=[VMEM] * 3, out_specs=V...  5.1 us
  transfers between devices with their start and end apart: 16, of which 8 were waited for; matrix products, arithmetic and copies ran while one was open for 0% of the time, Pallas kernels for 26%

profile of v8, /device:TPU:0, one launch (start us, length us, event | category | flops | bytes accessed | tf_op | source)
XLA Modules:
  0.0 107.7 jit_solution(5930399721865903093)
XLA Ops:
  0.0 1.5 %stamp.1 = bf16[2,136,256]{2,1,0:T(8,128)(2,1)S(1)} custom-call(s32[4,4]{1,0:T(4,128)} %cols_ref.1, bf16[4,64,256]{2,1,0:T(8,128)(2,1)} %vals_ref.1), custom_call_target="tpu_custom_call" | custom-call | tf_op jit(solution)/shard_map/stamp/pallas_call | solution.py:337
  1.5 3.2 %collective-permute-start = (bf16[2,136,256]{2,1,0:T(8,128)(2,1)S(1)}, bf16[2,136,256]{2,1,0:T(8,128)(2,1)S(1)}, u32[]{:S(2)}, u32[]{:S(2)}) collective-permute-start(bf16[2,136,256]{2,1,0:T(8,128)(2,1)S(1)} %stamp.1), channel_id=1, source_target_pairs={{0,64},{1,80},{2,32},{3,48},{4,0},{5,16},{6,96},{7,112},{8,72},{9,... | collective-permute-start | bytes 417800 | tf_op jit(solution)/shard_map/ppermute | solution.py:58
  4.7 4.5 %collective-permute-done.refs_0_ = bf16[2,136,256]{2,1,0:T(8,128)(2,1)S(1)} collective-permute-done((bf16[2,136,256]{2,1,0:T(8,128)(2,1)S(1)}, bf16[2,136,256]{2,1,0:T(8,128)(2,1)S(1)}, u32[]{:S(2)}, u32[]{:S(2)}) %collective-permute-start) | collective-permute-done | bytes 139296 | tf_op jit(solution)/shard_map/ppermute | solution.py:58
  9.3 3.5 %collective-permute-start.3 = (bf16[2,136,256]{2,1,0:T(8,128)(2,1)S(1)}, bf16[2,136,256]{2,1,0:T(8,128)(2,1)S(1)}, u32[]{:S(2)}, u32[]{:S(2)}) collective-permute-start(bf16[2,136,256]{2,1,0:T(8,128)(2,1)S(1)} %collective-permute-done.refs_0_), channel_id=1, source_target_pairs={{0,16},{1,17},{2,18},{3,19},{4,20},{5,21},{6,22},{7,23},{8,24},{9,... | collective-permute-start | bytes 417800 | tf_op jit(solution)/shard_map/ppermute | solution.py:58
  12.7 6.8 %collective-permute-start.2 = (bf16[2,136,256]{2,1,0:T(8,128)(2,1)S(1)}, bf16[2,136,256]{2,1,0:T(8,128)(2,1)S(1)}, u32[]{:S(2)}, u32[]{:S(2)}) collective-permute-start(bf16[2,136,256]{2,1,0:T(8,128)(2,1)S(1)} %collective-permute-done.refs_0_), channel_id=1, source_target_pairs={{0,96},{1,97},{2,98},{3,99},{4,100},{5,101},{6,102},{7,103},{8,104... | collective-permute-start | bytes 417800 | tf_op jit(solution)/shard_map/ppermute | solution.py:58
  19.5 0.0 collective-permute-start.1
  19.5 0.3 shard_map.46.refs_3_
  19.9 0.0 collective-permute-done.3.refs_2_
  19.9 2.2 %collective-permute-done.2.refs_1_ = bf16[2,136,256]{2,1,0:T(8,128)(2,1)S(1)} collective-permute-done((bf16[2,136,256]{2,1,0:T(8,128)(2,1)S(1)}, bf16[2,136,256]{2,1,0:T(8,128)(2,1)S(1)}, u32[]{:S(2)}, u32[]{:S(2)}) %collective-permute-start.2) | collective-permute-done | bytes 139296 | tf_op jit(solution)/shard_map/ppermute | solution.py:58
  22.1 3.7 %collective-permute-done.1.refs_0_ = bf16[2,136,256]{2,1,0:T(8,128)(2,1)S(1)} collective-permute-done((bf16[2,136,256]{2,1,0:T(8,128)(2,1)S(1)}, bf16[2,136,256]{2,1,0:T(8,128)(2,1)S(1)}, u32[]{:S(2)}, u32[]{:S(2)}) %collective-permute-start.1) | collective-permute-done | bytes 139296 | tf_op jit(solution)/shard_map/ppermute | solution.py:58
  25.8 0.1 pad_maximum_fusion
  25.9 0.1 collective-permute-start.6
  26.0 2.3 %collective-permute-start.9 = (bf16[2,136,256]{2,1,0:T(8,128)(2,1)S(1)}, bf16[2,136,256]{2,1,0:T(8,128)(2,1)S(1)}, u32[]{:S(2)}, u32[]{:S(2)}) collective-permute-start(bf16[2,136,256]{2,1,0:T(8,128)(2,1)S(1)} %stamp.1), channel_id=1, source_target_pairs={{0,4},{1,5},{2,6},{3,7},{4,0},{5,1},{6,2},{7,3},{8,12},{9,13},{10,... | collective-permute-start | bytes 417800 | tf_op jit(solution)/shard_map/ppermute | solution.py:58
  28.3 0.8 collective-permute-start.8
  29.1 1.2 %collective-permute-start.7 = (bf16[2,136,256]{2,1,0:T(8,128)(2,1)S(1)}, bf16[2,136,256]{2,1,0:T(8,128)(2,1)S(1)}, u32[]{:S(2)}, u32[]{:S(2)}) collective-permute-start(bf16[2,136,256]{2,1,0:T(8,128)(2,1)S(1)} %stamp.1), channel_id=1, source_target_pairs={{0,2},{1,3},{2,4},{3,5},{4,6},{5,7},{6,0},{7,1},{8,10},{9,11},{10,... | collective-permute-start | bytes 417800 | tf_op jit(solution)/shard_map/ppermute | solution.py:58
  30.3 0.1 collective-permute-start.5
  30.4 3.7 %collective-permute-done.9 = bf16[2,136,256]{2,1,0:T(8,128)(2,1)S(1)} collective-permute-done((bf16[2,136,256]{2,1,0:T(8,128)(2,1)S(1)}, bf16[2,136,256]{2,1,0:T(8,128)(2,1)S(1)}, u32[]{:S(2)}, u32[]{:S(2)}) %collective-permute-start.9) | collective-permute-done | bytes 139296 | tf_op jit(solution)/shard_map/ppermute | solution.py:58
  34.1 0.0 collective-permute-start.4
  34.1 2.8 %collective-permute-done.8 = bf16[2,136,256]{2,1,0:T(8,128)(2,1)S(1)} collective-permute-done((bf16[2,136,256]{2,1,0:T(8,128)(2,1)S(1)}, bf16[2,136,256]{2,1,0:T(8,128)(2,1)S(1)}, u32[]{:S(2)}, u32[]{:S(2)}) %collective-permute-start.8) | collective-permute-done | bytes 139296 | tf_op jit(solution)/shard_map/ppermute | solution.py:58
  36.9 0.0 collective-permute-done.7
  36.9 0.1 pad_maximum_fusion.1.line
  36.9 1.6 %turn.1.turned_in = bf16[2,512,2048]{2,1,0:T(8,128)(2,1)S(1)} custom-call(bf16[8,136,256]{2,1,0:T(8,128)(2,1)S(1)} %pad_maximum_fusion.1.line), custom_call_target="tpu_custom_call" | custom-call | flops 1073741824 | bytes 8388608 | tf_op jit(solution)/shard_map/turn/pallas_call | solution.py:280
  38.6 1.1 %shard_map.47.refs_3_ = bf16[64,64,1024]{2,1,0:T(8,128)(2,1)S(1)} custom-call(bf16[2,136,256]{2,1,0:T(8,128)(2,1)S(1)} %collective-permute-done.1.refs_0_, bf16[2,136,256]{2,1,0:T(8,128)(2,1)S(1)} %collective-permute-done.2.refs_1_, bf16[2,136,256]{2,1,0:T(8,128)(2,1)S(1)} %collective-permute-done.3.refs_2_, ...), custom_call_target="tpu_custom_call", output_to_operand_aliasing={{}: (3, {})} | custom-call | flops 1073741824 | bytes 8388608 | tf_op jit(solution)/shard_map/pallas_call | solution.py:261
  39.6 0.0 collective-permute-done.5.refs_1_
  39.7 1.7 %collective-permute-done.4.refs_0_ = bf16[3,136,256]{2,1,0:T(8,128)(2,1)S(1)} collective-permute-done((bf16[3,136,256]{2,1,0:T(8,128)(2,1)S(1)}, bf16[3,136,256]{2,1,0:T(8,128)(2,1)S(1)}, u32[]{:S(2)}, u32[]{:S(2)}) %collective-permute-start.4) | collective-permute-done | bytes 208928 | tf_op jit(solution)/shard_map/ppermute | solution.py:58
  41.4 0.0 collective-permute-done.6.refs_2_
  41.4 0.1 collective-permute-start.12
  41.6 0.1 collective-permute-start.11
  41.6 2.0 %collective-permute-start.10 = (bf16[1,136,256]{2,1,0:T(8,128)(2,1)S(1)}, bf16[1,136,256]{2,1,0:T(8,128)(2,1)S(1)}, u32[]{:S(2)}, u32[]{:S(2)}) collective-permute-start(bf16[1,136,256]{2,1,0:T(8,128)(2,1)S(1)} %slice.14), channel_id=1, source_target_pairs={{0,32},{1,33},{2,34},{3,35},{4,36},{5,37},{6,38},{7,39},{8,40},{9,... | collective-permute-start | bytes 208904 | tf_op jit(solution)/shard_map/ppermute | solution.py:58
  43.7 2.5 %shard_map.48 = (bf16[64,64,1024]{2,1,0:T(8,128)(2,1)S(1)}, bf16[32,64,1024]{2,1,0:T(8,128)(2,1)S(1)}) custom-call(bf16[3,136,256]{2,1,0:T(8,128)(2,1)S(1)} %collective-permute-done.4.refs_0_, bf16[3,136,256]{2,1,0:T(8,128)(2,1)S(1)} %collective-permute-done.5.refs_1_, ...), custom_call_target="tpu_custom_call", output_to_operand_aliasing={{0}: (3, {})} | custom-call | flops 1073741824 | bytes 8388608 | tf_op jit(solution)/shard_map/pallas_call | solution.py:261
  46.1 0.1 collective-permute-done.11.refs_1_
  46.2 1.3 %collective-permute-done.10.refs_0_ = bf16[1,136,256]{2,1,0:T(8,128)(2,1)S(1)} collective-permute-done((bf16[1,136,256]{2,1,0:T(8,128)(2,1)S(1)}, bf16[1,136,256]{2,1,0:T(8,128)(2,1)S(1)}, u32[]{:S(2)}, u32[]{:S(2)}) %collective-permute-start.10) | collective-permute-done | bytes 69664 | tf_op jit(solution)/shard_map/ppermute | solution.py:58
  47.5 0.0 collective-permute-done.12.refs_2_
  47.5 0.0 copy-start
  47.5 0.1 collective-permute-start.13
  47.6 0.1 collective-permute-start.14
  47.7 1.3 %shard_map.49.refs_1_ = bf16[64,64,1024]{2,1,0:T(8,128)(2,1)S(1)} custom-call(bf16[1,136,256]{2,1,0:T(8,128)(2,1)S(1)} %collective-permute-done.10.refs_0_, bf16[1,136,256]{2,1,0:T(8,128)(2,1)S(1)} %collective-permute-done.11.refs_1_, bf16[6,136,256]{2,1,0:T(8,128)(2,1)S(1)} %collective-permute-done.12.refs_2_, ...), custom_call_target="tpu_custom_call", output_to_operand_aliasing={{}: (3, {})} | custom-call | flops 1073741824 | bytes 8388608 | tf_op jit(solution)/shard_map/pallas_call | solution.py:261
  49.0 0.0 collective-permute-done.13.refs_0_
  49.0 0.0 copy-done
  49.1 16.6 %fine_product.1 = (bf16[2048,1024]{1,0:T(8,128)(2,1)S(1)}, bf16[2048,1024]{1,0:T(8,128)(2,1)S(1)}, bf16[64,64,1024]{2,1,0:T(8,128)(2,1)S(1)}) custom-call(s32[16,32]{1,0:T(8,128)S(1)} %bitcast.4, bf16[32,64,1024]{2,1,0:T(8,128)(2,1)S(1)} %get-tuple-element.36.a_ref, ...), custom_call_target="tpu_custom_call", output_to_operand_aliasing={{2}: (3, {})} | custom-call | flops 17179869184 | bytes 8388608 | tf_op jit(solution)/shard_map/fine_product/pallas_call | solution.py:267
  65.7 0.0 collective-permute-done.14.beside
  65.7 6.7 %other_half.1 = (bf16[2,512,2048]{2,1,0:T(8,128)(2,1)S(1)}, f32[64,64,128]{2,1,0:T(8,128)S(1)}) custom-call(bf16[2048,1024]{1,0:T(8,128)(2,1)S(1)} %get-tuple-element.41.hi, bf16[2048,1024]{1,0:T(8,128)(2,1)S(1)} %get-tuple-element.42.lo, bf16[8,136,256]{2,1,0:T(8,128)(2,1)S(1)} %collective-permute-done.14.beside, ...), custom_call_target="tpu_custom_call", output_to_operand_aliasing={{0}: (3, {})} | custom-call | flops 8589934592 | bytes 8388608 | tf_op jit(solution)/shard_map/other_half/pallas_call | solution.py:292
  72.4 0.5 collective-permute-start.15
  72.9 5.1 %own_half.1.a_ref = f32[64,64,128]{2,1,0:T(8,128)S(1)} custom-call(bf16[2048,1024]{1,0:T(8,128)(2,1)S(1)} %get-tuple-element.41.hi, bf16[2048,1024]{1,0:T(8,128)(2,1)S(1)} %get-tuple-element.42.lo, bf16[2,512,2048]{2,1,0:T(8,128)(2,1)S(1)} %get-tuple-element.45.turned), custom_call_target="tpu_custom_call" | custom-call | flops 8589934592 | bytes 8388608 | tf_op jit(solution)/shard_map/own_half/pallas_call | solution.py:305
  78.0 0.0 collective-permute-done.15.b_ref
  78.0 1.1 pack.1
  79.1 27.6 %all_to_all.5.in_ref = s16[64,72,128]{2,1,0:T(8,128)(2,1)S(1)} all-to-all(s16[64,72,128]{2,1,0:T(8,128)(2,1)S(1)} %pack.1), channel_id=1, replica_groups=mesh['x'=4,'yh'=2,'core'=2,'z'=4,'yl'=2] {'x','z','yh','yl'}, dimensions={0} | all-to-all | bytes 2359296 | tf_op jit(solution)/shard_map/all_to_all | solution.py:434
  106.7 1.0 unpack.1
  (7 shorter events, 0.1 us)
Async XLA Ops:
  1.5 7.7 %collective-permute-start = (bf16[2,136,256]{2,1,0:T(8,128)(2,1)S(1)}, bf16[2,136,256]{2,1,0:T(8,128)(2,1)S(1)}, u32[]{:S(2)}, u32[]{:S(2)}) collective-permute-start(bf16[2,136,256]{2,1,0:T(8,128)(2,1)S(1)} %stamp.1), channel_id=1, source_target_pairs={{0,64},{1,80},{2,32},{3,48},{4,0},{5,16},{6,96},{7,112},{8,72},{9,... | collective-permute-start | bytes 417800 | tf_op jit(solution)/shard_map/ppermute | solution.py:58
  9.3 10.6 %collective-permute-start.3 = (bf16[2,136,256]{2,1,0:T(8,128)(2,1)S(1)}, bf16[2,136,256]{2,1,0:T(8,128)(2,1)S(1)}, u32[]{:S(2)}, u32[]{:S(2)}) collective-permute-start(bf16[2,136,256]{2,1,0:T(8,128)(2,1)S(1)} %collective-permute-done.refs_0_), channel_id=1, source_target_pairs={{0,16},{1,17},{2,18},{3,19},{4,20},{5,21},{6,22},{7,23},{8,24},{9,... | collective-permute-start | bytes 417800 | tf_op jit(solution)/shard_map/ppermute | solution.py:58
  12.7 9.4 %collective-permute-start.2 = (bf16[2,136,256]{2,1,0:T(8,128)(2,1)S(1)}, bf16[2,136,256]{2,1,0:T(8,128)(2,1)S(1)}, u32[]{:S(2)}, u32[]{:S(2)}) collective-permute-start(bf16[2,136,256]{2,1,0:T(8,128)(2,1)S(1)} %collective-permute-done.refs_0_), channel_id=1, source_target_pairs={{0,96},{1,97},{2,98},{3,99},{4,100},{5,101},{6,102},{7,103},{8,104... | collective-permute-start | bytes 417800 | tf_op jit(solution)/shard_map/ppermute | solution.py:58
  19.5 6.3 %collective-permute-start.1 = (bf16[2,136,256]{2,1,0:T(8,128)(2,1)S(1)}, bf16[2,136,256]{2,1,0:T(8,128)(2,1)S(1)}, u32[]{:S(2)}, u32[]{:S(2)}) collective-permute-start(bf16[2,136,256]{2,1,0:T(8,128)(2,1)S(1)} %collective-permute-done.refs_0_), channel_id=1, source_target_pairs={{0,32},{1,33},{2,34},{3,35},{4,36},{5,37},{6,38},{7,39},{8,40},{9,... | collective-permute-start | bytes 417800 | tf_op jit(solution)/shard_map/ppermute | solution.py:58
  25.9 15.5 %collective-permute-start.6 = (bf16[8,136,256]{2,1,0:T(8,128)(2,1)S(1)}, bf16[8,136,256]{2,1,0:T(8,128)(2,1)S(1)}, u32[]{:S(2)}, u32[]{:S(2)}) collective-permute-start(bf16[8,136,256]{2,1,0:T(8,128)(2,1)S(1)} %pad_maximum_fusion), channel_id=1, source_target_pairs={{0,8},{1,9},{2,10},{3,11},{4,12},{5,13},{6,14},{7,15},{8,0},{9,1},... | collective-permute-start | bytes 1671176 | tf_op jit(solution)/shard_map/ppermute | solution.py:58
  26.0 8.1 %collective-permute-start.9 = (bf16[2,136,256]{2,1,0:T(8,128)(2,1)S(1)}, bf16[2,136,256]{2,1,0:T(8,128)(2,1)S(1)}, u32[]{:S(2)}, u32[]{:S(2)}) collective-permute-start(bf16[2,136,256]{2,1,0:T(8,128)(2,1)S(1)} %stamp.1), channel_id=1, source_target_pairs={{0,4},{1,5},{2,6},{3,7},{4,0},{5,1},{6,2},{7,3},{8,12},{9,13},{10,... | collective-permute-start | bytes 417800 | tf_op jit(solution)/shard_map/ppermute | solution.py:58
  28.3 8.6 %collective-permute-start.8 = (bf16[2,136,256]{2,1,0:T(8,128)(2,1)S(1)}, bf16[2,136,256]{2,1,0:T(8,128)(2,1)S(1)}, u32[]{:S(2)}, u32[]{:S(2)}) collective-permute-start(bf16[2,136,256]{2,1,0:T(8,128)(2,1)S(1)} %stamp.1), channel_id=1, source_target_pairs={{0,6},{1,7},{2,0},{3,1},{4,2},{5,3},{6,4},{7,5},{8,14},{9,15},{10,... | collective-permute-start | bytes 417800 | tf_op jit(solution)/shard_map/ppermute | solution.py:58
  29.1 7.8 %collective-permute-start.7 = (bf16[2,136,256]{2,1,0:T(8,128)(2,1)S(1)}, bf16[2,136,256]{2,1,0:T(8,128)(2,1)S(1)}, u32[]{:S(2)}, u32[]{:S(2)}) collective-permute-start(bf16[2,136,256]{2,1,0:T(8,128)(2,1)S(1)} %stamp.1), channel_id=1, source_target_pairs={{0,2},{1,3},{2,4},{3,5},{4,6},{5,7},{6,0},{7,1},{8,10},{9,11},{10,... | collective-permute-start | bytes 417800 | tf_op jit(solution)/shard_map/ppermute | solution.py:58
  30.3 9.3 %collective-permute-start.5 = (bf16[3,136,256]{2,1,0:T(8,128)(2,1)S(1)}, bf16[3,136,256]{2,1,0:T(8,128)(2,1)S(1)}, u32[]{:S(2)}, u32[]{:S(2)}) collective-permute-start(bf16[3,136,256]{2,1,0:T(8,128)(2,1)S(1)} %get-tuple-element.47), channel_id=1, source_target_pairs={{0,96},{1,97},{2,98},{3,99},{4,100},{5,101},{6,102},{7,103},{8,104... | collective-permute-start | bytes 626696 | tf_op jit(solution)/shard_map/ppermute | solution.py:58
  34.1 7.3 %collective-permute-start.4 = (bf16[3,136,256]{2,1,0:T(8,128)(2,1)S(1)}, bf16[3,136,256]{2,1,0:T(8,128)(2,1)S(1)}, u32[]{:S(2)}, u32[]{:S(2)}) collective-permute-start(bf16[3,136,256]{2,1,0:T(8,128)(2,1)S(1)} %get-tuple-element.48), channel_id=1, source_target_pairs={{0,32},{1,33},{2,34},{3,35},{4,36},{5,37},{6,38},{7,39},{8,40},{9,... | collective-permute-start | bytes 626696 | tf_op jit(solution)/shard_map/ppermute | solution.py:58
  41.4 6.1 %collective-permute-start.12 = (bf16[6,136,256]{2,1,0:T(8,128)(2,1)S(1)}, bf16[6,136,256]{2,1,0:T(8,128)(2,1)S(1)}, u32[]{:S(2)}, u32[]{:S(2)}) collective-permute-start(bf16[6,136,256]{2,1,0:T(8,128)(2,1)S(1)} %pad_maximum_fusion.2), channel_id=1, source_target_pairs={{0,8},{1,9},{2,10},{3,11},{4,12},{5,13},{6,14},{7,15},{8,0},{9,1},... | collective-permute-start | bytes 1253384 | tf_op jit(solution)/shard_map/ppermute | solution.py:58
  41.6 4.6 %collective-permute-start.11 = (bf16[1,136,256]{2,1,0:T(8,128)(2,1)S(1)}, bf16[1,136,256]{2,1,0:T(8,128)(2,1)S(1)}, u32[]{:S(2)}, u32[]{:S(2)}) collective-permute-start(bf16[1,136,256]{2,1,0:T(8,128)(2,1)S(1)} %slice.15), channel_id=1, source_target_pairs={{0,96},{1,97},{2,98},{3,99},{4,100},{5,101},{6,102},{7,103},{8,104... | collective-permute-start | bytes 208904 | tf_op jit(solution)/shard_map/ppermute | solution.py:58
  41.6 5.8 %collective-permute-start.10 = (bf16[1,136,256]{2,1,0:T(8,128)(2,1)S(1)}, bf16[1,136,256]{2,1,0:T(8,128)(2,1)S(1)}, u32[]{:S(2)}, u32[]{:S(2)}) collective-permute-start(bf16[1,136,256]{2,1,0:T(8,128)(2,1)S(1)} %slice.14), channel_id=1, source_target_pairs={{0,32},{1,33},{2,34},{3,35},{4,36},{5,37},{6,38},{7,39},{8,40},{9,... | collective-permute-start | bytes 208904 | tf_op jit(solution)/shard_map/ppermute | solution.py:58
  47.5 1.5 %copy-start = (s32[32,1,16]{0,2,1:T(8,128)S(1)}, s32[32,1,16]{0,2,1:T(8,128)}, u32[]{:S(2)}) copy-start(s32[32,1,16]{0,2,1:T(8,128)} %param.5) | copy-start | bytes 6148
  47.5 1.5 %collective-permute-start.13 = (bf16[2,136,256]{2,1,0:T(8,128)(2,1)S(1)}, bf16[2,136,256]{2,1,0:T(8,128)(2,1)S(1)}, u32[]{:S(2)}, u32[]{:S(2)}) collective-permute-start(bf16[2,136,256]{2,1,0:T(8,128)(2,1)S(1)} %pad_maximum_fusion.5), channel_id=1, source_target_pairs={{0,8},{1,9},{2,10},{3,11},{4,12},{5,13},{6,14},{7,15},{8,0},{9,1},... | collective-permute-start | bytes 417800 | tf_op jit(solution)/shard_map/ppermute | solution.py:58
  47.6 18.1 %collective-permute-start.14 = (bf16[8,136,256]{2,1,0:T(8,128)(2,1)S(1)}, bf16[8,136,256]{2,1,0:T(8,128)(2,1)S(1)}, u32[]{:S(2)}, u32[]{:S(2)}) collective-permute-start(bf16[8,136,256]{2,1,0:T(8,128)(2,1)S(1)} %pad_maximum_fusion.1.line), channel_id=1, source_target_pairs={{0,1},{1,0},{2,3},{3,2},{4,5},{5,4},{6,7},{7,6},{8,9},{9,8},{10,11... | collective-permute-start | bytes 1671176 | tf_op jit(solution)/shard_map/ppermute | solution.py:58
  72.4 5.6 %collective-permute-start.15 = (f32[64,64,128]{2,1,0:T(8,128)S(1)}, f32[64,64,128]{2,1,0:T(8,128)S(1)}, u32[]{:S(2)}, u32[]{:S(2)}) collective-permute-start(f32[64,64,128]{2,1,0:T(8,128)S(1)} %get-tuple-element.46), channel_id=1, source_target_pairs={{0,8},{1,9},{2,10},{3,11},{4,12},{5,13},{6,14},{7,15},{8,0},{9,1},... | collective-permute-start | bytes 6291464 | tf_op jit(solution)/shard_map/ppermute | solution.py:58

commit v9 on v8

--- a/solution.py
+++ b/solution.py
@@ -354,16 +354,15 @@
     )
     what = ((BEHIND, False), (AHEAD, False), (ACROSS, False))
     line = jnp.concatenate([piece, z1, z2, z3])
-    b2, a2, e1, line, dense, turned = together(
+    turned = run_turn(line)
+    beside = send(line, BESIDE)
+    b2, a2, e1, dense = together(
         send(jnp.concatenate([f, b1[:1]]), NEXT_X),
         send(jnp.concatenate([f, a1[1:]]), LAST_X),
         send(jnp.concatenate([near, b1, a1, f]), OTHER_CORE),
-        line,
         run_place(what, (b1, a1, f), dense),
-        run_turn(line),
     )
     what = ((BEHIND2, False), (AHEAD2, False), (NEAR + BEHIND + AHEAD + ACROSS, True))
-    beside = send(line, BESIDE)
     b3, a3, e2, (dense, a) = together(
         send(b2[:1], NEXT_X),
         send(a2[1:2], LAST_X),

time: 108 us -> 114 us (1.056)
  starting transfers between devices: 20.8 us -> 27.3 us
  waiting for transfers between devices: 20 us -> 18.6 us
    ppermute x16, starting transfers between devices: 20.8 us -> 27.3 us  [send(): return lax.ppermute(value, AXES, pairs)]
    ppermute x16, waiting for transfers between devices: 20 us -> 18.6 us  [send(): return lax.ppermute(value, AXES, pairs)]
  transfers between devices with their start and end apart: 16 -> 16, of which waited for: 8 -> 6; matrix products, arithmetic and copies ran while one was open for 0% -> 0% of each run, Pallas kernels for 26% -> 25%
where the time goes in v9:
time: 114 us
  Pallas kernels  38.8 us (34%)
  blocking collectives  28.5 us (25%)
  starting transfers between devices  27.3 us (24%)
  waiting for transfers between devices  18.6 us (16%)
    all_to_all x1, blocking collectives, shards(): mixed = lax.all_to_all(packed, ('x', 'z', 'yh', 'yl'), 0, 0, tiled=True)  28.5 us
    ppermute x16, starting transfers between devices, send(): return lax.ppermute(value, AXES, pairs)  27.3 us
    ppermute x16, waiting for transfers between devices, send(): return lax.ppermute(value, AXES, pairs)  18.6 us
    pallas_call x1, Pallas kernels, run_fine_product(): pl.pallas_call(functools.partial(fine_product, what), out_shape=(pltpu.VM...  16.6 us
    pallas_call x1, Pallas kernels, run_other_half(): pl.pallas_call(other_half, out_shape=(pltpu.VMEM(turned.shape, BF16), HAL...  6.72 us
    pallas_call x4, Pallas kernels, run_place(): out = call(*arrays, *given, *fetched)  5.18 us
    pallas_call x1, Pallas kernels, run_own_half(): pl.pallas_call(own_half, out_shape=HALF, in_specs=[VMEM] * 3, out_specs=V...  5.1 us
  transfers between devices with their start and end apart: 16, of which 6 were waited for; matrix products, arithmetic and copies ran while one was open for 0% of the time, Pallas kernels for 25%

profile of v9, /device:TPU:0, one launch (start us, length us, event | category | flops | bytes accessed | tf_op | source)
XLA Modules:
  0.0 113.8 jit_solution(11493272275651276103)
XLA Ops:
  0.0 1.5 %stamp.1 = bf16[2,136,256]{2,1,0:T(8,128)(2,1)S(1)} custom-call(s32[4,4]{1,0:T(4,128)} %cols_ref.1, bf16[4,64,256]{2,1,0:T(8,128)(2,1)} %vals_ref.1), custom_call_target="tpu_custom_call" | custom-call | tf_op jit(solution)/shard_map/stamp/pallas_call | solution.py:337
  1.5 3.2 %collective-permute-start = (bf16[2,136,256]{2,1,0:T(8,128)(2,1)S(1)}, bf16[2,136,256]{2,1,0:T(8,128)(2,1)S(1)}, u32[]{:S(2)}, u32[]{:S(2)}) collective-permute-start(bf16[2,136,256]{2,1,0:T(8,128)(2,1)S(1)} %stamp.1), channel_id=1, source_target_pairs={{0,64},{1,80},{2,32},{3,48},{4,0},{5,16},{6,96},{7,112},{8,72},{9,... | collective-permute-start | bytes 417800 | tf_op jit(solution)/shard_map/ppermute | solution.py:58
  4.7 4.5 %collective-permute-done.refs_0_ = bf16[2,136,256]{2,1,0:T(8,128)(2,1)S(1)} collective-permute-done((bf16[2,136,256]{2,1,0:T(8,128)(2,1)S(1)}, bf16[2,136,256]{2,1,0:T(8,128)(2,1)S(1)}, u32[]{:S(2)}, u32[]{:S(2)}) %collective-permute-start) | collective-permute-done | bytes 139296 | tf_op jit(solution)/shard_map/ppermute | solution.py:58
  9.3 0.3 collective-permute-start.1
  9.5 3.7 %collective-permute-start.2 = (bf16[2,136,256]{2,1,0:T(8,128)(2,1)S(1)}, bf16[2,136,256]{2,1,0:T(8,128)(2,1)S(1)}, u32[]{:S(2)}, u32[]{:S(2)}) collective-permute-start(bf16[2,136,256]{2,1,0:T(8,128)(2,1)S(1)} %collective-permute-done.refs_0_), channel_id=1, source_target_pairs={{0,96},{1,97},{2,98},{3,99},{4,100},{5,101},{6,102},{7,103},{8,104... | collective-permute-start | bytes 417800 | tf_op jit(solution)/shard_map/ppermute | solution.py:58
  13.2 6.3 %collective-permute-start.3 = (bf16[2,136,256]{2,1,0:T(8,128)(2,1)S(1)}, bf16[2,136,256]{2,1,0:T(8,128)(2,1)S(1)}, u32[]{:S(2)}, u32[]{:S(2)}) collective-permute-start(bf16[2,136,256]{2,1,0:T(8,128)(2,1)S(1)} %collective-permute-done.refs_0_), channel_id=1, source_target_pairs={{0,16},{1,17},{2,18},{3,19},{4,20},{5,21},{6,22},{7,23},{8,24},{9,... | collective-permute-start | bytes 417800 | tf_op jit(solution)/shard_map/ppermute | solution.py:58
  19.5 0.3 shard_map.46.refs_3_
  19.9 0.0 collective-permute-done.1.refs_0_
  19.9 0.0 collective-permute-done.2.refs_1_
  19.9 2.7 %collective-permute-done.3.refs_2_ = bf16[2,136,256]{2,1,0:T(8,128)(2,1)S(1)} collective-permute-done((bf16[2,136,256]{2,1,0:T(8,128)(2,1)S(1)}, bf16[2,136,256]{2,1,0:T(8,128)(2,1)S(1)}, u32[]{:S(2)}, u32[]{:S(2)}) %collective-permute-start.3) | collective-permute-done | bytes 139296 | tf_op jit(solution)/shard_map/ppermute | solution.py:58
  22.6 0.1 pad_maximum_fusion
  22.7 0.1 collective-permute-start.6
  22.8 0.1 collective-permute-start.4
  22.9 3.2 %collective-permute-start.5 = (bf16[3,136,256]{2,1,0:T(8,128)(2,1)S(1)}, bf16[3,136,256]{2,1,0:T(8,128)(2,1)S(1)}, u32[]{:S(2)}, u32[]{:S(2)}) collective-permute-start(bf16[3,136,256]{2,1,0:T(8,128)(2,1)S(1)} %get-tuple-element.43), channel_id=1, source_target_pairs={{0,96},{1,97},{2,98},{3,99},{4,100},{5,101},{6,102},{7,103},{8,104... | collective-permute-start | bytes 626696 | tf_op jit(solution)/shard_map/ppermute | solution.py:58
  26.1 1.1 shard_map.47.refs_3_
  27.2 4.5 %collective-permute-done.4.refs_0_ = bf16[3,136,256]{2,1,0:T(8,128)(2,1)S(1)} collective-permute-done((bf16[3,136,256]{2,1,0:T(8,128)(2,1)S(1)}, bf16[3,136,256]{2,1,0:T(8,128)(2,1)S(1)}, u32[]{:S(2)}, u32[]{:S(2)}) %collective-permute-start.4) | collective-permute-done | bytes 208928 | tf_op jit(solution)/shard_map/ppermute | solution.py:58
  31.6 0.0 collective-permute-done.5.refs_1_
  31.7 0.0 collective-permute-done.6.refs_2_
  31.7 0.1 collective-permute-start.9
  31.8 0.2 collective-permute-start.11
  32.0 3.5 %collective-permute-start.12 = (bf16[2,136,256]{2,1,0:T(8,128)(2,1)S(1)}, bf16[2,136,256]{2,1,0:T(8,128)(2,1)S(1)}, u32[]{:S(2)}, u32[]{:S(2)}) collective-permute-start(bf16[2,136,256]{2,1,0:T(8,128)(2,1)S(1)} %stamp.1), channel_id=1, source_target_pairs={{0,6},{1,7},{2,0},{3,1},{4,2},{5,3},{6,4},{7,5},{8,14},{9,15},{10,... | collective-permute-start | bytes 417800 | tf_op jit(solution)/shard_map/ppermute | solution.py:58
  35.4 1.4 %collective-permute-start.13 = (bf16[2,136,256]{2,1,0:T(8,128)(2,1)S(1)}, bf16[2,136,256]{2,1,0:T(8,128)(2,1)S(1)}, u32[]{:S(2)}, u32[]{:S(2)}) collective-permute-start(bf16[2,136,256]{2,1,0:T(8,128)(2,1)S(1)} %stamp.1), channel_id=1, source_target_pairs={{0,4},{1,5},{2,6},{3,7},{4,0},{5,1},{6,2},{7,3},{8,12},{9,13},{10,... | collective-permute-start | bytes 417800 | tf_op jit(solution)/shard_map/ppermute | solution.py:58
  36.8 2.8 %collective-permute-done.11 = bf16[2,136,256]{2,1,0:T(8,128)(2,1)S(1)} collective-permute-done((bf16[2,136,256]{2,1,0:T(8,128)(2,1)S(1)}, bf16[2,136,256]{2,1,0:T(8,128)(2,1)S(1)}, u32[]{:S(2)}, u32[]{:S(2)}) %collective-permute-start.11) | collective-permute-done | bytes 139296 | tf_op jit(solution)/shard_map/ppermute | solution.py:58
  39.6 2.3 %collective-permute-done.12 = bf16[2,136,256]{2,1,0:T(8,128)(2,1)S(1)} collective-permute-done((bf16[2,136,256]{2,1,0:T(8,128)(2,1)S(1)}, bf16[2,136,256]{2,1,0:T(8,128)(2,1)S(1)}, u32[]{:S(2)}, u32[]{:S(2)}) %collective-permute-start.12) | collective-permute-done | bytes 139296 | tf_op jit(solution)/shard_map/ppermute | solution.py:58
  41.9 1.9 %collective-permute-done.13 = bf16[2,136,256]{2,1,0:T(8,128)(2,1)S(1)} collective-permute-done((bf16[2,136,256]{2,1,0:T(8,128)(2,1)S(1)}, bf16[2,136,256]{2,1,0:T(8,128)(2,1)S(1)}, u32[]{:S(2)}, u32[]{:S(2)}) %collective-permute-start.13) | collective-permute-done | bytes 139296 | tf_op jit(solution)/shard_map/ppermute | solution.py:58
  43.8 0.1 pad_maximum_fusion.1.line
  43.9 0.1 collective-permute-start.7
  44.0 3.2 %collective-permute-start.8 = (bf16[1,136,256]{2,1,0:T(8,128)(2,1)S(1)}, bf16[1,136,256]{2,1,0:T(8,128)(2,1)S(1)}, u32[]{:S(2)}, u32[]{:S(2)}) collective-permute-start(bf16[1,136,256]{2,1,0:T(8,128)(2,1)S(1)} %slice.15), channel_id=1, source_target_pairs={{0,96},{1,97},{2,98},{3,99},{4,100},{5,101},{6,102},{7,103},{8,104... | collective-permute-start | bytes 208904 | tf_op jit(solution)/shard_map/ppermute | solution.py:58
  47.2 2.5 %shard_map.48 = (bf16[64,64,1024]{2,1,0:T(8,128)(2,1)S(1)}, bf16[32,64,1024]{2,1,0:T(8,128)(2,1)S(1)}) custom-call(bf16[3,136,256]{2,1,0:T(8,128)(2,1)S(1)} %collective-permute-done.4.refs_0_, bf16[3,136,256]{2,1,0:T(8,128)(2,1)S(1)} %collective-permute-done.5.refs_1_, ...), custom_call_target="tpu_custom_call", output_to_operand_aliasing={{0}: (3, {})} | custom-call | flops 1073741824 | bytes 8388608 | tf_op jit(solution)/shard_map/pallas_call | solution.py:261
  49.7 0.0 collective-permute-done.7.refs_0_
  49.7 0.0 collective-permute-done.8.refs_1_
  49.7 0.0 collective-permute-done.9.refs_2_
  49.7 0.1 collective-permute-start.10
  49.8 1.6 %turn.1.turned_in = bf16[2,512,2048]{2,1,0:T(8,128)(2,1)S(1)} custom-call(bf16[8,136,256]{2,1,0:T(8,128)(2,1)S(1)} %pad_maximum_fusion.1.line), custom_call_target="tpu_custom_call" | custom-call | flops 1073741824 | bytes 8388608 | tf_op jit(solution)/shard_map/turn/pallas_call | solution.py:280
  51.4 0.0 copy-start
  51.4 1.7 %collective-permute-start.14 = (bf16[8,136,256]{2,1,0:T(8,128)(2,1)S(1)}, bf16[8,136,256]{2,1,0:T(8,128)(2,1)S(1)}, u32[]{:S(2)}, u32[]{:S(2)}) collective-permute-start(bf16[8,136,256]{2,1,0:T(8,128)(2,1)S(1)} %pad_maximum_fusion.1.line), channel_id=1, source_target_pairs={{0,1},{1,0},{2,3},{3,2},{4,5},{5,4},{6,7},{7,6},{8,9},{9,8},{10,11... | collective-permute-start | bytes 1671176 | tf_op jit(solution)/shard_map/ppermute | solution.py:58
  53.1 1.3 %shard_map.49.refs_1_ = bf16[64,64,1024]{2,1,0:T(8,128)(2,1)S(1)} custom-call(bf16[1,136,256]{2,1,0:T(8,128)(2,1)S(1)} %collective-permute-done.7.refs_0_, bf16[1,136,256]{2,1,0:T(8,128)(2,1)S(1)} %collective-permute-done.8.refs_1_, bf16[6,136,256]{2,1,0:T(8,128)(2,1)S(1)} %collective-permute-done.9.refs_2_, ...), custom_call_target="tpu_custom_call", output_to_operand_aliasing={{}: (3, {})} | custom-call | flops 1073741824 | bytes 8388608 | tf_op jit(solution)/shard_map/pallas_call | solution.py:261
  54.5 0.0 collective-permute-done.10.refs_0_
  54.5 0.0 copy-done
  54.5 16.6 %fine_product.1 = (bf16[2048,1024]{1,0:T(8,128)(2,1)S(1)}, bf16[2048,1024]{1,0:T(8,128)(2,1)S(1)}, bf16[64,64,1024]{2,1,0:T(8,128)(2,1)S(1)}) custom-call(s32[16,32]{1,0:T(8,128)S(1)} %bitcast.4, bf16[32,64,1024]{2,1,0:T(8,128)(2,1)S(1)} %get-tuple-element.34.a_ref, ...), custom_call_target="tpu_custom_call", output_to_operand_aliasing={{2}: (3, {})} | custom-call | flops 17179869184 | bytes 8388608 | tf_op jit(solution)/shard_map/fine_product/pallas_call | solution.py:267
  71.1 0.0 collective-permute-done.14.beside
  71.1 6.7 %other_half.1 = (bf16[2,512,2048]{2,1,0:T(8,128)(2,1)S(1)}, f32[64,64,128]{2,1,0:T(8,128)S(1)}) custom-call(bf16[2048,1024]{1,0:T(8,128)(2,1)S(1)} %get-tuple-element.39.hi, bf16[2048,1024]{1,0:T(8,128)(2,1)S(1)} %get-tuple-element.40.lo, bf16[8,136,256]{2,1,0:T(8,128)(2,1)S(1)} %collective-permute-done.14.beside, ...), custom_call_target="tpu_custom_call", output_to_operand_aliasing={{0}: (3, {})} | custom-call | flops 8589934592 | bytes 8388608 | tf_op jit(solution)/shard_map/other_half/pallas_call | solution.py:292
  77.9 0.3 collective-permute-start.15
  78.1 5.1 %own_half.1.a_ref = f32[64,64,128]{2,1,0:T(8,128)S(1)} custom-call(bf16[2048,1024]{1,0:T(8,128)(2,1)S(1)} %get-tuple-element.39.hi, bf16[2048,1024]{1,0:T(8,128)(2,1)S(1)} %get-tuple-element.40.lo, bf16[2,512,2048]{2,1,0:T(8,128)(2,1)S(1)} %get-tuple-element.41.turned), custom_call_target="tpu_custom_call" | custom-call | flops 8589934592 | bytes 8388608 | tf_op jit(solution)/shard_map/own_half/pallas_call | solution.py:305
  83.2 0.0 collective-permute-done.15.b_ref
  83.3 1.1 pack.1
  84.3 28.5 %all_to_all.5.in_ref = s16[64,72,128]{2,1,0:T(8,128)(2,1)S(1)} all-to-all(s16[64,72,128]{2,1,0:T(8,128)(2,1)S(1)} %pack.1), channel_id=1, replica_groups=mesh['x'=4,'yh'=2,'core'=2,'z'=4,'yl'=2] {'x','z','yh','yl'}, dimensions={0} | all-to-all | bytes 2359296 | tf_op jit(solution)/shard_map/all_to_all | solution.py:433
  112.8 1.0 unpack.1
  (7 shorter events, 0.1 us)
Async XLA Ops:
  1.5 7.7 %collective-permute-start = (bf16[2,136,256]{2,1,0:T(8,128)(2,1)S(1)}, bf16[2,136,256]{2,1,0:T(8,128)(2,1)S(1)}, u32[]{:S(2)}, u32[]{:S(2)}) collective-permute-start(bf16[2,136,256]{2,1,0:T(8,128)(2,1)S(1)} %stamp.1), channel_id=1, source_target_pairs={{0,64},{1,80},{2,32},{3,48},{4,0},{5,16},{6,96},{7,112},{8,72},{9,... | collective-permute-start | bytes 417800 | tf_op jit(solution)/shard_map/ppermute | solution.py:58
  9.3 10.6 %collective-permute-start.1 = (bf16[2,136,256]{2,1,0:T(8,128)(2,1)S(1)}, bf16[2,136,256]{2,1,0:T(8,128)(2,1)S(1)}, u32[]{:S(2)}, u32[]{:S(2)}) collective-permute-start(bf16[2,136,256]{2,1,0:T(8,128)(2,1)S(1)} %collective-permute-done.refs_0_), channel_id=1, source_target_pairs={{0,32},{1,33},{2,34},{3,35},{4,36},{5,37},{6,38},{7,39},{8,40},{9,... | collective-permute-start | bytes 417800 | tf_op jit(solution)/shard_map/ppermute | solution.py:58
  9.5 10.4 %collective-permute-start.2 = (bf16[2,136,256]{2,1,0:T(8,128)(2,1)S(1)}, bf16[2,136,256]{2,1,0:T(8,128)(2,1)S(1)}, u32[]{:S(2)}, u32[]{:S(2)}) collective-permute-start(bf16[2,136,256]{2,1,0:T(8,128)(2,1)S(1)} %collective-permute-done.refs_0_), channel_id=1, source_target_pairs={{0,96},{1,97},{2,98},{3,99},{4,100},{5,101},{6,102},{7,103},{8,104... | collective-permute-start | bytes 417800 | tf_op jit(solution)/shard_map/ppermute | solution.py:58
  13.2 9.4 %collective-permute-start.3 = (bf16[2,136,256]{2,1,0:T(8,128)(2,1)S(1)}, bf16[2,136,256]{2,1,0:T(8,128)(2,1)S(1)}, u32[]{:S(2)}, u32[]{:S(2)}) collective-permute-start(bf16[2,136,256]{2,1,0:T(8,128)(2,1)S(1)} %collective-permute-done.refs_0_), channel_id=1, source_target_pairs={{0,16},{1,17},{2,18},{3,19},{4,20},{5,21},{6,22},{7,23},{8,24},{9,... | collective-permute-start | bytes 417800 | tf_op jit(solution)/shard_map/ppermute | solution.py:58
  22.7 9.0 %collective-permute-start.6 = (bf16[8,136,256]{2,1,0:T(8,128)(2,1)S(1)}, bf16[8,136,256]{2,1,0:T(8,128)(2,1)S(1)}, u32[]{:S(2)}, u32[]{:S(2)}) collective-permute-start(bf16[8,136,256]{2,1,0:T(8,128)(2,1)S(1)} %pad_maximum_fusion), channel_id=1, source_target_pairs={{0,8},{1,9},{2,10},{3,11},{4,12},{5,13},{6,14},{7,15},{8,0},{9,1},... | collective-permute-start | bytes 1671176 | tf_op jit(solution)/shard_map/ppermute | solution.py:58
  22.8 8.8 %collective-permute-start.4 = (bf16[3,136,256]{2,1,0:T(8,128)(2,1)S(1)}, bf16[3,136,256]{2,1,0:T(8,128)(2,1)S(1)}, u32[]{:S(2)}, u32[]{:S(2)}) collective-permute-start(bf16[3,136,256]{2,1,0:T(8,128)(2,1)S(1)} %get-tuple-element.44), channel_id=1, source_target_pairs={{0,32},{1,33},{2,34},{3,35},{4,36},{5,37},{6,38},{7,39},{8,40},{9,... | collective-permute-start | bytes 626696 | tf_op jit(solution)/shard_map/ppermute | solution.py:58
  22.9 8.8 %collective-permute-start.5 = (bf16[3,136,256]{2,1,0:T(8,128)(2,1)S(1)}, bf16[3,136,256]{2,1,0:T(8,128)(2,1)S(1)}, u32[]{:S(2)}, u32[]{:S(2)}) collective-permute-start(bf16[3,136,256]{2,1,0:T(8,128)(2,1)S(1)} %get-tuple-element.43), channel_id=1, source_target_pairs={{0,96},{1,97},{2,98},{3,99},{4,100},{5,101},{6,102},{7,103},{8,104... | collective-permute-start | bytes 626696 | tf_op jit(solution)/shard_map/ppermute | solution.py:58
  31.7 18.0 %collective-permute-start.9 = (bf16[6,136,256]{2,1,0:T(8,128)(2,1)S(1)}, bf16[6,136,256]{2,1,0:T(8,128)(2,1)S(1)}, u32[]{:S(2)}, u32[]{:S(2)}) collective-permute-start(bf16[6,136,256]{2,1,0:T(8,128)(2,1)S(1)} %pad_maximum_fusion.2), channel_id=1, source_target_pairs={{0,8},{1,9},{2,10},{3,11},{4,12},{5,13},{6,14},{7,15},{8,0},{9,1},... | collective-permute-start | bytes 1253384 | tf_op jit(solution)/shard_map/ppermute | solution.py:58
  31.8 7.8 %collective-permute-start.11 = (bf16[2,136,256]{2,1,0:T(8,128)(2,1)S(1)}, bf16[2,136,256]{2,1,0:T(8,128)(2,1)S(1)}, u32[]{:S(2)}, u32[]{:S(2)}) collective-permute-start(bf16[2,136,256]{2,1,0:T(8,128)(2,1)S(1)} %stamp.1), channel_id=1, source_target_pairs={{0,2},{1,3},{2,4},{3,5},{4,6},{5,7},{6,0},{7,1},{8,10},{9,11},{10,... | collective-permute-start | bytes 417800 | tf_op jit(solution)/shard_map/ppermute | solution.py:58
  32.0 9.9 %collective-permute-start.12 = (bf16[2,136,256]{2,1,0:T(8,128)(2,1)S(1)}, bf16[2,136,256]{2,1,0:T(8,128)(2,1)S(1)}, u32[]{:S(2)}, u32[]{:S(2)}) collective-permute-start(bf16[2,136,256]{2,1,0:T(8,128)(2,1)S(1)} %stamp.1), channel_id=1, source_target_pairs={{0,6},{1,7},{2,0},{3,1},{4,2},{5,3},{6,4},{7,5},{8,14},{9,15},{10,... | collective-permute-start | bytes 417800 | tf_op jit(solution)/shard_map/ppermute | solution.py:58
  35.4 8.3 %collective-permute-start.13 = (bf16[2,136,256]{2,1,0:T(8,128)(2,1)S(1)}, bf16[2,136,256]{2,1,0:T(8,128)(2,1)S(1)}, u32[]{:S(2)}, u32[]{:S(2)}) collective-permute-start(bf16[2,136,256]{2,1,0:T(8,128)(2,1)S(1)} %stamp.1), channel_id=1, source_target_pairs={{0,4},{1,5},{2,6},{3,7},{4,0},{5,1},{6,2},{7,3},{8,12},{9,13},{10,... | collective-permute-start | bytes 417800 | tf_op jit(solution)/shard_map/ppermute | solution.py:58
  43.9 5.8 %collective-permute-start.7 = (bf16[1,136,256]{2,1,0:T(8,128)(2,1)S(1)}, bf16[1,136,256]{2,1,0:T(8,128)(2,1)S(1)}, u32[]{:S(2)}, u32[]{:S(2)}) collective-permute-start(bf16[1,136,256]{2,1,0:T(8,128)(2,1)S(1)} %slice.14), channel_id=1, source_target_pairs={{0,32},{1,33},{2,34},{3,35},{4,36},{5,37},{6,38},{7,39},{8,40},{9,... | collective-permute-start | bytes 208904 | tf_op jit(solution)/shard_map/ppermute | solution.py:58
  44.0 5.7 %collective-permute-start.8 = (bf16[1,136,256]{2,1,0:T(8,128)(2,1)S(1)}, bf16[1,136,256]{2,1,0:T(8,128)(2,1)S(1)}, u32[]{:S(2)}, u32[]{:S(2)}) collective-permute-start(bf16[1,136,256]{2,1,0:T(8,128)(2,1)S(1)} %slice.15), channel_id=1, source_target_pairs={{0,96},{1,97},{2,98},{3,99},{4,100},{5,101},{6,102},{7,103},{8,104... | collective-permute-start | bytes 208904 | tf_op jit(solution)/shard_map/ppermute | solution.py:58
  49.7 4.7 %collective-permute-start.10 = (bf16[2,136,256]{2,1,0:T(8,128)(2,1)S(1)}, bf16[2,136,256]{2,1,0:T(8,128)(2,1)S(1)}, u32[]{:S(2)}, u32[]{:S(2)}) collective-permute-start(bf16[2,136,256]{2,1,0:T(8,128)(2,1)S(1)} %pad_maximum_fusion.5), channel_id=1, source_target_pairs={{0,8},{1,9},{2,10},{3,11},{4,12},{5,13},{6,14},{7,15},{8,0},{9,1},... | collective-permute-start | bytes 417800 | tf_op jit(solution)/shard_map/ppermute | solution.py:58
  51.4 3.0 %copy-start = (s32[32,1,16]{0,2,1:T(8,128)S(1)}, s32[32,1,16]{0,2,1:T(8,128)}, u32[]{:S(2)}) copy-start(s32[32,1,16]{0,2,1:T(8,128)} %param.5) | copy-start | bytes 6148
  51.4 19.7 %collective-permute-start.14 = (bf16[8,136,256]{2,1,0:T(8,128)(2,1)S(1)}, bf16[8,136,256]{2,1,0:T(8,128)(2,1)S(1)}, u32[]{:S(2)}, u32[]{:S(2)}) collective-permute-start(bf16[8,136,256]{2,1,0:T(8,128)(2,1)S(1)} %pad_maximum_fusion.1.line), channel_id=1, source_target_pairs={{0,1},{1,0},{2,3},{3,2},{4,5},{5,4},{6,7},{7,6},{8,9},{9,8},{10,11... | collective-permute-start | bytes 1671176 | tf_op jit(solution)/shard_map/ppermute | solution.py:58
  77.9 5.4 %collective-permute-start.15 = (f32[64,64,128]{2,1,0:T(8,128)S(1)}, f32[64,64,128]{2,1,0:T(8,128)S(1)}, u32[]{:S(2)}, u32[]{:S(2)}) collective-permute-start(f32[64,64,128]{2,1,0:T(8,128)S(1)} %get-tuple-element.42), channel_id=1, source_target_pairs={{0,8},{1,9},{2,10},{3,11},{4,12},{5,13},{6,14},{7,15},{8,0},{9,1},... | collective-permute-start | bytes 6291464 | tf_op jit(solution)/shard_map/ppermute | solution.py:58
